TPU v7x, 256 devices: a whole 4x4x8 slice. The times are simulated.
256 devices in a mesh: src: 32 (over z, y_hi, core), tgt: 8 (over y_lo, x).
Axes of the slice: x: 4, y: 4 (y_hi: 2, y_lo: 2; y = y_hi * 2 + y_lo), z: 8, core: 2. Of those that a mesh axis runs over, the one named last changes fastest.
Arguments:
- src_emb: bfloat16 [16384, 1024], P('src', 'tgt'), may hold values from -16 to 16
- tgt_emb: bfloat16 [32768, 1024], P('tgt', 'src'), may hold values from -16 to 16
- src_ids: int32 [16384], P('src'), may hold values from 0 to 16383
- tgt_ids: int32 [32768], P('tgt'), may hold values from 0 to 16383
Outputs:
- margin: float32 [16384, 32768], P('src', 'tgt')
All inputs are finite; a program needn't handle non-finite values.
Results may differ from a plain program's by a relative error of at most 0.004.
Values may be sent and summed in bfloat16 or wider, within the bound.
No kernel may reach another device: no remote copies, remote signals or barrier semaphores. Data moves between devices by JAX's collectives and lax.ppermute only.
A program may use at most 64 MiB of HBM per device.

v0:
```python
import jax
import jax.numpy as jnp
from jax import lax
from jax.sharding import Mesh
from jax.sharding import PartitionSpec as P

SRC = ("src_0", "src_1", "src_2")


epsilon = 1e-06
excluded_score = -2.0


def from_everyone(array, axis):
    size = lax.axis_size(axis)
    return lax.all_to_all(
        jnp.broadcast_to(array[None], (size, *array.shape)), axis, 0, 0, tiled=True
    )


def joined_along(blocks, dim):
    shape = list(blocks.shape[1:])
    shape[dim] *= blocks.shape[0]
    return jnp.moveaxis(blocks, 0, dim).reshape(shape)


def gather_directly(array, axis, dim):
    blocks = from_everyone(array, axis)
    return joined_along(blocks, dim)


def joined_by_halves(pieces, combine):
    while len(jax.tree.leaves(pieces)[0]) > 1:
        pieces = jax.vmap(combine)(
            *(jax.tree.map(lambda part: part[side::2], pieces) for side in (0, 1))
        )
    return jax.tree.map(lambda part: part[0], pieces)


def combined_all(array, axis, combine):
    pieces = jax.tree.map(lambda part: from_everyone(part, axis), array)
    return joined_by_halves(pieces, combine)


def joined_all(array, axes, combine):
    for axis in axes:
        pieces = lax.all_gather(array.astype(jnp.bfloat16), axis)
        widened = [pieces[k].astype(array.dtype) for k in range(lax.axis_size(axis))]
        array = widened[0]
        for other in widened[1:]:
            array = combine(array, other)
    return array


def unit_rows(embedded):
    values = embedded.astype(jnp.float32)
    scale = jnp.sqrt(jnp.sum(values * values, axis=1, keepdims=True) + epsilon)
    return (values / scale).astype(jnp.bfloat16)


def best_four(values, axis=1):
    upper = jnp.float32(jnp.inf)
    levels = []
    counts = []
    for step in range(4):
        below = jnp.where(values < upper, values, -jnp.inf)
        level = jnp.max(below, axis=axis, keepdims=True)
        counts.append(jnp.sum((values == level).astype(jnp.int32), axis=axis))
        level = jnp.squeeze(level, axis=axis)
        levels.append(level)
        upper = jnp.expand_dims(level, axis)
    entries = []
    for place in range(4):
        chosen = levels[3]
        running = counts[0] + counts[1] + counts[2]
        for level_index in (2, 1, 0):
            chosen = jnp.where(running > place, levels[level_index], chosen)
            if level_index > 0:
                running = running - counts[level_index]
        entries.append(chosen)
    return jnp.stack(entries, axis=-1)


def merge_lists(first, second):
    return best_four(jnp.concatenate([first, second], axis=1))


def body(src_emb, tgt_emb, src_ids, tgt_ids):
    src_whole = gather_directly(src_emb, "tgt", 1)
    tgt_whole = lax.all_gather(tgt_emb, SRC, axis=1, tiled=True)
    src_unit = unit_rows(src_whole)
    tgt_unit = unit_rows(tgt_whole)
    src_rows = src_unit.shape[0]
    tgt_rows = tgt_unit.shape[0]
    width = src_unit.shape[1]
    block_rows = min(512, src_rows)
    blocks = src_rows // block_rows
    src_blocks = src_unit.reshape(blocks, block_rows, width)
    id_blocks = src_ids.reshape(blocks, block_rows)

    def cosines(rows, row_ids):
        scores = lax.dot_general(
            rows, tgt_unit, (((1,), (1,)), ((), ())), preferred_element_type=jnp.float32
        )
        same = row_ids[:, None] == tgt_ids[None, :]
        return (jnp.where(same, jnp.float32(excluded_score), scores), same)

    def first_pass(column_best, pieces):
        rows, row_ids = pieces
        scores, same = cosines(rows, row_ids)
        row_best = best_four(scores, 1)
        merged = merge_lists(column_best, best_four(scores, 0))
        return (merged, row_best)

    start = jnp.full((tgt_rows, 4), excluded_score, jnp.float32)
    column_best, row_best = lax.scan(first_pass, start, (src_blocks, id_blocks))
    row_best = row_best.reshape(src_rows, 4)
    row_final = combined_all(row_best, "tgt", merge_lists)
    column_final = joined_all(column_best, SRC, merge_lists)
    knn_src = jnp.mean(row_final, axis=-1).reshape(blocks, block_rows)
    knn_tgt = jnp.mean(column_final, axis=-1)

    def second_pass(pieces):
        rows, row_ids, row_knn = pieces
        scores, same = cosines(rows, row_ids)
        ratio = scores / (0.5 * (row_knn[:, None] + knn_tgt[None, :]))
        return jnp.where(same, jnp.float32(0.0), ratio)

    margin = lax.map(second_pass, (src_blocks, id_blocks, knn_src))
    return margin.reshape(src_rows, tgt_rows)


def solution(mesh):
    finer = Mesh(
        mesh.devices.reshape(8, 2, 2, mesh.shape["tgt"]), ("src_0", "src_1", "src_2", "tgt")
    )
    in_specs = (P(SRC, "tgt"), P("tgt", SRC), P(SRC), P("tgt"))
    out_specs = P(SRC, "tgt")
    return jax.shard_map(body, mesh=finer, in_specs=in_specs, out_specs=out_specs, check_vma=False)
```

profile of v0, /device:TPU:1, one launch (start us, length us, event | category | flops | bytes accessed | tf_op | source)
XLA Modules:
  0.0 203.7 jit_solution(8985213978395246016)
XLA Ops:
  6.5 0.7 all-gather.2.cloned.1.call-update
  7.3 1.0 copy.7
  8.4 20.4 %all_to_all.10 = bf16[8,512,128]{1,2,0:T(8,128)(2,1)S(1)} all-to-all(bf16[8,512,128]{1,2,0:T(8,128)(2,1)S(1)} %broadcast_in_dim.180), channel_id=1, replica_groups=mesh['src_0'=8,'src_1'=2,'src_2'=2,'tgt'=8] {'tgt'}, dimensions={0} | all-to-all | bytes 2097152 | tf_op jit(solution)/shard_map/all_to_all | solution.py:16
  28.8 0.3 multiply_reduce_fusion
  29.1 0.2 fusion.14
  29.3 86.8 %all-gather.2.cloned.1.call-done = bf16[4096,1024]{0,1:T(8,128)(2,1)} async-done(((bf16[4096,32]{0,1:T(8,128)(2,1)}), bf16[4096,1024]{0,1:T(8,128)(2,1)}) %all-gather.2.cloned.1.call-update) | async-done | bytes 8388624 | tf_op jit(solution)/shard_map/all_gather | solution.py:90
  116.1 5.2 %fusion = f32[4096]{0:T(1024)S(1)} fusion(bf16[4096,1024]{0,1:T(8,128)(2,1)} %all-gather.2.cloned.1.call-done), kind=kLoop, calls=%fused_computation.9 | loop fusion | flops 12578816 | bytes 8404992 | tf_op jit(solution)/shard_map/reduce_sum | solution.py:57
  121.4 0.5 copy-done.1
  121.9 6.1 %fusion.11 = (f32[512]{0:T(512)S(1)}, f32[512,4096]{1,0:T(8,128)S(1)}) fusion(bf16[512,1024]{0,1:T(8,128)(2,1)S(1)} %fusion.14, bf16[4096,1024]{0,1:T(8,128)(2,1)S(1)} %copy-done.1, f32[4096]{0:T(1024)S(1)} %add_sqrt_fusion, s32[4096]{0:T(1024)S(1)} %copy-done.2, s32[512]{0:T(512)S(1)} %copy-done.3), kind=kOutput, calls=%fused_computation.27 | convolution fusion | flops 4318035456 | bytes 17862656 | tf_op jit(solution)/shard_map/while/body/eval_jaxpr/dot_general | solution.py:102
  128.0 1.0 fusion.2
  128.9 1.0 fusion.3
  129.9 2.1 %fusion.4 = (f32[512]{0:T(512)S(1)}, f32[4096]{0:T(1024)S(1)}) fusion(f32[512,4096]{1,0:T(8,128)S(1)} %get-tuple-element.194, f32[512]{0:T(512)S(1)} %fusion.3), kind=kLoop, calls=%fused_computation.15 | loop fusion | flops 12578304 | bytes 8409088 | tf_op jit(solution)/shard_map/while/body/eval_jaxpr/reduce_max | solution.py:67
  132.0 1.0 fusion.5
  133.0 1.0 fusion.6
  134.0 5.7 %convert_reduce_fusion.3 = (s32[512]{0:T(512)S(1)}, s32[4096]{0:T(1024)S(1)}, s32[4096]{0:T(1024)S(1)}, s32[512]{0:T(512)S(1)}, s32[512]{0:T(512)S(1)}, /*index=5*/s32[4096]{0:T(1024)S(1)}) fusion(f32[512,4096]{1,0:T(8,128)S(1)} %get-tuple-element.194, f32[512]{0:T(512)S(1)} %fusion.3, f32[4096]{0:T(1024)S(1)} %get-tuple-element.47, f32[4096]{0:T(1024)S(1)} %fusion.6, ...), kind=kLoop, calls=%fused_computation.22 | loop fusion | flops 37734912 | bytes 8499200 | tf_op jit(solution)/shard_map/while/body/eval_jaxpr/reduce_sum | solution.py:68
  139.7 1.0 fusion.7
  141.1 0.1 convert_reduce_fusion.33
  141.5 18.5 %all_gather.16 = bf16[8,4096,4]{1,2,0:T(4,128)(2,1)S(1)} all-gather(bf16[1,4096,4]{1,2,0:T(4,128)(2,1)S(1)} %pad_maximum_fusion.6), channel_id=1, replica_groups=mesh['src_0'=8,'src_1'=2,'src_2'=2,'tgt'=8] {'src_0'}, dimensions={0}, use_global_device_ids=true | all-gather | bytes 294912 | tf_op jit(solution)/shard_map/all_gather | solution.py:47
  160.3 0.2 convert_reduce_fusion.30
  160.9 0.1 convert_reduce_fusion.27
  161.4 0.1 convert_reduce_fusion.24
  162.0 0.1 convert_reduce_fusion.21
  162.5 0.1 convert_reduce_fusion.18
  163.5 0.1 convert_reduce_fusion.12
  164.0 4.9 %all_gather.17 = bf16[2,4096,4]{1,2,0:T(4,128)(2,1)S(1)} all-gather(bf16[1,4096,4]{1,2,0:T(4,128)(2,1)S(1)} %pad_maximum_fusion.7), channel_id=1, replica_groups=mesh['src_0'=8,'src_1'=2,'src_2'=2,'tgt'=8] {'src_1'}, dimensions={0}, use_global_device_ids=true | all-gather | bytes 98304 | tf_op jit(solution)/shard_map/all_gather | solution.py:47
  169.2 0.2 convert_reduce_fusion.9
  169.6 9.2 %all_gather.18 = bf16[2,4096,4]{1,2,0:T(4,128)(2,1)S(1)} all-gather(bf16[1,4096,4]{1,2,0:T(4,128)(2,1)S(1)} %pad_maximum_fusion.8), channel_id=1, replica_groups=mesh['src_0'=8,'src_1'=2,'src_2'=2,'tgt'=8] {'src_2'}, dimensions={0}, use_global_device_ids=true | all-gather | bytes 98304 | tf_op jit(solution)/shard_map/all_gather | solution.py:47
  179.1 0.2 convert_reduce_fusion.7
  179.4 0.6 broadcast_in_dim.182
  180.0 4.0 %all-to-all-start.1 = ((f32[8,512,4]{1,2,0:T(4,128)}), f32[8,512,4]{1,2,0:T(4,128)S(1)}, u32[]{:S(2)}, u32[]{:S(2)}) async-start(f32[8,512,4]{1,2,0:T(4,128)} %broadcast_in_dim.182), calls=%async_computation.1 | async-start | bytes 131072 | tf_op jit(solution)/shard_map/all_to_all | solution.py:16
  184.1 5.2 %all-to-all-done.1 = f32[8,512,4]{1,2,0:T(4,128)S(1)} async-done(((f32[8,512,4]{1,2,0:T(4,128)}), f32[8,512,4]{1,2,0:T(4,128)S(1)}, u32[]{:S(2)}, u32[]{:S(2)}) %all-to-all-start.1) | async-done | bytes 65568 | tf_op jit(solution)/shard_map/all_to_all | solution.py:16
  190.2 6.7 %compare_select_fusion.7 = f32[512,4096]{1,0:T(8,128)} fusion(f32[512,4096]{1,0:T(8,128)} %copy-done, f32[4096]{0:T(1024)S(1)} %add_multiply_fusion, f32[512]{0:T(512)S(1)} %add_multiply_fusion.1, s32[4096]{0:T(1024)S(1)} %copy-done.2, s32[512]{0:T(512)S(1)} %copy-done.3), kind=kLoop, calls=%fused_computation.11 | loop fusion | flops 10485760 | bytes 16814080 | tf_op jit(solution)/shard_map/while/body/eval_jaxpr/jit(_where)/select_n | solution.py:127
  (128 shorter events, 5.1 us)
Async XLA Ops:
  6.5 114.8 %copy-start.3 = (s32[512]{0:T(512)S(1)}, s32[512]{0:T(512)}, u32[]{:S(2)}) copy-start(s32[512]{0:T(512)} %param.6) | copy-start | bytes 6148
  6.5 114.8 %copy-start.2 = (s32[4096]{0:T(1024)S(1)}, s32[4096]{0:T(1024)}, u32[]{:S(2)}) copy-start(s32[4096]{0:T(1024)} %param.7) | copy-start | bytes 49156
  6.5 109.6 %all-gather.2.cloned.1.call-start = ((), (), s32[]{:S(2)}) async-start(), calls=%async_computation.2 | async-start | bytes 8650752 | tf_op jit(solution)/shard_map/all_gather | solution.py:90
  116.1 5.8 %copy-start.1 = (bf16[4096,1024]{0,1:T(8,128)(2,1)S(1)}, bf16[4096,1024]{0,1:T(8,128)(2,1)}, u32[]{:S(2)}) copy-start(bf16[4096,1024]{0,1:T(8,128)(2,1)} %all-gather.2.cloned.1.call-done) | copy-start | bytes 25165828
  128.0 11.8 %copy-start = (f32[512,4096]{1,0:T(8,128)}, f32[512,4096]{1,0:T(8,128)S(1)}, u32[]{:S(2)}) copy-start(f32[512,4096]{1,0:T(8,128)S(1)} %get-tuple-element.194) | copy-start | bytes 25165828
  180.0 9.2 %all-to-all-start.1 = ((f32[8,512,4]{1,2,0:T(4,128)}), f32[8,512,4]{1,2,0:T(4,128)S(1)}, u32[]{:S(2)}, u32[]{:S(2)}) async-start(f32[8,512,4]{1,2,0:T(4,128)} %broadcast_in_dim.182), calls=%async_computation.1 | async-start | bytes 131072 | tf_op jit(solution)/shard_map/all_to_all | solution.py:16
Sparse Core Ops, SparseCore 0:
  10.1 105.9 all-gather.1
where the time goes:
time: 204 us
  waiting for transfers between devices  92.7 us (45%)
  blocking collectives  53.1 us (26%)
  other arithmetic  30.2 us (15%)
  between operations  14.2 us (7%)
  matrix products  6.08 us (3%)
  starting transfers between devices  4.01 us (2%)
  local copies, waits for them, and re-layouts  3.43 us (2%)
    all_gather x1, waiting for transfers between devices, body(): tgt_whole = lax.all_gather(tgt_emb, SRC, axis=1, tiled=True)  86.8 us
    all_gather x3, blocking collectives, joined_all(): pieces = lax.all_gather(array.astype(jnp.bfloat16), axis)  32.6 us
    all_to_all x1, blocking collectives, from_everyone(): lax.all_to_all(jnp.broadcast_to(array[None], (size, *array.shape)), axis,...  20.4 us
    reduce_max x58, other arithmetic, best_four(): level = jnp.max(below, axis=axis, keepdims=True)  9.79 us
    reduce_sum x14, other arithmetic, best_four(): counts.append(jnp.sum((values == level).astype(jnp.int32), axis=axis))  7.35 us
    select_n x1, other arithmetic, second_pass(): return jnp.where(same, jnp.float32(0.0), ratio)  6.66 us
    dot_general x1, matrix products, cosines(): lax.dot_general(rows, tgt_unit, (((1,), (1,)), ((), ())), preferred_eleme...  6.08 us
    reduce_sum x2, other arithmetic, unit_rows(): scale = jnp.sqrt(jnp.sum(values * values, axis=1, keepdims=True) + epsilon)  5.5 us
  transfers between devices with their start and end apart: 2, of which 2 were waited for; matrix products, arithmetic and copies ran while one was open for 1% of the time, Pallas kernels for 0%

commit v1 on v0

v1 whole, which is shorter than its diff:
```python
import functools

import jax
import jax.numpy as jnp
from jax import lax
from jax.experimental import pallas as pl
from jax.experimental.pallas import tpu as pltpu
from jax.sharding import Mesh
from jax.sharding import PartitionSpec as P

SRC = ("z", "yh", "core")
TGT = ("yl", "x")
EPS = 1e-06
EXCLUDED = -2.0


def bitonic_sorted(m):
    a, b, c, d = m
    a, c = jnp.maximum(a, c), jnp.minimum(a, c)
    b, d = jnp.maximum(b, d), jnp.minimum(b, d)
    a, b = jnp.maximum(a, b), jnp.minimum(a, b)
    c, d = jnp.maximum(c, d), jnp.minimum(c, d)
    return (a, b, c, d)


def top_half(first, second):
    return tuple(jnp.maximum(first[i], second[3 - i]) for i in range(4))


def merged(first, second):
    return bitonic_sorted(top_half(first, second))


def sorted_four(a, b, c, d):
    a, b = jnp.maximum(a, b), jnp.minimum(a, b)
    c, d = jnp.maximum(c, d), jnp.minimum(c, d)
    a, c = jnp.maximum(a, c), jnp.minimum(a, c)
    b, d = jnp.maximum(b, d), jnp.minimum(b, d)
    b, c = jnp.maximum(b, c), jnp.minimum(b, c)
    return (a, b, c, d)


def merged_all(lists):
    while len(lists) > 1:
        lists = [
            merged(lists[k], lists[k + 1]) if k + 1 < len(lists) else lists[k]
            for k in range(0, len(lists), 2)
        ]
    return lists[0]


def over_sublanes(lists):
    for shift in (4, 2, 1):
        lists = merged(lists, tuple(pltpu.roll(p, shift, 0) for p in lists))
    return lists


def score_kernel(
    n_blocks, places, tile, *refs
):
    blocks = refs[:n_blocks]
    src_ref, sid_ref, tid_ref = refs[n_blocks : n_blocks + 3]
    out_ref, row_ref, col_ref = refs[n_blocks + 3 : n_blocks + 6]
    tall, sraw, sunit, dots, rows, tsem, ssem = refs[n_blocks + 6 :]
    step = pl.program_id(0)
    steps = pl.num_programs(0)
    rows_n, feats = sunit.shape
    width = tall.shape[1]
    n_tiles = width // tile
    z = lax.axis_index("z")
    yh = lax.axis_index("yh")
    core = lax.axis_index("core")

    def copies():
        found = []
        for block, where in zip(blocks, places):
            for k, (dz, dy, dc) in enumerate(where):
                owner = (
                    lax.rem(z + 8 + dz, 8) * 4
                    + lax.rem(yh + dy, 2) * 2
                    + lax.rem(core + dc, 2)
                )
                piece = block.at[k] if len(block.shape) == 3 else block
                found.append((piece, pl.multiple_of(owner * 32, 32)))
        return found

    def copy(piece, start, n, tile_index):
        cols = pl.ds(pl.multiple_of(tile_index * tile, tile), tile)
        return pltpu.make_async_copy(
            piece.at[:, cols], tall.at[pl.ds(start, 32), cols], tsem.at[tile_index, n]
        )

    def src_copy(j):
        return pltpu.make_async_copy(
            src_ref.at[j], sraw.at[:, pl.ds(128 * j, 128)], ssem.at[j]
        )

    @pl.when(step == 0)
    def _():
        for j in range(8):
            src_copy(j).start()
        for t in range(n_tiles):
            for n, (piece, start) in enumerate(copies()):
                copy(piece, start, n, t).start()
        for j in range(8):
            src_copy(j).wait()
        for r in range(0, rows_n, 64):
            x = sraw[r : r + 64, :].astype(jnp.float32)
            scale = jnp.sqrt(jnp.sum(x * x, axis=1, keepdims=True) + EPS)
            sunit[r : r + 64, :] = (x / scale).astype(jnp.bfloat16)
        rows[...] = jnp.full(rows.shape, EXCLUDED, jnp.float32)

    for n, (piece, start) in enumerate(copies()):
        copy(piece, start, n, step).wait()

    cols = pl.ds(pl.multiple_of(step * tile, tile), tile)
    square = jnp.zeros((8, tile), jnp.float32)
    for k in range(0, feats, 64):
        x = tall[k : k + 64, cols].astype(jnp.float32)
        x = x * x
        for i in range(0, 64, 8):
            square = square + x[i : i + 8, :]
    inverse = 1.0 / jnp.sqrt(jnp.sum(square, axis=0, keepdims=True) + EPS)
    dots[...] = jnp.dot(sunit[...], tall[:, cols], preferred_element_type=jnp.float32)
    tid = tid_ref[...]
    groups = tile // 128

    def sweep(g, best):
        r = pl.multiple_of(g * 32, 32)
        pieces = []
        for k in range(4):
            here = pl.ds(r + 8 * k, 8)
            same = sid_ref[here, :] == tid
            x = jnp.where(same, jnp.float32(EXCLUDED), dots[here, :] * inverse)
            out_ref[here, :] = x
            pieces.append(x)
            for q in range(0, groups, 4):
                four = sorted_four(*(x[:, 128 * i : 128 * i + 128] for i in range(q, q + 4)))
                kept = merged(tuple(rows[i, here, :] for i in range(4)), four)
                for i in range(4):
                    rows[i, here, :] = kept[i]
        return merged(best, sorted_four(*pieces))

    empty = jnp.full((8, tile), EXCLUDED, jnp.float32)
    best = lax.fori_loop(0, rows_n // 32, sweep, (empty,) * 4)
    best = over_sublanes(best)
    for i in range(4):
        col_ref[i : i + 1, :] = best[i][0:1, :]

    @pl.when(step == steps - 1)
    def _():
        for r in range(0, rows_n, 128):
            turned = [rows[i, r : r + 128, :].T for i in range(4)]
            lists = [
                tuple(turned[i][q : q + 8, :] for i in range(4)) for q in range(0, 128, 8)
            ]
            final = over_sublanes(merged_all(lists))
            for i in range(4):
                row_ref[i : i + 1, r : r + 128] = final[i][0:1, :]


def scores_and_lists(blocks, places, src_all, sid, tid):
    tile = 512
    width = blocks[0].shape[-1]
    rows_n = src_all.shape[1]
    feats = 1024
    n_copies = sum(len(w) for w in places)
    any_spec = pl.BlockSpec(memory_space=pl.ANY)
    return pl.pallas_call(
        functools.partial(score_kernel, len(blocks), places, tile),
        grid=(width // tile,),
        out_shape=(
            jax.ShapeDtypeStruct((rows_n, width), jnp.float32),
            jax.ShapeDtypeStruct((4, rows_n), jnp.float32),
            jax.ShapeDtypeStruct((4, width), jnp.float32),
        ),
        in_specs=[any_spec] * len(blocks)
        + [
            any_spec,
            pl.BlockSpec((rows_n, 1), lambda i: (0, 0)),
            pl.BlockSpec((1, tile), lambda i: (0, i)),
        ],
        out_specs=(
            pl.BlockSpec((rows_n, tile), lambda i: (0, i)),
            pl.BlockSpec((4, rows_n), lambda i: (0, 0)),
            pl.BlockSpec((4, tile), lambda i: (0, i)),
        ),
        scratch_shapes=[
            pltpu.VMEM((feats, width), jnp.bfloat16),
            pltpu.VMEM((rows_n, feats), jnp.bfloat16),
            pltpu.VMEM((rows_n, feats), jnp.bfloat16),
            pltpu.VMEM((rows_n, tile), jnp.float32),
            pltpu.VMEM((4, rows_n, 128), jnp.float32),
            pltpu.SemaphoreType.DMA((width // tile, n_copies)),
            pltpu.SemaphoreType.DMA((8,)),
        ],
        compiler_params=pltpu.CompilerParams(
            dimension_semantics=("arbitrary",), vmem_limit_bytes=32 << 20
        ),
        cost_estimate=pl.CostEstimate(
            flops=2 * rows_n * width * feats, bytes_accessed=18 << 20, transcendentals=0
        ),
        name="scores",
    )(*blocks, src_all, sid, tid)


def margin_kernel(scores_ref, row_ref, knn_ref, out_ref, ksrc):
    @pl.when(pl.program_id(0) == 0)
    def _():
        lists = [tuple(row_ref[k, i : i + 1, :] for i in range(4)) for k in range(8)]
        a, b, c, d = merged_all(lists)
        mean = 0.25 * ((a + b) + (c + d))
        ksrc[...] = jnp.broadcast_to(mean, (128, mean.shape[1])).T

    rows_n = out_ref.shape[0]
    start = pl.multiple_of(pl.program_id(0) * rows_n, rows_n)
    knn_tgt = knn_ref[...]

    for r in range(0, rows_n, 8):
        knn_src = ksrc[pl.ds(start + r, 8), 0:1]
        x = scores_ref[r : r + 8, :]
        ratio = x / (0.5 * (knn_src + knn_tgt))
        out_ref[r : r + 8, :] = jnp.where(x < -1.5, jnp.float32(0.0), ratio)


def margin(scores, row_lists, knn_tgt):
    rows_n, width = scores.shape
    block = 64
    return pl.pallas_call(
        margin_kernel,
        grid=(rows_n // block,),
        out_shape=jax.ShapeDtypeStruct((rows_n, width), jnp.float32),
        in_specs=[
            pl.BlockSpec((block, width), lambda i: (i, 0)),
            pl.BlockSpec(row_lists.shape, lambda i: (0, 0, 0)),
            pl.BlockSpec((1, width), lambda i: (0, 0)),
        ],
        out_specs=pl.BlockSpec((block, width), lambda i: (i, 0)),
        scratch_shapes=[pltpu.VMEM((rows_n, 128), jnp.float32)],
        compiler_params=pltpu.CompilerParams(
            dimension_semantics=("arbitrary",), vmem_limit_bytes=24 << 20
        ),
        name="margin",
    )(scores, row_lists, knn_tgt)


def shifted(array, axis, size, by):
    return lax.ppermute(array, axis, [(i, (i + by) % size) for i in range(size)])


def from_everyone(array, axes, size):
    spread = jnp.broadcast_to(array[None], (size, *array.shape))
    return lax.all_to_all(spread, axes, 0, 0, tiled=True)


def body(src_emb, tgt_emb, src_ids, tgt_ids):
    src_all = lax.all_gather(src_emb, TGT, axis=0)
    own = tgt_emb.T
    up = lambda a: shifted(a, "z", 8, 1)
    down = lambda a: shifted(a, "z", 8, 7)
    over = lambda a: shifted(a, "core", 2, 1)
    other = shifted(own, "yh", 2, 1)
    rings = {}
    held = {("a", 1): own, ("a", -1): own, ("b", 1): other, ("b", -1): other}
    rings[(0, 0)] = own
    rings[(0, 1)] = other
    for step in range(1, 5):
        for name, dy in (("a", 0), ("b", 1)):
            for way in (1, -1):
                if step == 4 and way != (1 if name == "a" else -1):
                    continue
                held[name, way] = (up if way == 1 else down)(held[name, way])
                rings[(-step * way, dy)] = held[name, way]
    order = [
        [(0, 0), (0, 1), (-1, 0), (1, 0)],
        [(-1, 1), (1, 1), (-2, 0), (2, 0)],
        [(-2, 1), (2, 1), (-3, 0), (3, 0)],
        [(-3, 1), (3, 1), (-4, 0), (4, 1)],
    ]
    blocks, places = [], []
    for group in order:
        for key in group:
            blocks.append(rings[key])
            places.append(((*key, 0),))
        blocks.append(over(jnp.stack([rings[key] for key in group])))
        places.append(tuple((*key, 1) for key in group))

    scores, row_best, col_best = scores_and_lists(
        blocks, tuple(places), src_all, src_ids[:, None], tgt_ids[None, :]
    )
    row_lists = from_everyone(row_best, TGT, 8)
    col_best = col_best.astype(jnp.bfloat16)
    pair = over(col_best)
    half = col_best.shape[1] // 2
    start = lax.axis_index("core") * half
    mine, theirs = (
        lax.dynamic_slice_in_dim(a, start, half, 1).astype(jnp.float32)
        for a in (col_best, pair)
    )
    both = jnp.stack(merged(tuple(mine), tuple(theirs))).astype(jnp.bfloat16)
    col_lists = from_everyone(both, ("z", "yh"), 16).astype(jnp.float32)
    lists = [tuple(col_lists[k]) for k in range(16)]
    a, b, c, d = merged_all(lists)
    knn_half = 0.25 * ((a + b) + (c + d))
    knn_other = over(knn_half)
    first = lax.axis_index("core") == 0
    knn_tgt = jnp.concatenate(
        [jnp.where(first, knn_half, knn_other), jnp.where(first, knn_other, knn_half)]
    )
    return margin(scores, row_lists, knn_tgt[None, :])


def solution(mesh):
    finer = Mesh(mesh.devices.reshape(8, 2, 2, 2, 4), ("z", "yh", "core", "yl", "x"))
    in_specs = (P(SRC, TGT), P(TGT, SRC), P(SRC), P(TGT))
    return jax.shard_map(
        body, mesh=finer, in_specs=in_specs, out_specs=P(SRC, TGT), check_vma=False
    )
```

time: 204 us -> 153 us (0.75)
  waiting for transfers between devices: 92.7 us -> 24.6 us
  starting transfers between devices: 4.01 us -> 46.3 us
  blocking collectives: 53.1 us -> 17.3 us
  Pallas kernels: 0 us -> 31.3 us
  other arithmetic: 30.2 us -> 6.38 us
  local copies, waits for them, and re-layouts: 3.43 us -> 12.7 us
  matrix products: 6.08 us -> 0 us
    all_gather x1, waiting for transfers between devices: 86.8 us -> 0.02 us  [body(): src_all = lax.all_gather(src_emb, TGT, axis=0)]
    ppermute x0 -> x21, starting transfers between devices: none -> 41.9 us  [shifted(): lax.ppermute(array, axis, [(i, (i + by) % size) for i in range(size)])]
    all_gather x3 -> x0, blocking collectives: 32.6 us -> none  [joined_all(): pieces = lax.all_gather(array.astype(jnp.bfloat16), axis)]
    pallas_call x0 -> x2, Pallas kernels: none -> 31.3 us  [the longest x1 25.8 us: scores_and_lists(): pl.pallas_call(functools.partial(score_kernel, len(blocks), places, tile)...]
    ppermute x0 -> x21, waiting for transfers between devices: none -> 19.4 us  [shifted(): lax.ppermute(array, axis, [(i, (i + by) % size) for i in range(size)])]
    reduce_sum x16 -> x0, other arithmetic: 12.8 us -> none  [the longest x14 7.35 us: best_four(): counts.append(jnp.sum((values == level).astype(jnp.int32), axis=axis))]
    unnamed x9 -> x28, local copies, waits for them, and re-layouts: 1.53 us -> 11.8 us
    reduce_max x58 -> x0, other arithmetic: 9.79 us -> none  [best_four(): level = jnp.max(below, axis=axis, keepdims=True)]
  transfers between devices with their start and end apart: 2 -> 23, of which waited for: 2 -> 8; matrix products, arithmetic and copies ran while one was open for 1% -> 4% of each run, Pallas kernels for 0% -> 0%
where the time goes in v1:
time: 153 us; the launch traced here: 152 us
  starting transfers between devices  46.3 us (30%)
  Pallas kernels  31.3 us (20%)
  waiting for transfers between devices  24.6 us (16%)
  blocking collectives  17.3 us (11%)
  between operations  13.6 us (9%)
  local copies, waits for them, and re-layouts  12.7 us (8%)
  other arithmetic  6.38 us (4%)
    ppermute x21, starting transfers between devices, shifted(): lax.ppermute(array, axis, [(i, (i + by) % size) for i in range(size)])  41.9 us
    pallas_call x1, Pallas kernels, scores_and_lists(): pl.pallas_call(functools.partial(score_kernel, len(blocks), places, tile)...  25.8 us
    ppermute x21, waiting for transfers between devices, shifted(): lax.ppermute(array, axis, [(i, (i + by) % size) for i in range(size)])  19.4 us
    all_to_all x1, blocking collectives, from_everyone(): return lax.all_to_all(spread, axes, 0, 0, tiled=True)  17.3 us
    unnamed x28, local copies, waits for them, and re-layouts  11.8 us
    another operation x4, other arithmetic, body(): blocks.append(over(jnp.stack([rings[key] for key in group])))  5.56 us
    pallas_call x1, Pallas kernels, margin(): pl.pallas_call(margin_kernel, grid=(rows_n // block,), out_shape=jax.Shap...  5.5 us
    all_to_all x1, waiting for transfers between devices, from_everyone(): return lax.all_to_all(spread, axes, 0, 0, tiled=True)  5.17 us
  transfers between devices with their start and end apart: 23, of which 8 were waited for; matrix products, arithmetic and copies ran while one was open for 4% of the time, Pallas kernels for 0%

profile of v1, /device:TPU:1, one launch (start us, length us, event | category | flops | bytes accessed | tf_op | source)
XLA Modules:
  0.0 152.2 jit_solution(7269204740741918376)
XLA Ops:
  6.5 3.8 %collective-permute-start = (bf16[32,4096]{1,0:T(8,128)(2,1)}, bf16[32,4096]{1,0:T(8,128)(2,1)S(1)}, u32[]{:S(2)}, u32[]{:S(2)}) collective-permute-start(bf16[32,4096]{1,0:T(8,128)(2,1)} %bitcast.23), channel_id=1, source_target_pairs={{0,16},{16,0},{1,17},{17,1},{2,18},{18,2},{3,19},{19,3},{4,20},{20... | collective-permute-start | bytes 786440 | tf_op jit(solution)/shard_map/ppermute | solution.py:248
  10.4 1.6 %collective-permute-start.1 = (bf16[32,4096]{1,0:T(8,128)(2,1)}, bf16[32,4096]{1,0:T(8,128)(2,1)S(1)}, u32[]{:S(2)}, u32[]{:S(2)}) collective-permute-start(bf16[32,4096]{1,0:T(8,128)(2,1)} %bitcast.24), channel_id=1, source_target_pairs={{0,32},{32,64},{64,96},{96,128},{128,160},{160,192},{192,224},{224... | collective-permute-start | bytes 786440 | tf_op jit(solution)/shard_map/ppermute | solution.py:248
  12.0 3.9 %collective-permute-start.2 = (bf16[32,4096]{1,0:T(8,128)(2,1)}, bf16[32,4096]{1,0:T(8,128)(2,1)S(1)}, u32[]{:S(2)}, u32[]{:S(2)}) collective-permute-start(bf16[32,4096]{1,0:T(8,128)(2,1)} %bitcast.25), channel_id=1, source_target_pairs={{0,224},{32,0},{64,32},{96,64},{128,96},{160,128},{192,160},{224,1... | collective-permute-start | bytes 786440 | tf_op jit(solution)/shard_map/ppermute | solution.py:248
  16.0 6.0 %collective-permute-start.5 = (bf16[32,4096]{1,0:T(8,128)(2,1)S(1)}, bf16[32,4096]{1,0:T(8,128)(2,1)S(1)}, u32[]{:S(2)}, u32[]{:S(2)}) collective-permute-start(bf16[32,4096]{1,0:T(8,128)(2,1)S(1)} %collective-permute-done.refs_1_), channel_id=1, source_target_pairs={{0,224},{32,0},{64,32},{96,64},{128,96},{160,128},{192,160},{224,1... | collective-permute-start | bytes 786440 | tf_op jit(solution)/shard_map/ppermute | solution.py:248
  22.1 2.7 %collective-permute-start.7 = (bf16[32,4096]{1,0:T(8,128)(2,1)S(1)}, bf16[32,4096]{1,0:T(8,128)(2,1)S(1)}, u32[]{:S(2)}, u32[]{:S(2)}) collective-permute-start(bf16[32,4096]{1,0:T(8,128)(2,1)S(1)} %collective-permute-done.2.refs_3_), channel_id=1, source_target_pairs={{0,224},{32,0},{64,32},{96,64},{128,96},{160,128},{192,160},{224,1... | collective-permute-start | bytes 786440 | tf_op jit(solution)/shard_map/ppermute | solution.py:248
  24.8 1.2 collective-permute-done.5.refs_6_
  26.0 3.4 %collective-permute-start.10 = (bf16[32,4096]{1,0:T(8,128)(2,1)S(1)}, bf16[32,4096]{1,0:T(8,128)(2,1)S(1)}, u32[]{:S(2)}, u32[]{:S(2)}) collective-permute-start(bf16[32,4096]{1,0:T(8,128)(2,1)S(1)} %collective-permute-done.5.refs_6_), channel_id=1, source_target_pairs={{0,224},{32,0},{64,32},{96,64},{128,96},{160,128},{192,160},{224,1... | collective-permute-start | bytes 786440 | tf_op jit(solution)/shard_map/ppermute | solution.py:248
  29.4 2.0 %pad_maximum_fusion = bf16[4,32,4096]{2,1,0:T(8,128)(2,1)} fusion(bf16[1,32,4096]{2,1,0:T(8,128)(2,1)S(1)} %bitcast.30, bf16[1,32,4096]{2,1,0:T(8,128)(2,1)S(1)} %bitcast.29, bf16[1,32,4096]{2,1,0:T(8,128)(2,1)S(1)} %bitcast.28, bf16[1,32,4096]{2,1,0:T(8,128)(2,1)} %bitcast.26), kind=kLoop, calls=%fused_computation | loop fusion | flops 1572864 | bytes 2097152 | tf_op jit(solution)/shard_map/stack | solution.py:285
  31.4 4.8 %collective-permute-start.3 = (bf16[4,32,4096]{2,1,0:T(8,128)(2,1)}, bf16[4,32,4096]{2,1,0:T(8,128)(2,1)}, u32[]{:S(2)}, u32[]{:S(2)}) collective-permute-start(bf16[4,32,4096]{2,1,0:T(8,128)(2,1)} %pad_maximum_fusion), channel_id=1, source_target_pairs={{0,8},{8,0},{1,9},{9,1},{2,10},{10,2},{3,11},{11,3},{4,12},{12,4},... | collective-permute-start | bytes 3145736 | tf_op jit(solution)/shard_map/ppermute | solution.py:248
  36.4 2.7 %collective-permute-start.12 = (bf16[32,4096]{1,0:T(8,128)(2,1)S(1)}, bf16[32,4096]{1,0:T(8,128)(2,1)S(1)}, u32[]{:S(2)}, u32[]{:S(2)}) collective-permute-start(bf16[32,4096]{1,0:T(8,128)(2,1)S(1)} %collective-permute-done.7.refs_8_), channel_id=1, source_target_pairs={{0,224},{32,0},{64,32},{96,64},{128,96},{160,128},{192,160},{224,1... | collective-permute-start | bytes 786440 | tf_op jit(solution)/shard_map/ppermute | solution.py:248
  39.0 1.7 %collective-permute-start.15 = (bf16[32,4096]{1,0:T(8,128)(2,1)S(1)}, bf16[32,4096]{1,0:T(8,128)(2,1)S(1)}, u32[]{:S(2)}, u32[]{:S(2)}) collective-permute-start(bf16[32,4096]{1,0:T(8,128)(2,1)S(1)} %collective-permute-done.10.refs_11_), channel_id=1, source_target_pairs={{0,224},{32,0},{64,32},{96,64},{128,96},{160,128},{192,160},{224,1... | collective-permute-start | bytes 786440 | tf_op jit(solution)/shard_map/ppermute | solution.py:248
  40.7 1.1 pad_maximum_fusion.1
  41.9 3.7 %collective-permute-done.9.refs_10_ = bf16[32,4096]{1,0:T(8,128)(2,1)S(1)} collective-permute-done((bf16[32,4096]{1,0:T(8,128)(2,1)S(1)}, bf16[32,4096]{1,0:T(8,128)(2,1)S(1)}, u32[]{:S(2)}, u32[]{:S(2)}) %collective-permute-start.9) | collective-permute-done | bytes 262176 | tf_op jit(solution)/shard_map/ppermute | solution.py:248
  45.5 1.1 collective-permute-start.8
  46.6 4.4 %collective-permute-done.11.refs_12_ = bf16[32,4096]{1,0:T(8,128)(2,1)S(1)} collective-permute-done((bf16[32,4096]{1,0:T(8,128)(2,1)S(1)}, bf16[32,4096]{1,0:T(8,128)(2,1)S(1)}, u32[]{:S(2)}, u32[]{:S(2)}) %collective-permute-start.11) | collective-permute-done | bytes 262176 | tf_op jit(solution)/shard_map/ppermute | solution.py:248
  51.1 2.9 %collective-permute-start.17 = (bf16[32,4096]{1,0:T(8,128)(2,1)S(1)}, bf16[32,4096]{1,0:T(8,128)(2,1)S(1)}, u32[]{:S(2)}, u32[]{:S(2)}) collective-permute-start(bf16[32,4096]{1,0:T(8,128)(2,1)S(1)} %collective-permute-done.15.refs_16_), channel_id=1, source_target_pairs={{0,224},{32,0},{64,32},{96,64},{128,96},{160,128},{192,160},{224,1... | collective-permute-start | bytes 786440 | tf_op jit(solution)/shard_map/ppermute | solution.py:248
  54.0 1.1 pad_maximum_fusion.2
  55.1 4.2 %collective-permute-done.14.refs_15_ = bf16[32,4096]{1,0:T(8,128)(2,1)S(1)} collective-permute-done((bf16[32,4096]{1,0:T(8,128)(2,1)S(1)}, bf16[32,4096]{1,0:T(8,128)(2,1)S(1)}, u32[]{:S(2)}, u32[]{:S(2)}) %collective-permute-start.14) | collective-permute-done | bytes 262176 | tf_op jit(solution)/shard_map/ppermute | solution.py:248
  59.3 2.9 %collective-permute-start.13 = (bf16[4,32,4096]{2,1,0:T(8,128)(2,1)}, bf16[4,32,4096]{2,1,0:T(8,128)(2,1)}, u32[]{:S(2)}, u32[]{:S(2)}) collective-permute-start(bf16[4,32,4096]{2,1,0:T(8,128)(2,1)} %pad_maximum_fusion.2), channel_id=1, source_target_pairs={{0,8},{8,0},{1,9},{9,1},{2,10},{10,2},{3,11},{11,3},{4,12},{12,4},... | collective-permute-start | bytes 3145736 | tf_op jit(solution)/shard_map/ppermute | solution.py:248
  62.2 2.7 %collective-permute-done.16.refs_17_ = bf16[32,4096]{1,0:T(8,128)(2,1)S(1)} collective-permute-done((bf16[32,4096]{1,0:T(8,128)(2,1)S(1)}, bf16[32,4096]{1,0:T(8,128)(2,1)S(1)}, u32[]{:S(2)}, u32[]{:S(2)}) %collective-permute-start.16) | collective-permute-done | bytes 262176 | tf_op jit(solution)/shard_map/ppermute | solution.py:248
  64.9 1.3 pad_maximum_fusion.3
  66.2 1.7 %collective-permute-start.18 = (bf16[4,32,4096]{2,1,0:T(8,128)(2,1)}, bf16[4,32,4096]{2,1,0:T(8,128)(2,1)}, u32[]{:S(2)}, u32[]{:S(2)}) collective-permute-start(bf16[4,32,4096]{2,1,0:T(8,128)(2,1)} %pad_maximum_fusion.3), channel_id=1, source_target_pairs={{0,8},{8,0},{1,9},{9,1},{2,10},{10,2},{3,11},{11,3},{4,12},{12,4},... | collective-permute-start | bytes 3145736 | tf_op jit(solution)/shard_map/ppermute | solution.py:248
  68.1 2.4 %collective-permute-done.18.refs_19_ = bf16[4,32,4096]{2,1,0:T(8,128)(2,1)} collective-permute-done((bf16[4,32,4096]{2,1,0:T(8,128)(2,1)}, bf16[4,32,4096]{2,1,0:T(8,128)(2,1)}, u32[]{:S(2)}, u32[]{:S(2)}) %collective-permute-start.18) | collective-permute-done | bytes 1048608 | tf_op jit(solution)/shard_map/ppermute | solution.py:248
  74.3 1.2 copy-done.11
  75.5 25.8 %scores.1 = (f32[512,4096]{1,0:T(8,128)S(1)}, f32[4,512]{1,0:T(4,128)S(1)}, f32[4,4096]{1,0:T(4,128)S(1)}) custom-call(bf16[32,4096]{1,0:T(8,128)(2,1)S(1)} %bitcast.27, bf16[32,4096]{1,0:T(8,128)(2,1)S(1)} %collective-permute-done.refs_1_, bf16[32,4096]{1,0:T(8,128)(2,1)S(1)} %collective-permute-done.1.refs_2_, ...), custom_call_target="tpu_custom_call" | custom-call | flops 4294967296 | bytes 18874368 | tf_op jit(solution)/shard_map/scores/pallas_call | solution.py:169
  101.4 3.4 %copy-done = f32[512,4096]{1,0:T(8,128)} copy-done((f32[512,4096]{1,0:T(8,128)}, f32[512,4096]{1,0:T(8,128)S(1)}, u32[]{:S(2)}) %copy-start) | copy-done | bytes 8388632
  106.4 17.3 %all_to_all.10 = bf16[16,4,2048]{2,1,0:T(4,128)(2,1)S(1)} all-to-all(bf16[16,4,2048]{2,1,0:T(4,128)(2,1)S(1)} %broadcast_in_dim.24), channel_id=1, replica_groups=mesh['z'=8,'yh'=2,'core'=2,'yl'=2,'x'=4] {'z','yh'}, dimensions={0} | all-to-all | bytes 524288 | tf_op jit(solution)/shard_map/all_to_all | solution.py:253
  124.4 2.0 %collective-permute-start.20 = (f32[2048]{0:T(1024)S(1)}, f32[2048]{0:T(1024)S(1)}, u32[]{:S(2)}, u32[]{:S(2)}) collective-permute-start(f32[2048]{0:T(1024)S(1)} %bitcast.46), channel_id=1, source_target_pairs={{0,8},{8,0},{1,9},{9,1},{2,10},{10,2},{3,11},{11,3},{4,12},{12,4},... | collective-permute-start | bytes 24584 | tf_op jit(solution)/shard_map/ppermute | solution.py:248
  127.0 4.3 %all-to-all-start = ((f32[8,4,512]{2,1,0:T(4,128)}), f32[8,4,512]{2,1,0:T(4,128)S(1)}, u32[]{:S(2)}, u32[]{:S(2)}) async-start(f32[8,4,512]{2,1,0:T(4,128)} %broadcast_in_dim.23), calls=%async_computation | async-start | bytes 131072 | tf_op jit(solution)/shard_map/all_to_all | solution.py:253
  131.3 5.2 %all-to-all-done.row_ref = f32[8,4,512]{2,1,0:T(4,128)S(1)} async-done(((f32[8,4,512]{2,1,0:T(4,128)}), f32[8,4,512]{2,1,0:T(4,128)S(1)}, u32[]{:S(2)}, u32[]{:S(2)}) %all-to-all-start) | async-done | bytes 65568 | tf_op jit(solution)/shard_map/all_to_all | solution.py:253
  136.5 3.4 %copy-done.1 = f32[512,4096]{1,0:T(8,128)S(1)} copy-done((f32[512,4096]{1,0:T(8,128)S(1)}, f32[512,4096]{1,0:T(8,128)}, u32[]{:S(2)}) %copy-start.1) | copy-done | bytes 8388632
  139.9 5.5 %margin.1 = f32[512,4096]{1,0:T(8,128)} custom-call(f32[512,4096]{1,0:T(8,128)S(1)} %copy-done.1, f32[8,4,512]{2,1,0:T(4,128)S(1)} %all-to-all-done.row_ref, f32[1,4096]{1,0:T(1,128)S(1)} %bitcast.43), custom_call_target="tpu_custom_call" | custom-call | tf_op jit(solution)/shard_map/margin/pallas_call | solution.py:229
  (63 shorter events, 7.2 us)
Async XLA Ops:
  6.5 63.9 %copy-start.2 = (bf16[4096,32]{0,1:T(8,128)(2,1)S(1)}, bf16[4096,32]{0,1:T(8,128)(2,1)}, u32[]{:S(2)}) copy-start(bf16[4096,32]{0,1:T(8,128)(2,1)} %param.5) | copy-start | bytes 786436
  6.5 61.3 %copy-start.13 = (s32[512]{0:T(512)S(1)}, s32[512]{0:T(512)}, u32[]{:S(2)}) copy-start(s32[512]{0:T(512)} %param.6) | copy-start | bytes 6148
  6.5 63.9 %copy-start.12 = (s32[4096]{0:T(1024)S(1)}, s32[4096]{0:T(1024)}, u32[]{:S(2)}) copy-start(s32[4096]{0:T(1024)} %param.7) | copy-start | bytes 49156
  6.5 61.5 %all-gather.3.cloned.1.call-start = ((), (), s32[]{:S(2)}) async-start(), calls=%async_computation.2 | async-start | bytes 1179648 | tf_op jit(solution)/shard_map/all_gather | solution.py:257
  6.5 9.4 %collective-permute-start = (bf16[32,4096]{1,0:T(8,128)(2,1)}, bf16[32,4096]{1,0:T(8,128)(2,1)S(1)}, u32[]{:S(2)}, u32[]{:S(2)}) collective-permute-start(bf16[32,4096]{1,0:T(8,128)(2,1)} %bitcast.23), channel_id=1, source_target_pairs={{0,16},{16,0},{1,17},{17,1},{2,18},{18,2},{3,19},{19,3},{4,20},{20... | collective-permute-start | bytes 786440 | tf_op jit(solution)/shard_map/ppermute | solution.py:248
  10.4 11.7 %collective-permute-start.1 = (bf16[32,4096]{1,0:T(8,128)(2,1)}, bf16[32,4096]{1,0:T(8,128)(2,1)S(1)}, u32[]{:S(2)}, u32[]{:S(2)}) collective-permute-start(bf16[32,4096]{1,0:T(8,128)(2,1)} %bitcast.24), channel_id=1, source_target_pairs={{0,32},{32,64},{64,96},{96,128},{128,160},{160,192},{192,224},{224... | collective-permute-start | bytes 786440 | tf_op jit(solution)/shard_map/ppermute | solution.py:248
  12.0 10.1 %collective-permute-start.2 = (bf16[32,4096]{1,0:T(8,128)(2,1)}, bf16[32,4096]{1,0:T(8,128)(2,1)S(1)}, u32[]{:S(2)}, u32[]{:S(2)}) collective-permute-start(bf16[32,4096]{1,0:T(8,128)(2,1)} %bitcast.25), channel_id=1, source_target_pairs={{0,224},{32,0},{64,32},{96,64},{128,96},{160,128},{192,160},{224,1... | collective-permute-start | bytes 786440 | tf_op jit(solution)/shard_map/ppermute | solution.py:248
  16.0 10.0 %collective-permute-start.5 = (bf16[32,4096]{1,0:T(8,128)(2,1)S(1)}, bf16[32,4096]{1,0:T(8,128)(2,1)S(1)}, u32[]{:S(2)}, u32[]{:S(2)}) collective-permute-start(bf16[32,4096]{1,0:T(8,128)(2,1)S(1)} %collective-permute-done.refs_1_), channel_id=1, source_target_pairs={{0,224},{32,0},{64,32},{96,64},{128,96},{160,128},{192,160},{224,1... | collective-permute-start | bytes 786440 | tf_op jit(solution)/shard_map/ppermute | solution.py:248
  21.9 14.3 %collective-permute-start.4 = (bf16[32,4096]{1,0:T(8,128)(2,1)S(1)}, bf16[32,4096]{1,0:T(8,128)(2,1)S(1)}, u32[]{:S(2)}, u32[]{:S(2)}) collective-permute-start(bf16[32,4096]{1,0:T(8,128)(2,1)S(1)} %collective-permute-done.refs_1_), channel_id=1, source_target_pairs={{0,32},{32,64},{64,96},{96,128},{128,160},{160,192},{192,224},{224... | collective-permute-start | bytes 786440 | tf_op jit(solution)/shard_map/ppermute | solution.py:248
  22.0 14.2 %collective-permute-start.6 = (bf16[32,4096]{1,0:T(8,128)(2,1)S(1)}, bf16[32,4096]{1,0:T(8,128)(2,1)S(1)}, u32[]{:S(2)}, u32[]{:S(2)}) collective-permute-start(bf16[32,4096]{1,0:T(8,128)(2,1)S(1)} %collective-permute-done.1.refs_2_), channel_id=1, source_target_pairs={{0,32},{32,64},{64,96},{96,128},{128,160},{160,192},{192,224},{224... | collective-permute-start | bytes 786440 | tf_op jit(solution)/shard_map/ppermute | solution.py:248
  22.1 14.2 %collective-permute-start.7 = (bf16[32,4096]{1,0:T(8,128)(2,1)S(1)}, bf16[32,4096]{1,0:T(8,128)(2,1)S(1)}, u32[]{:S(2)}, u32[]{:S(2)}) collective-permute-start(bf16[32,4096]{1,0:T(8,128)(2,1)S(1)} %collective-permute-done.2.refs_3_), channel_id=1, source_target_pairs={{0,224},{32,0},{64,32},{96,64},{128,96},{160,128},{192,160},{224,1... | collective-permute-start | bytes 786440 | tf_op jit(solution)/shard_map/ppermute | solution.py:248
  26.0 13.1 %collective-permute-start.10 = (bf16[32,4096]{1,0:T(8,128)(2,1)S(1)}, bf16[32,4096]{1,0:T(8,128)(2,1)S(1)}, u32[]{:S(2)}, u32[]{:S(2)}) collective-permute-start(bf16[32,4096]{1,0:T(8,128)(2,1)S(1)} %collective-permute-done.5.refs_6_), channel_id=1, source_target_pairs={{0,224},{32,0},{64,32},{96,64},{128,96},{160,128},{192,160},{224,1... | collective-permute-start | bytes 786440 | tf_op jit(solution)/shard_map/ppermute | solution.py:248
  31.4 36.6 %collective-permute-start.3 = (bf16[4,32,4096]{2,1,0:T(8,128)(2,1)}, bf16[4,32,4096]{2,1,0:T(8,128)(2,1)}, u32[]{:S(2)}, u32[]{:S(2)}) collective-permute-start(bf16[4,32,4096]{2,1,0:T(8,128)(2,1)} %pad_maximum_fusion), channel_id=1, source_target_pairs={{0,8},{8,0},{1,9},{9,1},{2,10},{10,2},{3,11},{11,3},{4,12},{12,4},... | collective-permute-start | bytes 3145736 | tf_op jit(solution)/shard_map/ppermute | solution.py:248
  36.3 9.3 %collective-permute-start.9 = (bf16[32,4096]{1,0:T(8,128)(2,1)S(1)}, bf16[32,4096]{1,0:T(8,128)(2,1)S(1)}, u32[]{:S(2)}, u32[]{:S(2)}) collective-permute-start(bf16[32,4096]{1,0:T(8,128)(2,1)S(1)} %collective-permute-done.4.refs_5_), channel_id=1, source_target_pairs={{0,32},{32,64},{64,96},{96,128},{128,160},{160,192},{192,224},{224... | collective-permute-start | bytes 786440 | tf_op jit(solution)/shard_map/ppermute | solution.py:248
  36.3 14.8 %collective-permute-start.11 = (bf16[32,4096]{1,0:T(8,128)(2,1)S(1)}, bf16[32,4096]{1,0:T(8,128)(2,1)S(1)}, u32[]{:S(2)}, u32[]{:S(2)}) collective-permute-start(bf16[32,4096]{1,0:T(8,128)(2,1)S(1)} %collective-permute-done.6.refs_7_), channel_id=1, source_target_pairs={{0,32},{32,64},{64,96},{96,128},{128,160},{160,192},{192,224},{224... | collective-permute-start | bytes 786440 | tf_op jit(solution)/shard_map/ppermute | solution.py:248
  36.4 14.7 %collective-permute-start.12 = (bf16[32,4096]{1,0:T(8,128)(2,1)S(1)}, bf16[32,4096]{1,0:T(8,128)(2,1)S(1)}, u32[]{:S(2)}, u32[]{:S(2)}) collective-permute-start(bf16[32,4096]{1,0:T(8,128)(2,1)S(1)} %collective-permute-done.7.refs_8_), channel_id=1, source_target_pairs={{0,224},{32,0},{64,32},{96,64},{128,96},{160,128},{192,160},{224,1... | collective-permute-start | bytes 786440 | tf_op jit(solution)/shard_map/ppermute | solution.py:248
  39.0 12.0 %collective-permute-start.15 = (bf16[32,4096]{1,0:T(8,128)(2,1)S(1)}, bf16[32,4096]{1,0:T(8,128)(2,1)S(1)}, u32[]{:S(2)}, u32[]{:S(2)}) collective-permute-start(bf16[32,4096]{1,0:T(8,128)(2,1)S(1)} %collective-permute-done.10.refs_11_), channel_id=1, source_target_pairs={{0,224},{32,0},{64,32},{96,64},{128,96},{160,128},{192,160},{224,1... | collective-permute-start | bytes 786440 | tf_op jit(solution)/shard_map/ppermute | solution.py:248
  45.5 22.5 %collective-permute-start.8 = (bf16[4,32,4096]{2,1,0:T(8,128)(2,1)}, bf16[4,32,4096]{2,1,0:T(8,128)(2,1)}, u32[]{:S(2)}, u32[]{:S(2)}) collective-permute-start(bf16[4,32,4096]{2,1,0:T(8,128)(2,1)} %pad_maximum_fusion.1), channel_id=1, source_target_pairs={{0,8},{8,0},{1,9},{9,1},{2,10},{10,2},{3,11},{11,3},{4,12},{12,4},... | collective-permute-start | bytes 3145736 | tf_op jit(solution)/shard_map/ppermute | solution.py:248
  51.0 8.3 %collective-permute-start.14 = (bf16[32,4096]{1,0:T(8,128)(2,1)S(1)}, bf16[32,4096]{1,0:T(8,128)(2,1)S(1)}, u32[]{:S(2)}, u32[]{:S(2)}) collective-permute-start(bf16[32,4096]{1,0:T(8,128)(2,1)S(1)} %collective-permute-done.9.refs_10_), channel_id=1, source_target_pairs={{0,32},{32,64},{64,96},{96,128},{128,160},{160,192},{192,224},{224... | collective-permute-start | bytes 786440 | tf_op jit(solution)/shard_map/ppermute | solution.py:248
  51.0 13.9 %collective-permute-start.16 = (bf16[32,4096]{1,0:T(8,128)(2,1)S(1)}, bf16[32,4096]{1,0:T(8,128)(2,1)S(1)}, u32[]{:S(2)}, u32[]{:S(2)}) collective-permute-start(bf16[32,4096]{1,0:T(8,128)(2,1)S(1)} %collective-permute-done.11.refs_12_), channel_id=1, source_target_pairs={{0,32},{32,64},{64,96},{96,128},{128,160},{160,192},{192,224},{224... | collective-permute-start | bytes 786440 | tf_op jit(solution)/shard_map/ppermute | solution.py:248
  51.0 16.8 %copy-start.3 = (bf16[32,4096]{1,0:T(8,128)(2,1)}, bf16[32,4096]{1,0:T(8,128)(2,1)S(1)}, u32[]{:S(2)}) copy-start(bf16[32,4096]{1,0:T(8,128)(2,1)S(1)} %collective-permute-done.15.refs_16_) | copy-start | bytes 786436
  51.1 13.8 %collective-permute-start.17 = (bf16[32,4096]{1,0:T(8,128)(2,1)S(1)}, bf16[32,4096]{1,0:T(8,128)(2,1)S(1)}, u32[]{:S(2)}, u32[]{:S(2)}) collective-permute-start(bf16[32,4096]{1,0:T(8,128)(2,1)S(1)} %collective-permute-done.15.refs_16_), channel_id=1, source_target_pairs={{0,224},{32,0},{64,32},{96,64},{128,96},{160,128},{192,160},{224,1... | collective-permute-start | bytes 786440 | tf_op jit(solution)/shard_map/ppermute | solution.py:248
  59.3 8.6 %copy-start.5 = (bf16[32,4096]{1,0:T(8,128)(2,1)}, bf16[32,4096]{1,0:T(8,128)(2,1)S(1)}, u32[]{:S(2)}) copy-start(bf16[32,4096]{1,0:T(8,128)(2,1)S(1)} %collective-permute-done.14.refs_15_) | copy-start | bytes 786436
  59.3 8.8 %collective-permute-start.13 = (bf16[4,32,4096]{2,1,0:T(8,128)(2,1)}, bf16[4,32,4096]{2,1,0:T(8,128)(2,1)}, u32[]{:S(2)}, u32[]{:S(2)}) collective-permute-start(bf16[4,32,4096]{2,1,0:T(8,128)(2,1)} %pad_maximum_fusion.2), channel_id=1, source_target_pairs={{0,8},{8,0},{1,9},{9,1},{2,10},{10,2},{3,11},{11,3},{4,12},{12,4},... | collective-permute-start | bytes 3145736 | tf_op jit(solution)/shard_map/ppermute | solution.py:248
  64.9 3.0 %copy-start.7 = (bf16[32,4096]{1,0:T(8,128)(2,1)}, bf16[32,4096]{1,0:T(8,128)(2,1)S(1)}, u32[]{:S(2)}) copy-start(bf16[32,4096]{1,0:T(8,128)(2,1)S(1)} %collective-permute-done.16.refs_17_) | copy-start | bytes 786436
  64.9 3.0 %copy-start.9 = (bf16[32,4096]{1,0:T(8,128)(2,1)}, bf16[32,4096]{1,0:T(8,128)(2,1)S(1)}, u32[]{:S(2)}) copy-start(bf16[32,4096]{1,0:T(8,128)(2,1)S(1)} %collective-permute-done.17.refs_18_) | copy-start | bytes 786436
  66.2 4.3 %collective-permute-start.18 = (bf16[4,32,4096]{2,1,0:T(8,128)(2,1)}, bf16[4,32,4096]{2,1,0:T(8,128)(2,1)}, u32[]{:S(2)}, u32[]{:S(2)}) collective-permute-start(bf16[4,32,4096]{2,1,0:T(8,128)(2,1)} %pad_maximum_fusion.3), channel_id=1, source_target_pairs={{0,8},{8,0},{1,9},{9,1},{2,10},{10,2},{3,11},{11,3},{4,12},{12,4},... | collective-permute-start | bytes 3145736 | tf_op jit(solution)/shard_map/ppermute | solution.py:248
  101.4 3.4 %copy-start = (f32[512,4096]{1,0:T(8,128)}, f32[512,4096]{1,0:T(8,128)S(1)}, u32[]{:S(2)}) copy-start(f32[512,4096]{1,0:T(8,128)S(1)} %get-tuple-element.8.scores_ref) | copy-start | bytes 25165828
  104.8 1.3 collective-permute-start.19
  124.4 7.0 %collective-permute-start.20 = (f32[2048]{0:T(1024)S(1)}, f32[2048]{0:T(1024)S(1)}, u32[]{:S(2)}, u32[]{:S(2)}) collective-permute-start(f32[2048]{0:T(1024)S(1)} %bitcast.46), channel_id=1, source_target_pairs={{0,8},{8,0},{1,9},{9,1},{2,10},{10,2},{3,11},{11,3},{4,12},{12,4},... | collective-permute-start | bytes 24584 | tf_op jit(solution)/shard_map/ppermute | solution.py:248
  127.0 9.5 %all-to-all-start = ((f32[8,4,512]{2,1,0:T(4,128)}), f32[8,4,512]{2,1,0:T(4,128)S(1)}, u32[]{:S(2)}, u32[]{:S(2)}) async-start(f32[8,4,512]{2,1,0:T(4,128)} %broadcast_in_dim.23), calls=%async_computation | async-start | bytes 131072 | tf_op jit(solution)/shard_map/all_to_all | solution.py:253
  136.5 3.4 %copy-start.1 = (f32[512,4096]{1,0:T(8,128)S(1)}, f32[512,4096]{1,0:T(8,128)}, u32[]{:S(2)}) copy-start(f32[512,4096]{1,0:T(8,128)} %copy-done) | copy-start | bytes 25165828
  (5 other events, 5.0 us)
Sparse Core Ops, SparseCore 0:
  22.1 35.5 all-gather.2

commit v2 on v0

v2 whole, which is shorter than its diff:
```python
import functools

import jax
import jax.numpy as jnp
from jax import lax
from jax.experimental import pallas as pl
from jax.experimental.pallas import tpu as pltpu
from jax.sharding import Mesh
from jax.sharding import PartitionSpec as P

SRC = ("z", "yh", "core")
TGT = ("yl", "x")
EPS = 1e-06
EXCLUDED = -2.0


def bitonic_sorted(m):
    a, b, c, d = m
    a, c = jnp.maximum(a, c), jnp.minimum(a, c)
    b, d = jnp.maximum(b, d), jnp.minimum(b, d)
    a, b = jnp.maximum(a, b), jnp.minimum(a, b)
    c, d = jnp.maximum(c, d), jnp.minimum(c, d)
    return (a, b, c, d)


def top_half(first, second):
    return tuple(jnp.maximum(first[i], second[3 - i]) for i in range(4))


def merged(first, second):
    return bitonic_sorted(top_half(first, second))


def sorted_four(a, b, c, d):
    a, b = jnp.maximum(a, b), jnp.minimum(a, b)
    c, d = jnp.maximum(c, d), jnp.minimum(c, d)
    a, c = jnp.maximum(a, c), jnp.minimum(a, c)
    b, d = jnp.maximum(b, d), jnp.minimum(b, d)
    b, c = jnp.maximum(b, c), jnp.minimum(b, c)
    return (a, b, c, d)


def merged_all(lists):
    while len(lists) > 1:
        lists = [
            merged(lists[k], lists[k + 1]) if k + 1 < len(lists) else lists[k]
            for k in range(0, len(lists), 2)
        ]
    return lists[0]


def over_sublanes(lists):
    for shift in (4, 2, 1):
        lists = merged(lists, tuple(pltpu.roll(p, shift, 0) for p in lists))
    return lists


def score_kernel(n_blocks, side, *refs):
    blocks = refs[:n_blocks]
    unit_refs = refs[n_blocks : n_blocks + 2]
    sid_ref, tid_ref = refs[n_blocks + 2 : n_blocks + 4]
    refs = refs[n_blocks + 4 :]
    if side:
        row_before, refs = refs[:2], refs[2:]
    score_refs, row_refs, col_ref = refs[:2], refs[2:4], refs[4]
    tall, unit, even, odd, rows, sids, stage, tsem, usem, osem = refs[5:]
    feats, width = tall.shape
    rows_n = unit.shape[0]
    half = rows_n // 2
    chunk, tile = even.shape
    n_units = width // tile
    z = lax.axis_index("z")
    yh = lax.axis_index("yh")

    def copy(n, t):
        dz, dy = PLACES[n]
        owner = lax.rem(z + (8 + dz), 8) * 2 + lax.rem(yh + dy, 2)
        where = pl.ds(pl.multiple_of(owner * 64, 64), 64)
        offset = side * width if blocks[n].shape[1] > width else 0
        return pltpu.make_async_copy(
            blocks[n].at[:, pl.ds(offset + t * tile, tile)],
            tall.at[where, pl.ds(t * tile, tile)],
            tsem.at[t, n],
        )

    unit_copies = [
        pltpu.make_async_copy(
            unit_refs[k], unit.at[pl.ds(k * half, half), :], usem.at[k]
        )
        for k in range(2)
    ]
    for n in range(n_blocks):
        copy(n, 0).start()
    for c in unit_copies:
        c.start()
    for t in range(1, n_units):
        for n in range(n_blocks):
            copy(n, t).start()
    for r in range(0, rows_n, 128):
        ids = jnp.broadcast_to(sid_ref[:, r : r + 128], (128, 128))
        sids[r : r + 128, :] = ids.T
    for r in range(0, rows_n, 32):
        for i in range(4):
            rows[i, r : r + 32, :] = jnp.full((32, 128), EXCLUDED, jnp.float32)

    def columns(u):
        return slice(u * tile, u * tile + tile)

    def inverse_norm(u):
        total = jnp.zeros((8, tile), jnp.float32)
        for k in range(0, feats, 16):
            x = tall[k : k + 16, columns(u)].astype(jnp.float32)
            x = x * x
            total = total + (x[:8] + x[8:])
        return 1.0 / jnp.sqrt(jnp.sum(total, axis=0, keepdims=True) + EPS)

    sequence = [(u, r) for u in range(n_units) for r in range(0, rows_n, chunk)]
    buffers = (even, odd)

    def dot(k):
        u, r = sequence[k]
        buffers[k % 2][...] = jnp.dot(
            unit[r : r + chunk, :],
            tall[:, columns(u)],
            preferred_element_type=jnp.float32,
        )

    def sweep(u, r, dots, inside, inverse, tid, best):
        pieces = []
        for k in range(0, 32, 8):
            here = slice(r + k, r + k + 8)
            ids = sids[here, :]
            same = jnp.concatenate([ids] * (tile // 128), axis=1) == tid
            dotted = dots[inside + k : inside + k + 8, :] * inverse
            x = jnp.where(same, jnp.float32(EXCLUDED), dotted)
            stage[here, columns(u)] = x
            pieces.append(x)
            kept = tuple(rows[i, here, :] for i in range(4))
            four = sorted_four(*(x[:, p : p + 128] for p in range(0, tile, 128)))
            kept = merged(kept, four)
            for i in range(4):
                rows[i, here, :] = kept[i]
        return merged(best, sorted_four(*pieces))

    def out_copy(k):
        u, r = sequence[k]
        cols = pl.ds(u * tile, tile)
        return pltpu.make_async_copy(
            stage.at[pl.ds(r, chunk), cols],
            score_refs[r // half].at[pl.ds(r % half, chunk), cols],
            osem.at[k],
        )

    for n in range(n_blocks):
        copy(n, 0).wait()
    for c in unit_copies:
        c.wait()
    dot(0)
    inverse = inverse_norm(0)
    best = (jnp.full((8, tile), EXCLUDED, jnp.float32),) * 4
    first = best
    for k, (u, r) in enumerate(sequence):
        if k + 1 < len(sequence):
            if sequence[k + 1][0] > u:
                for n in range(n_blocks):
                    copy(n, u + 1).wait()
                following = inverse_norm(u + 1)
            dot(k + 1)
        tid = tid_ref[:, columns(u)]
        for q in range(0, chunk, 32):
            best = sweep(u, r + q, buffers[k % 2], q, inverse, tid, best)
        out_copy(k).start()
        if r + chunk == rows_n:
            best = over_sublanes(best)
            for i in range(4):
                col_ref[i : i + 1, columns(u)] = best[i][0:1, :].astype(col_ref.dtype)
            if u + 1 < n_units:
                best, inverse = first, following

    for r in range(0, rows_n, 128):
        turned = [rows[i, r : r + 128, :].T for i in range(4)]
        lists = [
            tuple(turned[i][q : q + 8, :] for i in range(4)) for q in range(0, 128, 8)
        ]
        final = tuple(p[0:1, :] for p in over_sublanes(merged_all(lists)))
        here = slice(r % half, r % half + 128)
        if side:
            before = row_before[r // half]
            final = merged(final, tuple(before[i : i + 1, here] for i in range(4)))
        for i in range(4):
            row_refs[r // half][i : i + 1, here] = final[i]
    for k in range(len(sequence)):
        out_copy(k).wait()


def scores_and_lists(side, blocks, units, sid, tid, row_before):
    tile, chunk = 512, 256
    feats = 1024
    width = tid.shape[1]
    half = units[0].shape[0]
    vmem = pl.BlockSpec(memory_space=pltpu.VMEM)
    hbm = pl.BlockSpec(memory_space=pltpu.HBM)
    rest = [sid, tid, *row_before]
    return pl.pallas_call(
        functools.partial(score_kernel, len(blocks), side),
        out_shape=(
            pltpu.HBM((half, width), jnp.float32),
            pltpu.HBM((half, width), jnp.float32),
            jax.ShapeDtypeStruct((4, half), jnp.float32),
            jax.ShapeDtypeStruct((4, half), jnp.float32),
            jax.ShapeDtypeStruct((4, width), jnp.bfloat16),
        ),
        in_specs=[hbm] * (len(blocks) + 2) + [vmem] * len(rest),
        out_specs=(hbm, hbm, vmem, vmem, vmem),
        scratch_shapes=[
            pltpu.VMEM((feats, width), jnp.bfloat16),
            pltpu.VMEM((2 * half, feats), jnp.bfloat16),
            pltpu.VMEM((chunk, tile), jnp.float32),
            pltpu.VMEM((chunk, tile), jnp.float32),
            pltpu.VMEM((4, 2 * half, 128), jnp.float32),
            pltpu.VMEM((2 * half, 128), jnp.int32),
            pltpu.VMEM((2 * half, width), jnp.float32),
            pltpu.SemaphoreType.DMA((width // tile, len(blocks))),
            pltpu.SemaphoreType.DMA((2,)),
            pltpu.SemaphoreType.DMA((width // tile * (2 * half // chunk),)),
        ],
        compiler_params=pltpu.CompilerParams(vmem_limit_bytes=20 << 20),
        cost_estimate=pl.CostEstimate(
            flops=4 * half * width * feats, bytes_accessed=9 << 20, transcendentals=0
        ),
        name=f"scores{side}",
    )(*blocks, *units, *rest)


def unit_kernel(own_ref, beside_ref, *refs):
    out_ref = refs[-1]
    rows_n = out_ref.shape[0]
    yl = lax.axis_index("yl")
    x = lax.axis_index("x")
    for r in range(0, rows_n, 64):
        here = slice(r, r + 64)
        pieces = [(own_ref[here, :], 0, 0), (beside_ref[here, :], 1, 0)]
        for ref, dx in zip(refs, (3, 1, 2)):
            pieces += [(ref[k, here, :], k, dx) for k in range(2)]
        pieces = [(p.astype(jnp.float32), dy, dx) for p, dy, dx in pieces]
        total = sum(p * p for p, _, _ in pieces)
        scale = jnp.sqrt(jnp.sum(total, axis=1, keepdims=True) + EPS)
        for p, dy, dx in pieces:
            owner = lax.rem(yl + dy, 2) * 4 + lax.rem(x + dx, 4)
            cols = pl.ds(pl.multiple_of(owner * 128, 128), 128)
            out_ref[here, cols] = (p / scale).astype(jnp.bfloat16)


def unit_rows(own):
    beside = shifted(own, "yl", 2, 1)
    pair = jnp.stack([own, beside])
    parts = [own, beside] + [shifted(pair, "x", 4, k) for k in (1, 3, 2)]
    vmem = pl.BlockSpec(memory_space=pltpu.VMEM)
    return pl.pallas_call(
        unit_kernel,
        out_shape=jax.ShapeDtypeStruct((own.shape[0], 1024), jnp.bfloat16),
        in_specs=[vmem] * 5,
        out_specs=vmem,
        compiler_params=pltpu.CompilerParams(vmem_limit_bytes=8 << 20),
        name="unit",
    )(*parts)


def margin_kernel(kept0, kept1, got0, got1, row_ref, knn_own_ref, knn_got_ref, out_ref, ksrc):
    width = kept0.shape[1]
    core = lax.axis_index("core")

    @pl.when(pl.program_id(0) == 0)
    def _():
        a, b, c, d = (row_ref[i : i + 1, :] for i in range(4))
        mean = 0.25 * ((a + b) + (c + d))
        ksrc[...] = jnp.broadcast_to(mean, (128, mean.shape[1])).T

    rows_n = out_ref.shape[0]
    start = pl.multiple_of(pl.program_id(0) * rows_n, rows_n)
    own_place = core * (2 * width)
    got_place = (1 - core) * (2 * width)
    sides = (
        (kept0, knn_own_ref, 0, own_place),
        (kept1, knn_own_ref, width, own_place + width),
        (got0, knn_got_ref, 0, got_place),
        (got1, knn_got_ref, width, got_place + width),
    )
    for scores_ref, knn_ref, offset, place in sides:
        knn_tgt = knn_ref[:, offset : offset + width]
        cols = pl.ds(pl.multiple_of(place, width), width)
        for r in range(0, rows_n, 8):
            here = pl.ds(pl.multiple_of(start + r, 8), 8)
            x = scores_ref[r : r + 8, :]
            ratio = x / (0.5 * (ksrc[here, 0:1] + knn_tgt))
            out_ref[r : r + 8, cols] = jnp.where(x < -1.5, jnp.float32(0.0), ratio)


def margin(scores, row_list, knn_own, knn_got):
    rows_n, width = scores[0].shape
    block = 64
    vmem = pl.BlockSpec(memory_space=pltpu.VMEM)
    return pl.pallas_call(
        margin_kernel,
        grid=(rows_n // block,),
        out_shape=jax.ShapeDtypeStruct((rows_n, 4 * width), jnp.float32),
        in_specs=[pl.BlockSpec((block, width), lambda i: (i, 0))] * 4 + [vmem] * 3,
        out_specs=pl.BlockSpec((block, 4 * width), lambda i: (i, 0)),
        scratch_shapes=[pltpu.VMEM((rows_n, 128), jnp.float32)],
        compiler_params=pltpu.CompilerParams(
            dimension_semantics=("arbitrary",), vmem_limit_bytes=16 << 20
        ),
        name="margin",
    )(*scores, row_list, knn_own, knn_got)


def shifted(array, axis, size, by):
    return lax.ppermute(array, axis, [(i, (i + by) % size) for i in range(size)])


def from_everyone(array, axes, size):
    spread = jnp.broadcast_to(array[None], (size, *array.shape))
    return lax.all_to_all(spread, axes, 0, 0, tiled=True)


def up(array):
    return shifted(array, "z", 8, 1)


def down(array):
    return shifted(array, "z", 8, 7)


def across(array):
    return shifted(array, "yh", 2, 1)


def over(array):
    return shifted(array, "core", 2, 1)


PLACES = [(0, 0), (0, 1)] + [(dz, dy) for dz in (-1, 1, -2, 2, -3, 3, 4) for dy in (0, 1)]
BY_Y = (3, 4)


def gathered(own):
    a, b = {0: own}, {0: across(own)}
    for k in range(1, 5):
        a[-k] = up(a[1 - k])
        if k < 4:
            a[k] = down(a[k - 1])
            b[-k] = across(a[-k]) if k in BY_Y else up(b[1 - k])
            b[k] = across(a[k]) if k in BY_Y else down(b[k - 1])
    a[4] = a[-4]
    b[4] = across(a[4]) if 4 in BY_Y else down(b[3])
    return [(b if dy else a)[dz] for dz, dy in PLACES], b[0]


def body(src_emb, tgt_emb, src_ids, tgt_ids):
    core = lax.axis_index("core")
    first = core == 0
    own = tgt_emb.T
    half = own.shape[1] // 2
    mine = lax.dynamic_slice_in_dim(own, core * half, half, 1)
    theirs = over(lax.dynamic_slice_in_dim(own, (1 - core) * half, half, 1))
    chip = jnp.concatenate(
        [jnp.where(first, mine, theirs), jnp.where(first, theirs, mine)]
    )
    blocks, _ = gathered(chip)
    unit = unit_rows(src_emb)
    units = (unit, over(unit))
    sid = jnp.concatenate([src_ids, over(src_ids)])[None, :]
    tid = lax.dynamic_slice_in_dim(tgt_ids, core * half, half, 0)[None, :]

    quarter = half // 2
    kept0, sent0, row0, row0_pair, col0 = scores_and_lists(
        0, blocks, units, sid, tid[:, :quarter], ()
    )
    got0 = over(sent0)
    kept1, sent1, row1, row1_pair, col1 = scores_and_lists(
        1, blocks, units, sid, tid[:, quarter:], (row0, row0_pair)
    )
    col_lists = from_everyone(jnp.concatenate([col0, col1], axis=1), ("z", "yh"), 16)
    got1 = over(sent1)

    def joined(first, second):
        pairs = (
            merged(tuple(first[k : k + 4]), tuple(second[k : k + 4])) for k in (0, 4)
        )
        return jnp.stack([p for four in pairs for p in four])

    lists = jnp.concatenate([row1, row1_pair])
    lists = joined(lists, shifted(lists, "yl", 2, 1))
    lists = joined(lists, shifted(lists, "x", 4, 2))
    lists = joined(lists, shifted(lists, "x", 4, 1))
    col_lists = col_lists.astype(jnp.float32)
    a, b, c, d = merged_all([tuple(col_lists[k]) for k in range(16)])
    knn_own = 0.25 * ((a + b) + (c + d))
    swap = over(jnp.concatenate([lists[4:], knn_own.reshape(-1, lists.shape[1])]))
    row_list = jnp.stack(merged(tuple(lists[:4]), tuple(swap[:4])))
    knn_got = swap[4:].reshape(1, -1)
    return margin((kept0, kept1, got0, got1), row_list, knn_own[None, :], knn_got)


def solution(mesh):
    finer = Mesh(mesh.devices.reshape(8, 2, 2, 2, 4), ("z", "yh", "core", "yl", "x"))
    in_specs = (P(SRC, TGT), P(TGT, SRC), P(SRC), P(TGT))
    return jax.shard_map(
        body, mesh=finer, in_specs=in_specs, out_specs=P(SRC, TGT), check_vma=False
    )
```

time: 204 us -> 122 us (0.60)
  waiting for transfers between devices: 92.7 us -> 31.4 us
  starting transfers between devices: 4.01 us -> 59.9 us
  blocking collectives: 53.1 us -> 0 us
  other arithmetic: 30.2 us -> 3.34 us
  Pallas kernels: 0 us -> 21.5 us
  between operations: 14.2 us -> 0.23 us
  matrix products: 6.08 us -> 0 us
    all_gather x1 -> x0, waiting for transfers between devices: 86.8 us -> none  [body(): tgt_whole = lax.all_gather(tgt_emb, SRC, axis=1, tiled=True)]
    ppermute x0 -> x28, starting transfers between devices: none -> 52.3 us  [shifted(): lax.ppermute(array, axis, [(i, (i + by) % size) for i in range(size)])]
    all_gather x3 -> x0, blocking collectives: 32.6 us -> none  [joined_all(): pieces = lax.all_gather(array.astype(jnp.bfloat16), axis)]
    ppermute x0 -> x28, waiting for transfers between devices: none -> 28.3 us  [shifted(): lax.ppermute(array, axis, [(i, (i + by) % size) for i in range(size)])]
    pallas_call x0 -> x4, Pallas kernels: none -> 21.5 us  [the longest x2 12.8 us: scores_and_lists(): pl.pallas_call(functools.partial(score_kernel, len(blocks), side), out_sh...]
    all_to_all x1 -> x0, blocking collectives: 20.4 us -> none  [from_everyone(): lax.all_to_all(jnp.broadcast_to(array[None], (size, *array.shape)), axis,...]
    reduce_sum x16 -> x0, other arithmetic: 12.8 us -> none  [the longest x14 7.35 us: best_four(): counts.append(jnp.sum((values == level).astype(jnp.int32), axis=axis))]
    reduce_max x58 -> x0, other arithmetic: 9.79 us -> none  [best_four(): level = jnp.max(below, axis=axis, keepdims=True)]
  transfers between devices with their start and end apart: 2 -> 29, of which waited for: 2 -> 15; matrix products, arithmetic and copies ran while one was open for 1% -> 5% of each run, Pallas kernels for 0% -> 0%
where the time goes in v2:
time: 122 us; the launch traced here: 121 us
  starting transfers between devices  59.9 us (49%)
  waiting for transfers between devices  31.4 us (26%)
  Pallas kernels  21.5 us (18%)
  local copies, waits for them, and re-layouts  4.89 us (4%)
  other arithmetic  3.34 us (3%)
    ppermute x28, starting transfers between devices, shifted(): lax.ppermute(array, axis, [(i, (i + by) % size) for i in range(size)])  52.3 us
    ppermute x28, waiting for transfers between devices, shifted(): lax.ppermute(array, axis, [(i, (i + by) % size) for i in range(size)])  28.3 us
    pallas_call x2, Pallas kernels, scores_and_lists(): pl.pallas_call(functools.partial(score_kernel, len(blocks), side), out_sh...  12.8 us
    pallas_call x1, Pallas kernels, margin(): pl.pallas_call(margin_kernel, grid=(rows_n // block,), out_shape=jax.Shap...  8.19 us
    all_to_all x1, starting transfers between devices, from_everyone(): return lax.all_to_all(spread, axes, 0, 0, tiled=True)  7.53 us
    all_to_all x1, waiting for transfers between devices, from_everyone(): return lax.all_to_all(spread, axes, 0, 0, tiled=True)  3.02 us
    unnamed x10, local copies, waits for them, and re-layouts  2.51 us
  transfers between devices with their start and end apart: 29, of which 15 were waited for; matrix products, arithmetic and copies ran while one was open for 5% of the time, Pallas kernels for 0%

profile of v2, /device:TPU:1, one launch (start us, length us, event | category | flops | bytes accessed | tf_op | source)
XLA Modules:
  0.0 121.2 jit_solution(16551399626175594376)
XLA Ops:
  0.0 2.1 %collective-permute-start.16 = (bf16[512,128]{1,0:T(8,128)(2,1)}, bf16[512,128]{1,0:T(8,128)(2,1)S(1)}, u32[]{:S(2)}, u32[]{:S(2)}) collective-permute-start(bf16[512,128]{1,0:T(8,128)(2,1)} %own_ref.1), channel_id=1, source_target_pairs={{0,4},{4,0},{1,5},{5,1},{2,6},{6,2},{3,7},{7,3},{8,12},{12,8},{9,1... | collective-permute-start | bytes 393224 | tf_op jit(solution)/shard_map/ppermute | solution.py:318
  5.6 3.5 %collective-permute-start.19 = (bf16[2,512,128]{2,1,0:T(8,128)(2,1)S(1)}, bf16[2,512,128]{2,1,0:T(8,128)(2,1)S(1)}, u32[]{:S(2)}, u32[]{:S(2)}) collective-permute-start(bf16[2,512,128]{2,1,0:T(8,128)(2,1)S(1)} %pad_maximum_fusion.1), channel_id=1, source_target_pairs={{0,2},{1,3},{2,0},{3,1},{4,6},{5,7},{6,4},{7,5},{8,10},{9,11},{10,... | collective-permute-start | bytes 786440 | tf_op jit(solution)/shard_map/ppermute | solution.py:318
  10.2 1.7 %collective-permute-start.2 = (bf16[64,2048]{1,0:T(8,128)(2,1)S(1)}, bf16[64,2048]{1,0:T(8,128)(2,1)S(1)}, u32[]{:S(2)}, u32[]{:S(2)}) collective-permute-start(bf16[64,2048]{1,0:T(8,128)(2,1)S(1)} %pad_maximum_fusion.refs_0_), channel_id=1, source_target_pairs={{0,32},{32,64},{64,96},{96,128},{128,160},{160,192},{192,224},{224... | collective-permute-start | bytes 786440 | tf_op jit(solution)/shard_map/ppermute | solution.py:318
  13.3 4.0 %collective-permute-start.4 = (bf16[64,2048]{1,0:T(8,128)(2,1)S(1)}, bf16[64,2048]{1,0:T(8,128)(2,1)S(1)}, u32[]{:S(2)}, u32[]{:S(2)}) collective-permute-start(bf16[64,2048]{1,0:T(8,128)(2,1)S(1)} %pad_maximum_fusion.refs_0_), channel_id=1, source_target_pairs={{0,224},{32,0},{64,32},{96,64},{128,96},{160,128},{192,160},{224,1... | collective-permute-start | bytes 786440 | tf_op jit(solution)/shard_map/ppermute | solution.py:318
  17.4 2.9 %collective-permute-start.1 = (bf16[64,2048]{1,0:T(8,128)(2,1)S(1)}, bf16[64,2048]{1,0:T(8,128)(2,1)S(1)}, u32[]{:S(2)}, u32[]{:S(2)}) collective-permute-start(bf16[64,2048]{1,0:T(8,128)(2,1)S(1)} %pad_maximum_fusion.refs_0_), channel_id=1, source_target_pairs={{0,16},{16,0},{1,17},{17,1},{2,18},{18,2},{3,19},{19,3},{4,20},{20... | collective-permute-start | bytes 786440 | tf_op jit(solution)/shard_map/ppermute | solution.py:318
  22.7 2.4 %collective-permute-start.20 = (bf16[512,1024]{1,0:T(8,128)(2,1)S(1)}, bf16[512,1024]{1,0:T(8,128)(2,1)S(1)}, u32[]{:S(2)}, u32[]{:S(2)}) collective-permute-start(bf16[512,1024]{1,0:T(8,128)(2,1)S(1)} %unit.1.refs_16_), channel_id=1, source_target_pairs={{0,8},{8,0},{1,9},{9,1},{2,10},{10,2},{3,11},{11,3},{4,12},{12,4},... | collective-permute-start | bytes 3145736 | tf_op jit(solution)/shard_map/ppermute | solution.py:318
  25.1 4.7 %collective-permute-start.8 = (bf16[64,2048]{1,0:T(8,128)(2,1)S(1)}, bf16[64,2048]{1,0:T(8,128)(2,1)S(1)}, u32[]{:S(2)}, u32[]{:S(2)}) collective-permute-start(bf16[64,2048]{1,0:T(8,128)(2,1)S(1)} %collective-permute-done.4.refs_4_), channel_id=1, source_target_pairs={{0,224},{32,0},{64,32},{96,64},{128,96},{160,128},{192,160},{224,1... | collective-permute-start | bytes 786440 | tf_op jit(solution)/shard_map/ppermute | solution.py:318
  31.2 1.3 %collective-permute-start.21 = (s32[512]{0:T(512)S(1)}, s32[512]{0:T(512)S(1)}, u32[]{:S(2)}, u32[]{:S(2)}) collective-permute-start(s32[512]{0:T(512)S(1)} %copy-done.3), channel_id=1, source_target_pairs={{0,8},{8,0},{1,9},{9,1},{2,10},{10,2},{3,11},{11,3},{4,12},{12,4},... | collective-permute-start | bytes 6152 | tf_op jit(solution)/shard_map/ppermute | solution.py:318
  33.4 2.0 %collective-permute-done.8.refs_8_ = bf16[64,2048]{1,0:T(8,128)(2,1)S(1)} collective-permute-done((bf16[64,2048]{1,0:T(8,128)(2,1)S(1)}, bf16[64,2048]{1,0:T(8,128)(2,1)S(1)}, u32[]{:S(2)}, u32[]{:S(2)}) %collective-permute-start.8) | collective-permute-done | bytes 262176 | tf_op jit(solution)/shard_map/ppermute | solution.py:318
  35.4 3.4 %collective-permute-start.12 = (bf16[64,2048]{1,0:T(8,128)(2,1)S(1)}, bf16[64,2048]{1,0:T(8,128)(2,1)S(1)}, u32[]{:S(2)}, u32[]{:S(2)}) collective-permute-start(bf16[64,2048]{1,0:T(8,128)(2,1)S(1)} %collective-permute-done.8.refs_8_), channel_id=1, source_target_pairs={{0,224},{32,0},{64,32},{96,64},{128,96},{160,128},{192,160},{224,1... | collective-permute-start | bytes 786440 | tf_op jit(solution)/shard_map/ppermute | solution.py:318
  38.8 2.2 %collective-permute-done.5.refs_5_ = bf16[64,2048]{1,0:T(8,128)(2,1)S(1)} collective-permute-done((bf16[64,2048]{1,0:T(8,128)(2,1)S(1)}, bf16[64,2048]{1,0:T(8,128)(2,1)S(1)}, u32[]{:S(2)}, u32[]{:S(2)}) %collective-permute-start.5) | collective-permute-done | bytes 262176 | tf_op jit(solution)/shard_map/ppermute | solution.py:318
  41.0 3.4 %collective-permute-start.9 = (bf16[64,2048]{1,0:T(8,128)(2,1)S(1)}, bf16[64,2048]{1,0:T(8,128)(2,1)S(1)}, u32[]{:S(2)}, u32[]{:S(2)}) collective-permute-start(bf16[64,2048]{1,0:T(8,128)(2,1)S(1)} %collective-permute-done.5.refs_5_), channel_id=1, source_target_pairs={{0,224},{32,0},{64,32},{96,64},{128,96},{160,128},{192,160},{224,1... | collective-permute-start | bytes 786440 | tf_op jit(solution)/shard_map/ppermute | solution.py:318
  44.5 2.1 %collective-permute-done.12.refs_12_ = bf16[64,2048]{1,0:T(8,128)(2,1)S(1)} collective-permute-done((bf16[64,2048]{1,0:T(8,128)(2,1)S(1)}, bf16[64,2048]{1,0:T(8,128)(2,1)S(1)}, u32[]{:S(2)}, u32[]{:S(2)}) %collective-permute-start.12) | collective-permute-done | bytes 262176 | tf_op jit(solution)/shard_map/ppermute | solution.py:318
  46.7 2.9 %collective-permute-start.11 = (bf16[64,2048]{1,0:T(8,128)(2,1)S(1)}, bf16[64,2048]{1,0:T(8,128)(2,1)S(1)}, u32[]{:S(2)}, u32[]{:S(2)}) collective-permute-start(bf16[64,2048]{1,0:T(8,128)(2,1)S(1)} %collective-permute-done.10.refs_10_), channel_id=1, source_target_pairs={{0,16},{16,0},{1,17},{17,1},{2,18},{18,2},{3,19},{19,3},{4,20},{20... | collective-permute-start | bytes 786440 | tf_op jit(solution)/shard_map/ppermute | solution.py:318
  49.6 2.7 %collective-permute-done.9.refs_9_ = bf16[64,2048]{1,0:T(8,128)(2,1)S(1)} collective-permute-done((bf16[64,2048]{1,0:T(8,128)(2,1)S(1)}, bf16[64,2048]{1,0:T(8,128)(2,1)S(1)}, u32[]{:S(2)}, u32[]{:S(2)}) %collective-permute-start.9) | collective-permute-done | bytes 262176 | tf_op jit(solution)/shard_map/ppermute | solution.py:318
  52.3 2.9 %collective-permute-start.13 = (bf16[64,2048]{1,0:T(8,128)(2,1)S(1)}, bf16[64,2048]{1,0:T(8,128)(2,1)S(1)}, u32[]{:S(2)}, u32[]{:S(2)}) collective-permute-start(bf16[64,2048]{1,0:T(8,128)(2,1)S(1)} %collective-permute-done.12.refs_12_), channel_id=1, source_target_pairs={{0,16},{16,0},{1,17},{17,1},{2,18},{18,2},{3,19},{19,3},{4,20},{20... | collective-permute-start | bytes 786440 | tf_op jit(solution)/shard_map/ppermute | solution.py:318
  55.3 2.2 %collective-permute-done.7.refs_7_ = bf16[64,2048]{1,0:T(8,128)(2,1)S(1)} collective-permute-done((bf16[64,2048]{1,0:T(8,128)(2,1)S(1)}, bf16[64,2048]{1,0:T(8,128)(2,1)S(1)}, u32[]{:S(2)}, u32[]{:S(2)}) %collective-permute-start.7) | collective-permute-done | bytes 262176 | tf_op jit(solution)/shard_map/ppermute | solution.py:318
  57.5 3.3 %collective-permute-done.13.refs_13_ = bf16[64,2048]{1,0:T(8,128)(2,1)S(1)} collective-permute-done((bf16[64,2048]{1,0:T(8,128)(2,1)S(1)}, bf16[64,2048]{1,0:T(8,128)(2,1)S(1)}, u32[]{:S(2)}, u32[]{:S(2)}) %collective-permute-start.13) | collective-permute-done | bytes 262176 | tf_op jit(solution)/shard_map/ppermute | solution.py:318
  60.7 5.6 %collective-permute-done.15.refs_15_ = bf16[64,2048]{1,0:T(8,128)(2,1)S(1)} collective-permute-done((bf16[64,2048]{1,0:T(8,128)(2,1)S(1)}, bf16[64,2048]{1,0:T(8,128)(2,1)S(1)}, u32[]{:S(2)}, u32[]{:S(2)}) %collective-permute-start.15) | collective-permute-done | bytes 262176 | tf_op jit(solution)/shard_map/ppermute | solution.py:318
  66.3 6.4 %scores0.1 = (f32[512,1024]{1,0:T(8,128)}, f32[512,1024]{1,0:T(8,128)}, f32[4,512]{1,0:T(4,128)S(1)}, f32[4,512]{1,0:T(4,128)S(1)}, bf16[4,1024]{1,0:T(4,128)(2,1)S(1)}) custom-call(bf16[64,2048]{1,0:T(8,128)(2,1)S(1)} %pad_maximum_fusion.refs_0_, bf16[64,2048]{1,0:T(8,128)(2,1)S(1)} %collective-permute-done.1.refs_1_, ...), custom_call_target="tpu_custom_call" | custom-call | flops 2147483648 | bytes 9437184 | tf_op jit(solution)/shard_map/scores0/pallas_call | solution.py:204
  72.7 6.4 %scores1.1 = (f32[512,1024]{1,0:T(8,128)}, f32[512,1024]{1,0:T(8,128)}, f32[4,512]{1,0:T(4,128)S(1)}, f32[4,512]{1,0:T(4,128)S(1)}, bf16[4,1024]{1,0:T(4,128)(2,1)S(1)}) custom-call(bf16[64,2048]{1,0:T(8,128)(2,1)S(1)} %pad_maximum_fusion.refs_0_, bf16[64,2048]{1,0:T(8,128)(2,1)S(1)} %collective-permute-done.1.refs_1_, ...), custom_call_target="tpu_custom_call" | custom-call | flops 2147483648 | bytes 9437184 | tf_op jit(solution)/shard_map/scores1/pallas_call | solution.py:204
  79.2 1.4 %collective-permute-start.24 = (f32[8,512]{1,0:T(8,128)S(1)}, f32[8,512]{1,0:T(8,128)S(1)}, u32[]{:S(2)}, u32[]{:S(2)}) collective-permute-start(f32[8,512]{1,0:T(8,128)S(1)} %pad_maximum_fusion.2), channel_id=1, source_target_pairs={{0,4},{4,0},{1,5},{5,1},{2,6},{6,2},{3,7},{7,3},{8,12},{12,8},{9,1... | collective-permute-start | bytes 49160 | tf_op jit(solution)/shard_map/ppermute | solution.py:318
  80.6 1.3 %collective-permute-done.24 = f32[8,512]{1,0:T(8,128)S(1)} collective-permute-done((f32[8,512]{1,0:T(8,128)S(1)}, f32[8,512]{1,0:T(8,128)S(1)}, u32[]{:S(2)}, u32[]{:S(2)}) %collective-permute-start.24) | collective-permute-done | bytes 16416 | tf_op jit(solution)/shard_map/ppermute | solution.py:318
  82.0 2.4 %collective-permute-start.25 = (f32[8,512]{1,0:T(8,128)S(1)}, f32[8,512]{1,0:T(8,128)S(1)}, u32[]{:S(2)}, u32[]{:S(2)}) collective-permute-start(f32[8,512]{1,0:T(8,128)S(1)} %stack.15), channel_id=1, source_target_pairs={{0,2},{1,3},{2,0},{3,1},{4,6},{5,7},{6,4},{7,5},{8,10},{9,11},{10,... | collective-permute-start | bytes 49160 | tf_op jit(solution)/shard_map/ppermute | solution.py:318
  85.2 7.5 %all-to-all-start = ((bf16[16,4,2048]{2,1,0:T(4,128)(2,1)}), bf16[16,4,2048]{2,1,0:T(4,128)(2,1)S(1)}, u32[]{:S(2)}, u32[]{:S(2)}) async-start(bf16[16,4,2048]{2,1,0:T(4,128)(2,1)} %broadcast_in_dim.15), calls=%async_computation | async-start | bytes 524288 | tf_op jit(solution)/shard_map/all_to_all | solution.py:323
  92.7 3.6 %collective-permute-start.23 = (f32[512,1024]{1,0:T(8,128)}, f32[512,1024]{1,0:T(8,128)}, u32[]{:S(2)}, u32[]{:S(2)}) collective-permute-start(f32[512,1024]{1,0:T(8,128)} %get-tuple-element.20), channel_id=1, source_target_pairs={{0,8},{8,0},{1,9},{9,1},{2,10},{10,2},{3,11},{11,3},{4,12},{12,4},... | collective-permute-start | bytes 6291464 | tf_op jit(solution)/shard_map/ppermute | solution.py:318
  97.2 3.8 %collective-permute-done.26 = f32[8,512]{1,0:T(8,128)S(1)} collective-permute-done((f32[8,512]{1,0:T(8,128)S(1)}, f32[8,512]{1,0:T(8,128)S(1)}, u32[]{:S(2)}, u32[]{:S(2)}) %collective-permute-start.26) | collective-permute-done | bytes 16416 | tf_op jit(solution)/shard_map/ppermute | solution.py:318
  101.0 3.0 %all-to-all-done = bf16[16,4,2048]{2,1,0:T(4,128)(2,1)S(1)} async-done(((bf16[16,4,2048]{2,1,0:T(4,128)(2,1)}), bf16[16,4,2048]{2,1,0:T(4,128)(2,1)S(1)}, u32[]{:S(2)}, u32[]{:S(2)}) %all-to-all-start) | async-done | bytes 262176 | tf_op jit(solution)/shard_map/all_to_all | solution.py:323
  104.6 1.2 %fusion = (f32[2048]{0:T(1024)S(1)}, f32[1,1,2048]{2,1,0:T(1,128)S(1)}) fusion(f32[]{:T(128)} %broadcast.17, f32[16,4,2048]{2,1,0:T(4,128)S(1)} %convert_element_type.3), kind=kLoop, calls=%fused_computation.95 | loop fusion | flops 376832 | bytes 540676 | tf_op jit(solution)/shard_map/mul | solution.py:398
  105.9 4.6 %collective-permute-start.27 = (f32[8,512]{1,0:T(8,128)S(1)}, f32[8,512]{1,0:T(8,128)S(1)}, u32[]{:S(2)}, u32[]{:S(2)}) collective-permute-start(f32[8,512]{1,0:T(8,128)S(1)} %concatenate.26), channel_id=1, source_target_pairs={{0,8},{8,0},{1,9},{9,1},{2,10},{10,2},{3,11},{11,3},{4,12},{12,4},... | collective-permute-start | bytes 49160 | tf_op jit(solution)/shard_map/ppermute | solution.py:318
  111.4 1.6 %copy-done.1 = f32[512,1024]{1,0:T(8,128)S(1)} copy-done((f32[512,1024]{1,0:T(8,128)S(1)}, f32[512,1024]{1,0:T(8,128)}, u32[]{:S(2)}) %copy-start.1) | copy-done | bytes 2097176
  113.0 8.2 %margin.1 = f32[512,4096]{1,0:T(8,128)} custom-call(f32[512,1024]{1,0:T(8,128)S(1)} %copy-done, f32[512,1024]{1,0:T(8,128)S(1)} %copy-done.1, f32[512,1024]{1,0:T(8,128)} %collective-permute-done.22.got0, f32[512,1024]{1,0:T(8,128)} %collective-permute-done.23.got1, f32[4,512]{1,0:T(4,128)S(1)} %pad_maximum_fusion.4.row_ref, f32[1,2048]{1,0:T(1,128)S(1)} %bitcast.16, ...), custom_call_target="tpu_custom_call" | custom-call | tf_op jit(solution)/shard_map/margin/pallas_call | solution.py:303
  (68 shorter events, 14.1 us)
Async XLA Ops:
  0.0 31.2 %copy-start.3 = (s32[512]{0:T(512)S(1)}, s32[512]{0:T(512)}, u32[]{:S(2)}) copy-start(s32[512]{0:T(512)} %param.6) | copy-start | bytes 6148
  0.0 4.7 %collective-permute-start.16 = (bf16[512,128]{1,0:T(8,128)(2,1)}, bf16[512,128]{1,0:T(8,128)(2,1)S(1)}, u32[]{:S(2)}, u32[]{:S(2)}) collective-permute-start(bf16[512,128]{1,0:T(8,128)(2,1)} %own_ref.1), channel_id=1, source_target_pairs={{0,4},{4,0},{1,5},{5,1},{2,6},{6,2},{3,7},{7,3},{8,12},{12,8},{9,1... | collective-permute-start | bytes 393224 | tf_op jit(solution)/shard_map/ppermute | solution.py:318
  3.0 6.1 %collective-permute-start = (bf16[32,2048]{1,0:T(8,128)(2,1)S(1)}, bf16[32,2048]{1,0:T(8,128)(2,1)S(1)}, u32[]{:S(2)}, u32[]{:S(2)}) collective-permute-start(bf16[32,2048]{1,0:T(8,128)(2,1)S(1)} %dynamic-slice_bitcast_fusion), channel_id=1, source_target_pairs={{0,8},{8,0},{1,9},{9,1},{2,10},{10,2},{3,11},{11,3},{4,12},{12,4},... | collective-permute-start | bytes 393224 | tf_op jit(solution)/shard_map/ppermute | solution.py:318
  4.3 51.0 %dynamic-slice-start = ((s32[4096]{0:T(1024)}, s32[]{:T(128)}), s32[2048]{0:T(1024)S(1)}, s32[]{:S(2)}) async-start(s32[4096]{0:T(1024)} %param.7, s32[]{:T(128)} %select_n.20), calls=%async_computation.1 | async-start | bytes 16896 | tf_op jit(solution)/shard_map/dynamic_slice | solution.py:373
  5.6 11.7 %collective-permute-start.19 = (bf16[2,512,128]{2,1,0:T(8,128)(2,1)S(1)}, bf16[2,512,128]{2,1,0:T(8,128)(2,1)S(1)}, u32[]{:S(2)}, u32[]{:S(2)}) collective-permute-start(bf16[2,512,128]{2,1,0:T(8,128)(2,1)S(1)} %pad_maximum_fusion.1), channel_id=1, source_target_pairs={{0,2},{1,3},{2,0},{3,1},{4,6},{5,7},{6,4},{7,5},{8,10},{9,11},{10,... | collective-permute-start | bytes 786440 | tf_op jit(solution)/shard_map/ppermute | solution.py:318
  10.2 10.4 %collective-permute-start.2 = (bf16[64,2048]{1,0:T(8,128)(2,1)S(1)}, bf16[64,2048]{1,0:T(8,128)(2,1)S(1)}, u32[]{:S(2)}, u32[]{:S(2)}) collective-permute-start(bf16[64,2048]{1,0:T(8,128)(2,1)S(1)} %pad_maximum_fusion.refs_0_), channel_id=1, source_target_pairs={{0,32},{32,64},{64,96},{96,128},{128,160},{160,192},{192,224},{224... | collective-permute-start | bytes 786440 | tf_op jit(solution)/shard_map/ppermute | solution.py:318
  11.9 8.7 %collective-permute-start.18 = (bf16[2,512,128]{2,1,0:T(8,128)(2,1)S(1)}, bf16[2,512,128]{2,1,0:T(8,128)(2,1)S(1)}, u32[]{:S(2)}, u32[]{:S(2)}) collective-permute-start(bf16[2,512,128]{2,1,0:T(8,128)(2,1)S(1)} %pad_maximum_fusion.1), channel_id=1, source_target_pairs={{0,3},{1,0},{2,1},{3,2},{4,7},{5,4},{6,5},{7,6},{8,11},{9,8},{10,9... | collective-permute-start | bytes 786440 | tf_op jit(solution)/shard_map/ppermute | solution.py:318
  12.7 8.6 %collective-permute-start.17 = (bf16[2,512,128]{2,1,0:T(8,128)(2,1)S(1)}, bf16[2,512,128]{2,1,0:T(8,128)(2,1)S(1)}, u32[]{:S(2)}, u32[]{:S(2)}) collective-permute-start(bf16[2,512,128]{2,1,0:T(8,128)(2,1)S(1)} %pad_maximum_fusion.1), channel_id=1, source_target_pairs={{0,1},{1,2},{2,3},{3,0},{4,5},{5,6},{6,7},{7,4},{8,9},{9,10},{10,1... | collective-permute-start | bytes 786440 | tf_op jit(solution)/shard_map/ppermute | solution.py:318
  13.3 11.8 %collective-permute-start.4 = (bf16[64,2048]{1,0:T(8,128)(2,1)S(1)}, bf16[64,2048]{1,0:T(8,128)(2,1)S(1)}, u32[]{:S(2)}, u32[]{:S(2)}) collective-permute-start(bf16[64,2048]{1,0:T(8,128)(2,1)S(1)} %pad_maximum_fusion.refs_0_), channel_id=1, source_target_pairs={{0,224},{32,0},{64,32},{96,64},{128,96},{160,128},{192,160},{224,1... | collective-permute-start | bytes 786440 | tf_op jit(solution)/shard_map/ppermute | solution.py:318
  17.4 12.4 %collective-permute-start.1 = (bf16[64,2048]{1,0:T(8,128)(2,1)S(1)}, bf16[64,2048]{1,0:T(8,128)(2,1)S(1)}, u32[]{:S(2)}, u32[]{:S(2)}) collective-permute-start(bf16[64,2048]{1,0:T(8,128)(2,1)S(1)} %pad_maximum_fusion.refs_0_), channel_id=1, source_target_pairs={{0,16},{16,0},{1,17},{17,1},{2,18},{18,2},{3,19},{19,3},{4,20},{20... | collective-permute-start | bytes 786440 | tf_op jit(solution)/shard_map/ppermute | solution.py:318
  20.6 10.1 %collective-permute-start.6 = (bf16[64,2048]{1,0:T(8,128)(2,1)S(1)}, bf16[64,2048]{1,0:T(8,128)(2,1)S(1)}, u32[]{:S(2)}, u32[]{:S(2)}) collective-permute-start(bf16[64,2048]{1,0:T(8,128)(2,1)S(1)} %collective-permute-done.2.refs_2_), channel_id=1, source_target_pairs={{0,32},{32,64},{64,96},{96,128},{128,160},{160,192},{192,224},{224... | collective-permute-start | bytes 786440 | tf_op jit(solution)/shard_map/ppermute | solution.py:318
  22.7 38.0 %collective-permute-start.20 = (bf16[512,1024]{1,0:T(8,128)(2,1)S(1)}, bf16[512,1024]{1,0:T(8,128)(2,1)S(1)}, u32[]{:S(2)}, u32[]{:S(2)}) collective-permute-start(bf16[512,1024]{1,0:T(8,128)(2,1)S(1)} %unit.1.refs_16_), channel_id=1, source_target_pairs={{0,8},{8,0},{1,9},{9,1},{2,10},{10,2},{3,11},{11,3},{4,12},{12,4},... | collective-permute-start | bytes 3145736 | tf_op jit(solution)/shard_map/ppermute | solution.py:318
  25.1 10.3 %collective-permute-start.8 = (bf16[64,2048]{1,0:T(8,128)(2,1)S(1)}, bf16[64,2048]{1,0:T(8,128)(2,1)S(1)}, u32[]{:S(2)}, u32[]{:S(2)}) collective-permute-start(bf16[64,2048]{1,0:T(8,128)(2,1)S(1)} %collective-permute-done.4.refs_4_), channel_id=1, source_target_pairs={{0,224},{32,0},{64,32},{96,64},{128,96},{160,128},{192,160},{224,1... | collective-permute-start | bytes 786440 | tf_op jit(solution)/shard_map/ppermute | solution.py:318
  29.8 11.3 %collective-permute-start.5 = (bf16[64,2048]{1,0:T(8,128)(2,1)S(1)}, bf16[64,2048]{1,0:T(8,128)(2,1)S(1)}, u32[]{:S(2)}, u32[]{:S(2)}) collective-permute-start(bf16[64,2048]{1,0:T(8,128)(2,1)S(1)} %collective-permute-done.1.refs_1_), channel_id=1, source_target_pairs={{0,224},{32,0},{64,32},{96,64},{128,96},{160,128},{192,160},{224,1... | collective-permute-start | bytes 786440 | tf_op jit(solution)/shard_map/ppermute | solution.py:318
  30.7 13.7 %collective-permute-start.10 = (bf16[64,2048]{1,0:T(8,128)(2,1)S(1)}, bf16[64,2048]{1,0:T(8,128)(2,1)S(1)}, u32[]{:S(2)}, u32[]{:S(2)}) collective-permute-start(bf16[64,2048]{1,0:T(8,128)(2,1)S(1)} %collective-permute-done.6.refs_6_), channel_id=1, source_target_pairs={{0,32},{32,64},{64,96},{96,128},{128,160},{160,192},{192,224},{224... | collective-permute-start | bytes 786440 | tf_op jit(solution)/shard_map/ppermute | solution.py:318
  31.2 2.1 %collective-permute-start.21 = (s32[512]{0:T(512)S(1)}, s32[512]{0:T(512)S(1)}, u32[]{:S(2)}, u32[]{:S(2)}) collective-permute-start(s32[512]{0:T(512)S(1)} %copy-done.3), channel_id=1, source_target_pairs={{0,8},{8,0},{1,9},{9,1},{2,10},{10,2},{3,11},{11,3},{4,12},{12,4},... | collective-permute-start | bytes 6152 | tf_op jit(solution)/shard_map/ppermute | solution.py:318
  33.4 11.1 %collective-permute-start.3 = (bf16[64,2048]{1,0:T(8,128)(2,1)S(1)}, bf16[64,2048]{1,0:T(8,128)(2,1)S(1)}, u32[]{:S(2)}, u32[]{:S(2)}) collective-permute-start(bf16[64,2048]{1,0:T(8,128)(2,1)S(1)} %collective-permute-done.1.refs_1_), channel_id=1, source_target_pairs={{0,32},{32,64},{64,96},{96,128},{128,160},{160,192},{192,224},{224... | collective-permute-start | bytes 786440 | tf_op jit(solution)/shard_map/ppermute | solution.py:318
  35.4 11.2 %collective-permute-start.12 = (bf16[64,2048]{1,0:T(8,128)(2,1)S(1)}, bf16[64,2048]{1,0:T(8,128)(2,1)S(1)}, u32[]{:S(2)}, u32[]{:S(2)}) collective-permute-start(bf16[64,2048]{1,0:T(8,128)(2,1)S(1)} %collective-permute-done.8.refs_8_), channel_id=1, source_target_pairs={{0,224},{32,0},{64,32},{96,64},{128,96},{160,128},{192,160},{224,1... | collective-permute-start | bytes 786440 | tf_op jit(solution)/shard_map/ppermute | solution.py:318
  41.0 11.2 %collective-permute-start.9 = (bf16[64,2048]{1,0:T(8,128)(2,1)S(1)}, bf16[64,2048]{1,0:T(8,128)(2,1)S(1)}, u32[]{:S(2)}, u32[]{:S(2)}) collective-permute-start(bf16[64,2048]{1,0:T(8,128)(2,1)S(1)} %collective-permute-done.5.refs_5_), channel_id=1, source_target_pairs={{0,224},{32,0},{64,32},{96,64},{128,96},{160,128},{192,160},{224,1... | collective-permute-start | bytes 786440 | tf_op jit(solution)/shard_map/ppermute | solution.py:318
  44.4 10.7 %collective-permute-start.14 = (bf16[64,2048]{1,0:T(8,128)(2,1)S(1)}, bf16[64,2048]{1,0:T(8,128)(2,1)S(1)}, u32[]{:S(2)}, u32[]{:S(2)}) collective-permute-start(bf16[64,2048]{1,0:T(8,128)(2,1)S(1)} %collective-permute-done.10.refs_10_), channel_id=1, source_target_pairs={{0,32},{32,64},{64,96},{96,128},{128,160},{160,192},{192,224},{224... | collective-permute-start | bytes 786440 | tf_op jit(solution)/shard_map/ppermute | solution.py:318
  44.5 13.0 %collective-permute-start.7 = (bf16[64,2048]{1,0:T(8,128)(2,1)S(1)}, bf16[64,2048]{1,0:T(8,128)(2,1)S(1)}, u32[]{:S(2)}, u32[]{:S(2)}) collective-permute-start(bf16[64,2048]{1,0:T(8,128)(2,1)S(1)} %collective-permute-done.3.refs_3_), channel_id=1, source_target_pairs={{0,32},{32,64},{64,96},{96,128},{128,160},{160,192},{192,224},{224... | collective-permute-start | bytes 786440 | tf_op jit(solution)/shard_map/ppermute | solution.py:318
  46.7 14.1 %collective-permute-start.11 = (bf16[64,2048]{1,0:T(8,128)(2,1)S(1)}, bf16[64,2048]{1,0:T(8,128)(2,1)S(1)}, u32[]{:S(2)}, u32[]{:S(2)}) collective-permute-start(bf16[64,2048]{1,0:T(8,128)(2,1)S(1)} %collective-permute-done.10.refs_10_), channel_id=1, source_target_pairs={{0,16},{16,0},{1,17},{17,1},{2,18},{18,2},{3,19},{19,3},{4,20},{20... | collective-permute-start | bytes 786440 | tf_op jit(solution)/shard_map/ppermute | solution.py:318
  52.3 8.5 %collective-permute-start.13 = (bf16[64,2048]{1,0:T(8,128)(2,1)S(1)}, bf16[64,2048]{1,0:T(8,128)(2,1)S(1)}, u32[]{:S(2)}, u32[]{:S(2)}) collective-permute-start(bf16[64,2048]{1,0:T(8,128)(2,1)S(1)} %collective-permute-done.12.refs_12_), channel_id=1, source_target_pairs={{0,16},{16,0},{1,17},{17,1},{2,18},{18,2},{3,19},{19,3},{4,20},{20... | collective-permute-start | bytes 786440 | tf_op jit(solution)/shard_map/ppermute | solution.py:318
  55.2 11.2 %collective-permute-start.15 = (bf16[64,2048]{1,0:T(8,128)(2,1)S(1)}, bf16[64,2048]{1,0:T(8,128)(2,1)S(1)}, u32[]{:S(2)}, u32[]{:S(2)}) collective-permute-start(bf16[64,2048]{1,0:T(8,128)(2,1)S(1)} %collective-permute-done.14.refs_14_), channel_id=1, source_target_pairs={{0,16},{16,0},{1,17},{17,1},{2,18},{18,2},{3,19},{19,3},{4,20},{20... | collective-permute-start | bytes 786440 | tf_op jit(solution)/shard_map/ppermute | solution.py:318
  79.2 32.2 %copy-start = (f32[512,1024]{1,0:T(8,128)S(1)}, f32[512,1024]{1,0:T(8,128)}, u32[]{:S(2)}) copy-start(f32[512,1024]{1,0:T(8,128)} %get-tuple-element.15.kept0) | copy-start | bytes 6291460
  79.2 2.7 %collective-permute-start.24 = (f32[8,512]{1,0:T(8,128)S(1)}, f32[8,512]{1,0:T(8,128)S(1)}, u32[]{:S(2)}, u32[]{:S(2)}) collective-permute-start(f32[8,512]{1,0:T(8,128)S(1)} %pad_maximum_fusion.2), channel_id=1, source_target_pairs={{0,4},{4,0},{1,5},{5,1},{2,6},{6,2},{3,7},{7,3},{8,12},{12,8},{9,1... | collective-permute-start | bytes 49160 | tf_op jit(solution)/shard_map/ppermute | solution.py:318
  82.0 14.7 %collective-permute-start.25 = (f32[8,512]{1,0:T(8,128)S(1)}, f32[8,512]{1,0:T(8,128)S(1)}, u32[]{:S(2)}, u32[]{:S(2)}) collective-permute-start(f32[8,512]{1,0:T(8,128)S(1)} %stack.15), channel_id=1, source_target_pairs={{0,2},{1,3},{2,0},{3,1},{4,6},{5,7},{6,4},{7,5},{8,10},{9,11},{10,... | collective-permute-start | bytes 49160 | tf_op jit(solution)/shard_map/ppermute | solution.py:318
  85.2 18.8 %all-to-all-start = ((bf16[16,4,2048]{2,1,0:T(4,128)(2,1)}), bf16[16,4,2048]{2,1,0:T(4,128)(2,1)S(1)}, u32[]{:S(2)}, u32[]{:S(2)}) async-start(bf16[16,4,2048]{2,1,0:T(4,128)(2,1)} %broadcast_in_dim.15), calls=%async_computation | async-start | bytes 524288 | tf_op jit(solution)/shard_map/all_to_all | solution.py:323
  92.7 18.6 %collective-permute-start.23 = (f32[512,1024]{1,0:T(8,128)}, f32[512,1024]{1,0:T(8,128)}, u32[]{:S(2)}, u32[]{:S(2)}) collective-permute-start(f32[512,1024]{1,0:T(8,128)} %get-tuple-element.20), channel_id=1, source_target_pairs={{0,8},{8,0},{1,9},{9,1},{2,10},{10,2},{3,11},{11,3},{4,12},{12,4},... | collective-permute-start | bytes 6291464 | tf_op jit(solution)/shard_map/ppermute | solution.py:318
  96.3 15.1 %collective-permute-start.22 = (f32[512,1024]{1,0:T(8,128)}, f32[512,1024]{1,0:T(8,128)}, u32[]{:S(2)}, u32[]{:S(2)}) collective-permute-start(f32[512,1024]{1,0:T(8,128)} %get-tuple-element.19), channel_id=1, source_target_pairs={{0,8},{8,0},{1,9},{9,1},{2,10},{10,2},{3,11},{11,3},{4,12},{12,4},... | collective-permute-start | bytes 6291464 | tf_op jit(solution)/shard_map/ppermute | solution.py:318
  96.8 4.2 %collective-permute-start.26 = (f32[8,512]{1,0:T(8,128)S(1)}, f32[8,512]{1,0:T(8,128)S(1)}, u32[]{:S(2)}, u32[]{:S(2)}) collective-permute-start(f32[8,512]{1,0:T(8,128)S(1)} %stack.16), channel_id=1, source_target_pairs={{0,1},{1,2},{2,3},{3,0},{4,5},{5,6},{6,7},{7,4},{8,9},{9,10},{10,1... | collective-permute-start | bytes 49160 | tf_op jit(solution)/shard_map/ppermute | solution.py:318
  105.9 5.4 %collective-permute-start.27 = (f32[8,512]{1,0:T(8,128)S(1)}, f32[8,512]{1,0:T(8,128)S(1)}, u32[]{:S(2)}, u32[]{:S(2)}) collective-permute-start(f32[8,512]{1,0:T(8,128)S(1)} %concatenate.26), channel_id=1, source_target_pairs={{0,8},{8,0},{1,9},{9,1},{2,10},{10,2},{3,11},{11,3},{4,12},{12,4},... | collective-permute-start | bytes 49160 | tf_op jit(solution)/shard_map/ppermute | solution.py:318
  (2 other events, 2.5 us)

commit v3 on v2

--- a/solution.py
+++ b/solution.py
@@ -133,13 +133,16 @@
             same = jnp.concatenate([ids] * (tile // 128), axis=1) == tid
             dotted = dots[inside + k : inside + k + 8, :] * inverse
             x = jnp.where(same, jnp.float32(EXCLUDED), dotted)
-            stage[here, columns(u)] = x
             pieces.append(x)
             kept = tuple(rows[i, here, :] for i in range(4))
             four = sorted_four(*(x[:, p : p + 128] for p in range(0, tile, 128)))
             kept = merged(kept, four)
             for i in range(4):
                 rows[i, here, :] = kept[i]
+        for k in range(0, 4, 2):
+            here = slice(r + 8 * k, r + 8 * k + 16)
+            both = jnp.concatenate(pieces[k : k + 2], axis=0)
+            stage[here, columns(u)] = both.astype(stage.dtype)
         return merged(best, sorted_four(*pieces))
 
     def out_copy(k):
@@ -204,8 +207,8 @@
     return pl.pallas_call(
         functools.partial(score_kernel, len(blocks), side),
         out_shape=(
-            pltpu.HBM((half, width), jnp.float32),
-            pltpu.HBM((half, width), jnp.float32),
+            pltpu.HBM((half, width), jnp.bfloat16),
+            pltpu.HBM((half, width), jnp.bfloat16),
             jax.ShapeDtypeStruct((4, half), jnp.float32),
             jax.ShapeDtypeStruct((4, half), jnp.float32),
             jax.ShapeDtypeStruct((4, width), jnp.bfloat16),
@@ -219,7 +222,7 @@
             pltpu.VMEM((chunk, tile), jnp.float32),
             pltpu.VMEM((4, 2 * half, 128), jnp.float32),
             pltpu.VMEM((2 * half, 128), jnp.int32),
-            pltpu.VMEM((2 * half, width), jnp.float32),
+            pltpu.VMEM((2 * half, width), jnp.bfloat16),
             pltpu.SemaphoreType.DMA((width // tile, len(blocks))),
             pltpu.SemaphoreType.DMA((2,)),
             pltpu.SemaphoreType.DMA((width // tile * (2 * half // chunk),)),
@@ -232,38 +235,32 @@
     )(*blocks, *units, *rest)
 
 
-def unit_kernel(own_ref, beside_ref, *refs):
-    out_ref = refs[-1]
+def unit_kernel(src_ref, out_ref):
     rows_n = out_ref.shape[0]
-    yl = lax.axis_index("yl")
-    x = lax.axis_index("x")
     for r in range(0, rows_n, 64):
-        here = slice(r, r + 64)
-        pieces = [(own_ref[here, :], 0, 0), (beside_ref[here, :], 1, 0)]
-        for ref, dx in zip(refs, (3, 1, 2)):
-            pieces += [(ref[k, here, :], k, dx) for k in range(2)]
-        pieces = [(p.astype(jnp.float32), dy, dx) for p, dy, dx in pieces]
-        total = sum(p * p for p, _, _ in pieces)
+        pieces = [src_ref[j, r : r + 64, :].astype(jnp.float32) for j in range(8)]
+        total = sum(x * x for x in pieces)
         scale = jnp.sqrt(jnp.sum(total, axis=1, keepdims=True) + EPS)
-        for p, dy, dx in pieces:
-            owner = lax.rem(yl + dy, 2) * 4 + lax.rem(x + dx, 4)
-            cols = pl.ds(pl.multiple_of(owner * 128, 128), 128)
-            out_ref[here, cols] = (p / scale).astype(jnp.bfloat16)
-
-
-def unit_rows(own):
-    beside = shifted(own, "yl", 2, 1)
-    pair = jnp.stack([own, beside])
-    parts = [own, beside] + [shifted(pair, "x", 4, k) for k in (1, 3, 2)]
+        for j in range(8):
+            out_ref[r : r + 64, 128 * j : 128 * j + 128] = (pieces[j] / scale).astype(
+                jnp.bfloat16
+            )
+
+
+def after(array, others):
+    return lax.optimization_barrier((array, others))[0]
+
+
+def unit_rows(src_all):
     vmem = pl.BlockSpec(memory_space=pltpu.VMEM)
     return pl.pallas_call(
         unit_kernel,
-        out_shape=jax.ShapeDtypeStruct((own.shape[0], 1024), jnp.bfloat16),
-        in_specs=[vmem] * 5,
+        out_shape=jax.ShapeDtypeStruct((src_all.shape[1], 1024), jnp.bfloat16),
+        in_specs=[vmem],
         out_specs=vmem,
         compiler_params=pltpu.CompilerParams(vmem_limit_bytes=8 << 20),
         name="unit",
-    )(*parts)
+    )(src_all)
 
 
 def margin_kernel(kept0, kept1, got0, got1, row_ref, knn_own_ref, knn_got_ref, out_ref, ksrc):
@@ -273,7 +270,7 @@
     @pl.when(pl.program_id(0) == 0)
     def _():
         a, b, c, d = (row_ref[i : i + 1, :] for i in range(4))
-        mean = 0.25 * ((a + b) + (c + d))
+        mean = 0.125 * ((a + b) + (c + d))
         ksrc[...] = jnp.broadcast_to(mean, (128, mean.shape[1])).T
 
     rows_n = out_ref.shape[0]
@@ -287,13 +284,13 @@
         (got1, knn_got_ref, width, got_place + width),
     )
     for scores_ref, knn_ref, offset, place in sides:
-        knn_tgt = knn_ref[:, offset : offset + width]
+        knn_tgt = 0.125 * knn_ref[:, offset : offset + width]
         cols = pl.ds(pl.multiple_of(place, width), width)
-        for r in range(0, rows_n, 8):
-            here = pl.ds(pl.multiple_of(start + r, 8), 8)
-            x = scores_ref[r : r + 8, :]
-            ratio = x / (0.5 * (ksrc[here, 0:1] + knn_tgt))
-            out_ref[r : r + 8, cols] = jnp.where(x < -1.5, jnp.float32(0.0), ratio)
+        for r in range(0, rows_n, 16):
+            here = pl.ds(pl.multiple_of(start + r, 16), 16)
+            x = scores_ref[r : r + 16, :].astype(jnp.float32)
+            ratio = x / (ksrc[here, 0:1] + knn_tgt)
+            out_ref[r : r + 16, cols] = jnp.where(x < -1.5, jnp.float32(0.0), ratio)
 
 
 def margin(scores, row_list, knn_own, knn_got):
@@ -323,6 +320,16 @@
     return lax.all_to_all(spread, axes, 0, 0, tiled=True)
 
 
+def joined(arrays):
+    if len(arrays) == 1:
+        return arrays[0]
+    groups = [
+        merged_all([tuple(a[k : k + 4]) for a in arrays])
+        for k in range(0, arrays[0].shape[0], 4)
+    ]
+    return jnp.stack([p for four in groups for p in four])
+
+
 def up(array):
     return shifted(array, "z", 8, 1)
 
@@ -340,20 +347,23 @@
 
 
 PLACES = [(0, 0), (0, 1)] + [(dz, dy) for dz in (-1, 1, -2, 2, -3, 3, 4) for dy in (0, 1)]
-BY_Y = (3, 4)
-
-
-def gathered(own):
-    a, b = {0: own}, {0: across(own)}
-    for k in range(1, 5):
-        a[-k] = up(a[1 - k])
-        if k < 4:
-            a[k] = down(a[k - 1])
-            b[-k] = across(a[-k]) if k in BY_Y else up(b[1 - k])
-            b[k] = across(a[k]) if k in BY_Y else down(b[k - 1])
-    a[4] = a[-4]
-    b[4] = across(a[4]) if 4 in BY_Y else down(b[3])
-    return [(b if dy else a)[dz] for dz, dy in PLACES], b[0]
+
+
+def gathered(own, src_emb):
+    a = {0: own, -1: up(own), 1: down(own)}
+    a[2], a[-2] = down(a[1]), up(a[-1])
+    b = {0: across(own)}
+    src_all = from_everyone(src_emb, TGT, 8)
+    a[2], a[-2], b[0], src_all = lax.optimization_barrier(
+        (a[2], a[-2], b[0], src_all)
+    )
+    unit = unit_rows(src_all)
+    a[3], a[-3] = down(a[2]), up(a[-2])
+    a[4] = up(a[-3])
+    for k in range(1, 4):
+        b[k], b[-k] = down(b[k - 1]), up(b[1 - k])
+    b[4] = down(b[3])
+    return [(b if dy else a)[dz] for dz, dy in PLACES], unit
 
 
 def body(src_emb, tgt_emb, src_ids, tgt_ids):
@@ -366,8 +376,7 @@
     chip = jnp.concatenate(
         [jnp.where(first, mine, theirs), jnp.where(first, theirs, mine)]
     )
-    blocks, _ = gathered(chip)
-    unit = unit_rows(src_emb)
+    blocks, unit = gathered(chip, src_emb)
     units = (unit, over(unit))
     sid = jnp.concatenate([src_ids, over(src_ids)])[None, :]
     tid = lax.dynamic_slice_in_dim(tgt_ids, core * half, half, 0)[None, :]
@@ -380,26 +389,20 @@
     kept1, sent1, row1, row1_pair, col1 = scores_and_lists(
         1, blocks, units, sid, tid[:, quarter:], (row0, row0_pair)
     )
-    col_lists = from_everyone(jnp.concatenate([col0, col1], axis=1), ("z", "yh"), 16)
     got1 = over(sent1)
-
-    def joined(first, second):
-        pairs = (
-            merged(tuple(first[k : k + 4]), tuple(second[k : k + 4])) for k in (0, 4)
-        )
-        return jnp.stack([p for four in pairs for p in four])
-
-    lists = jnp.concatenate([row1, row1_pair])
-    lists = joined(lists, shifted(lists, "yl", 2, 1))
-    lists = joined(lists, shifted(lists, "x", 4, 2))
-    lists = joined(lists, shifted(lists, "x", 4, 1))
-    col_lists = col_lists.astype(jnp.float32)
-    a, b, c, d = merged_all([tuple(col_lists[k]) for k in range(16)])
-    knn_own = 0.25 * ((a + b) + (c + d))
-    swap = over(jnp.concatenate([lists[4:], knn_own.reshape(-1, lists.shape[1])]))
-    row_list = jnp.stack(merged(tuple(lists[:4]), tuple(swap[:4])))
-    knn_got = swap[4:].reshape(1, -1)
-    return margin((kept0, kept1, got0, got1), row_list, knn_own[None, :], knn_got)
+    cols = jnp.concatenate([col0, col1], axis=1)
+    rows = jnp.concatenate([row1, row1_pair])
+    rows = joined([rows, shifted(rows, "yl", 2, 1)])
+    cols = joined([cols, across(cols)])
+    spread = jnp.broadcast_to(cols[None], (8, *cols.shape))
+    far = lax.all_to_all(spread, "z", 0, 0, tiled=True)
+    rows = after(rows, spread)
+    rows = joined([rows] + [shifted(rows, "x", 4, k) for k in (1, 2, 3)])
+    row_list = joined([rows[:4], over(rows[4:])])
+    far = far.astype(jnp.float32)
+    a, b, c, d = merged_all([tuple(far[k]) for k in range(8)])
+    knn_own = ((a + b) + (c + d))[None, :]
+    return margin((kept0, kept1, got0, got1), row_list, knn_own, over(knn_own))
 
 
 def solution(mesh):

time: 122 us -> 114 us (0.934)
  starting transfers between devices: 59.9 us -> 55.9 us
  Pallas kernels: 21.5 us -> 18.8 us
    all_to_all x1, starting transfers between devices: 7.53 us -> 3.56 us  [from_everyone(): return lax.all_to_all(spread, axes, 0, 0, tiled=True)]
    all_to_all x0 -> x1, starting transfers between devices: none -> 3.37 us  [body(): far = lax.all_to_all(spread, 'z', 0, 0, tiled=True)]
    ppermute x28 -> x27, starting transfers between devices: 52.3 us -> 49 us  [shifted(): lax.ppermute(array, axis, [(i, (i + by) % size) for i in range(size)])]
    all_to_all x1, waiting for transfers between devices: 3.02 us -> 0.01 us  [from_everyone(): return lax.all_to_all(spread, axes, 0, 0, tiled=True)]
    ppermute x28 -> x27, waiting for transfers between devices: 28.3 us -> 31 us  [shifted(): lax.ppermute(array, axis, [(i, (i + by) % size) for i in range(size)])]
    pallas_call x1, Pallas kernels: 8.19 us -> 5.54 us  [margin(): pl.pallas_call(margin_kernel, grid=(rows_n // block,), out_shape=jax.Shap...]
    unnamed x10 -> x5, local copies, waits for them, and re-layouts: 2.51 us -> 1.23 us
  transfers between devices with their start and end apart: 29 -> 29, of which waited for: 15 -> 13; matrix products, arithmetic and copies ran while one was open for 5% -> 4% of each run, Pallas kernels for 0% -> 0%
where the time goes in v3:
time: 114 us
  starting transfers between devices  55.9 us (49%)
  waiting for transfers between devices  31 us (27%)
  Pallas kernels  18.8 us (16%)
  local copies, waits for them, and re-layouts  5.59 us (5%)
  other arithmetic  2.34 us (2%)
    ppermute x27, starting transfers between devices, shifted(): lax.ppermute(array, axis, [(i, (i + by) % size) for i in range(size)])  49 us
    ppermute x27, waiting for transfers between devices, shifted(): lax.ppermute(array, axis, [(i, (i + by) % size) for i in range(size)])  31 us
    pallas_call x2, Pallas kernels, scores_and_lists(): pl.pallas_call(functools.partial(score_kernel, len(blocks), side), out_sh...  12.9 us
    pallas_call x1, Pallas kernels, margin(): pl.pallas_call(margin_kernel, grid=(rows_n // block,), out_shape=jax.Shap...  5.54 us
    all_to_all x1, starting transfers between devices, from_everyone(): return lax.all_to_all(spread, axes, 0, 0, tiled=True)  3.56 us
    all_to_all x1, starting transfers between devices, body(): far = lax.all_to_all(spread, 'z', 0, 0, tiled=True)  3.37 us
  transfers between devices with their start and end apart: 29, of which 13 were waited for; matrix products, arithmetic and copies ran while one was open for 4% of the time, Pallas kernels for 0%

profile of v3, /device:TPU:1, one launch (start us, length us, event | category | flops | bytes accessed | tf_op | source)
XLA Modules:
  0.0 113.9 jit_solution(17249722529469888911)
XLA Ops:
  0.9 3.3 %collective-permute-start = (bf16[32,2048]{1,0:T(8,128)(2,1)S(1)}, bf16[32,2048]{1,0:T(8,128)(2,1)S(1)}, u32[]{:S(2)}, u32[]{:S(2)}) collective-permute-start(bf16[32,2048]{1,0:T(8,128)(2,1)S(1)} %dynamic-slice_bitcast_fusion), channel_id=1, source_target_pairs={{0,8},{8,0},{1,9},{9,1},{2,10},{10,2},{3,11},{11,3},{4,12},{12,4},... | collective-permute-start | bytes 393224 | tf_op jit(solution)/shard_map/ppermute | solution.py:315
  4.2 2.0 %broadcast_in_dim.8 = bf16[8,512,128]{2,1,0:T(8,128)(2,1)} broadcast(bf16[512,128]{1,0:T(8,128)(2,1)} %param.4), dimensions={1,2} | broadcast | bytes 1179648 | tf_op jit(solution)/shard_map/broadcast_in_dim | solution.py:319
  6.3 3.6 %all-to-all-start = ((bf16[8,512,128]{2,1,0:T(8,128)(2,1)}), bf16[8,512,128]{2,1,0:T(8,128)(2,1)S(1)}, u32[]{:S(2)}, u32[]{:S(2)}) async-start(bf16[8,512,128]{2,1,0:T(8,128)(2,1)} %broadcast_in_dim.8), calls=%async_computation | async-start | bytes 2097152 | tf_op jit(solution)/shard_map/all_to_all | solution.py:320
  10.8 1.4 %collective-permute-start.3 = (bf16[64,2048]{1,0:T(8,128)(2,1)S(1)}, bf16[64,2048]{1,0:T(8,128)(2,1)S(1)}, u32[]{:S(2)}, u32[]{:S(2)}) collective-permute-start(bf16[64,2048]{1,0:T(8,128)(2,1)S(1)} %pad_maximum_fusion.refs_0_), channel_id=1, source_target_pairs={{0,32},{32,64},{64,96},{96,128},{128,160},{160,192},{192,224},{224... | collective-permute-start | bytes 786440 | tf_op jit(solution)/shard_map/ppermute | solution.py:315
  12.3 4.0 %collective-permute-start.1 = (bf16[64,2048]{1,0:T(8,128)(2,1)S(1)}, bf16[64,2048]{1,0:T(8,128)(2,1)S(1)}, u32[]{:S(2)}, u32[]{:S(2)}) collective-permute-start(bf16[64,2048]{1,0:T(8,128)(2,1)S(1)} %pad_maximum_fusion.refs_0_), channel_id=1, source_target_pairs={{0,224},{32,0},{64,32},{96,64},{128,96},{160,128},{192,160},{224,1... | collective-permute-start | bytes 786440 | tf_op jit(solution)/shard_map/ppermute | solution.py:315
  16.3 2.6 %collective-permute-start.5 = (bf16[64,2048]{1,0:T(8,128)(2,1)S(1)}, bf16[64,2048]{1,0:T(8,128)(2,1)S(1)}, u32[]{:S(2)}, u32[]{:S(2)}) collective-permute-start(bf16[64,2048]{1,0:T(8,128)(2,1)S(1)} %pad_maximum_fusion.refs_0_), channel_id=1, source_target_pairs={{0,16},{16,0},{1,17},{17,1},{2,18},{18,2},{3,19},{19,3},{4,20},{20... | collective-permute-start | bytes 786440 | tf_op jit(solution)/shard_map/ppermute | solution.py:315
  18.9 3.8 %collective-permute-done.3.refs_2_ = bf16[64,2048]{1,0:T(8,128)(2,1)S(1)} collective-permute-done((bf16[64,2048]{1,0:T(8,128)(2,1)S(1)}, bf16[64,2048]{1,0:T(8,128)(2,1)S(1)}, u32[]{:S(2)}, u32[]{:S(2)}) %collective-permute-start.3) | collective-permute-done | bytes 262176 | tf_op jit(solution)/shard_map/ppermute | solution.py:315
  22.7 2.7 %collective-permute-start.2 = (bf16[64,2048]{1,0:T(8,128)(2,1)S(1)}, bf16[64,2048]{1,0:T(8,128)(2,1)S(1)}, u32[]{:S(2)}, u32[]{:S(2)}) collective-permute-start(bf16[64,2048]{1,0:T(8,128)(2,1)S(1)} %collective-permute-done.1.refs_4_), channel_id=1, source_target_pairs={{0,224},{32,0},{64,32},{96,64},{128,96},{160,128},{192,160},{224,1... | collective-permute-start | bytes 786440 | tf_op jit(solution)/shard_map/ppermute | solution.py:315
  25.3 6.2 %collective-permute-done.5.refs_1_ = bf16[64,2048]{1,0:T(8,128)(2,1)S(1)} collective-permute-done((bf16[64,2048]{1,0:T(8,128)(2,1)S(1)}, bf16[64,2048]{1,0:T(8,128)(2,1)S(1)}, u32[]{:S(2)}, u32[]{:S(2)}) %collective-permute-start.5) | collective-permute-done | bytes 262176 | tf_op jit(solution)/shard_map/ppermute | solution.py:315
  31.6 3.7 %collective-permute-start.7 = (bf16[64,2048]{1,0:T(8,128)(2,1)S(1)}, bf16[64,2048]{1,0:T(8,128)(2,1)S(1)}, u32[]{:S(2)}, u32[]{:S(2)}) collective-permute-start(bf16[64,2048]{1,0:T(8,128)(2,1)S(1)} %collective-permute-done.5.refs_1_), channel_id=1, source_target_pairs={{0,224},{32,0},{64,32},{96,64},{128,96},{160,128},{192,160},{224,1... | collective-permute-start | bytes 786440 | tf_op jit(solution)/shard_map/ppermute | solution.py:315
  35.7 1.6 %collective-permute-start.16 = (bf16[512,1024]{1,0:T(8,128)(2,1)S(1)}, bf16[512,1024]{1,0:T(8,128)(2,1)S(1)}, u32[]{:S(2)}, u32[]{:S(2)}) collective-permute-start(bf16[512,1024]{1,0:T(8,128)(2,1)S(1)} %unit.1.refs_16_), channel_id=1, source_target_pairs={{0,8},{8,0},{1,9},{9,1},{2,10},{10,2},{3,11},{11,3},{4,12},{12,4},... | collective-permute-start | bytes 3145736 | tf_op jit(solution)/shard_map/ppermute | solution.py:315
  37.3 2.3 %collective-permute-done.7.refs_5_ = bf16[64,2048]{1,0:T(8,128)(2,1)S(1)} collective-permute-done((bf16[64,2048]{1,0:T(8,128)(2,1)S(1)}, bf16[64,2048]{1,0:T(8,128)(2,1)S(1)}, u32[]{:S(2)}, u32[]{:S(2)}) %collective-permute-start.7) | collective-permute-done | bytes 262176 | tf_op jit(solution)/shard_map/ppermute | solution.py:315
  39.6 3.4 %collective-permute-start.9 = (bf16[64,2048]{1,0:T(8,128)(2,1)S(1)}, bf16[64,2048]{1,0:T(8,128)(2,1)S(1)}, u32[]{:S(2)}, u32[]{:S(2)}) collective-permute-start(bf16[64,2048]{1,0:T(8,128)(2,1)S(1)} %collective-permute-done.7.refs_5_), channel_id=1, source_target_pairs={{0,224},{32,0},{64,32},{96,64},{128,96},{160,128},{192,160},{224,1... | collective-permute-start | bytes 786440 | tf_op jit(solution)/shard_map/ppermute | solution.py:315
  43.0 3.4 %collective-permute-done.6.refs_3_ = bf16[64,2048]{1,0:T(8,128)(2,1)S(1)} collective-permute-done((bf16[64,2048]{1,0:T(8,128)(2,1)S(1)}, bf16[64,2048]{1,0:T(8,128)(2,1)S(1)}, u32[]{:S(2)}, u32[]{:S(2)}) %collective-permute-start.6) | collective-permute-done | bytes 262176 | tf_op jit(solution)/shard_map/ppermute | solution.py:315
  46.4 3.5 %collective-permute-start.13 = (bf16[64,2048]{1,0:T(8,128)(2,1)S(1)}, bf16[64,2048]{1,0:T(8,128)(2,1)S(1)}, u32[]{:S(2)}, u32[]{:S(2)}) collective-permute-start(bf16[64,2048]{1,0:T(8,128)(2,1)S(1)} %collective-permute-done.9.refs_9_), channel_id=1, source_target_pairs={{0,224},{32,0},{64,32},{96,64},{128,96},{160,128},{192,160},{224,1... | collective-permute-start | bytes 786440 | tf_op jit(solution)/shard_map/ppermute | solution.py:315
  49.9 3.4 %collective-permute-start.17 = (s32[512]{0:T(512)}, s32[512]{0:T(512)S(1)}, u32[]{:S(2)}, u32[]{:S(2)}) collective-permute-start(s32[512]{0:T(512)} %param.6), channel_id=1, source_target_pairs={{0,8},{8,0},{1,9},{9,1},{2,10},{10,2},{3,11},{11,3},{4,12},{12,4},... | collective-permute-start | bytes 6152 | tf_op jit(solution)/shard_map/ppermute | solution.py:315
  54.3 1.5 %collective-permute-start.14 = (bf16[64,2048]{1,0:T(8,128)(2,1)S(1)}, bf16[64,2048]{1,0:T(8,128)(2,1)S(1)}, u32[]{:S(2)}, u32[]{:S(2)}) collective-permute-start(bf16[64,2048]{1,0:T(8,128)(2,1)S(1)} %collective-permute-done.10.refs_10_), channel_id=1, source_target_pairs={{0,32},{32,64},{64,96},{96,128},{128,160},{160,192},{192,224},{224... | collective-permute-start | bytes 786440 | tf_op jit(solution)/shard_map/ppermute | solution.py:315
  55.8 2.7 %collective-permute-start.15 = (bf16[64,2048]{1,0:T(8,128)(2,1)S(1)}, bf16[64,2048]{1,0:T(8,128)(2,1)S(1)}, u32[]{:S(2)}, u32[]{:S(2)}) collective-permute-start(bf16[64,2048]{1,0:T(8,128)(2,1)S(1)} %collective-permute-done.13.refs_13_), channel_id=1, source_target_pairs={{0,224},{32,0},{64,32},{96,64},{128,96},{160,128},{192,160},{224,1... | collective-permute-start | bytes 786440 | tf_op jit(solution)/shard_map/ppermute | solution.py:315
  59.2 2.6 %collective-permute-done.12.refs_12_ = bf16[64,2048]{1,0:T(8,128)(2,1)S(1)} collective-permute-done((bf16[64,2048]{1,0:T(8,128)(2,1)S(1)}, bf16[64,2048]{1,0:T(8,128)(2,1)S(1)}, u32[]{:S(2)}, u32[]{:S(2)}) %collective-permute-start.12) | collective-permute-done | bytes 262176 | tf_op jit(solution)/shard_map/ppermute | solution.py:315
  62.2 5.6 %collective-permute-done.11.refs_11_ = bf16[64,2048]{1,0:T(8,128)(2,1)S(1)} collective-permute-done((bf16[64,2048]{1,0:T(8,128)(2,1)S(1)}, bf16[64,2048]{1,0:T(8,128)(2,1)S(1)}, u32[]{:S(2)}, u32[]{:S(2)}) %collective-permute-start.11) | collective-permute-done | bytes 262176 | tf_op jit(solution)/shard_map/ppermute | solution.py:315
  67.9 6.4 %scores0.1 = (bf16[512,1024]{1,0:T(8,128)(2,1)}, bf16[512,1024]{1,0:T(8,128)(2,1)}, f32[4,512]{1,0:T(4,128)S(1)}, f32[4,512]{1,0:T(4,128)S(1)}, bf16[4,1024]{1,0:T(4,128)(2,1)S(1)}) custom-call(bf16[64,2048]{1,0:T(8,128)(2,1)S(1)} %pad_maximum_fusion.refs_0_, bf16[64,2048]{1,0:T(8,128)(2,1)S(1)} %collective-permute-done.5.refs_1_, ...), custom_call_target="tpu_custom_call" | custom-call | flops 2147483648 | bytes 9437184 | tf_op jit(solution)/shard_map/scores0/pallas_call | solution.py:207
  74.3 6.5 %scores1.1 = (bf16[512,1024]{1,0:T(8,128)(2,1)}, bf16[512,1024]{1,0:T(8,128)(2,1)}, f32[4,512]{1,0:T(4,128)S(1)}, f32[4,512]{1,0:T(4,128)S(1)}, bf16[4,1024]{1,0:T(4,128)(2,1)S(1)}) custom-call(bf16[64,2048]{1,0:T(8,128)(2,1)S(1)} %pad_maximum_fusion.refs_0_, bf16[64,2048]{1,0:T(8,128)(2,1)S(1)} %collective-permute-done.5.refs_1_, ...), custom_call_target="tpu_custom_call" | custom-call | flops 2147483648 | bytes 9437184 | tf_op jit(solution)/shard_map/scores1/pallas_call | solution.py:207
  80.8 3.5 %collective-permute-start.21 = (bf16[4,2048]{1,0:T(4,128)(2,1)S(1)}, bf16[4,2048]{1,0:T(4,128)(2,1)S(1)}, u32[]{:S(2)}, u32[]{:S(2)}) collective-permute-start(bf16[4,2048]{1,0:T(4,128)(2,1)S(1)} %constant_dynamic-update-slice_fusion), channel_id=1, source_target_pairs={{0,16},{16,0},{1,17},{17,1},{2,18},{18,2},{3,19},{19,3},{4,20},{20... | collective-permute-start | bytes 49160 | tf_op jit(solution)/shard_map/ppermute | solution.py:315
  84.3 1.3 %collective-permute-start.20 = (f32[8,512]{1,0:T(8,128)S(1)}, f32[8,512]{1,0:T(8,128)S(1)}, u32[]{:S(2)}, u32[]{:S(2)}) collective-permute-start(f32[8,512]{1,0:T(8,128)S(1)} %pad_maximum_fusion.1), channel_id=1, source_target_pairs={{0,4},{4,0},{1,5},{5,1},{2,6},{6,2},{3,7},{7,3},{8,12},{12,8},{9,1... | collective-permute-start | bytes 49160 | tf_op jit(solution)/shard_map/ppermute | solution.py:315
  85.7 1.7 %collective-permute-done.20 = f32[8,512]{1,0:T(8,128)S(1)} collective-permute-done((f32[8,512]{1,0:T(8,128)S(1)}, f32[8,512]{1,0:T(8,128)S(1)}, u32[]{:S(2)}, u32[]{:S(2)}) %collective-permute-start.20) | collective-permute-done | bytes 16416 | tf_op jit(solution)/shard_map/ppermute | solution.py:315
  89.4 3.1 %collective-permute-start.19 = (bf16[512,1024]{1,0:T(8,128)(2,1)}, bf16[512,1024]{1,0:T(8,128)(2,1)S(1)}, u32[]{:S(2)}, u32[]{:S(2)}) collective-permute-start(bf16[512,1024]{1,0:T(8,128)(2,1)} %get-tuple-element.29), channel_id=1, source_target_pairs={{0,8},{8,0},{1,9},{9,1},{2,10},{10,2},{3,11},{11,3},{4,12},{12,4},... | collective-permute-start | bytes 3145736 | tf_op jit(solution)/shard_map/ppermute | solution.py:315
  92.6 3.4 %all-to-all-start.1 = ((bf16[8,4,2048]{2,1,0:T(4,128)(2,1)}), bf16[8,4,2048]{2,1,0:T(4,128)(2,1)S(1)}, u32[]{:S(2)}, u32[]{:S(2)}) async-start(bf16[8,4,2048]{2,1,0:T(4,128)(2,1)} %broadcast_in_dim.22), calls=%async_computation.1 | async-start | bytes 262144 | tf_op jit(solution)/shard_map/all_to_all | solution.py:398
  95.9 1.6 %collective-permute-start.24 = (f32[8,512]{1,0:T(8,128)S(1)}, f32[8,512]{1,0:T(8,128)S(1)}, u32[]{:S(2)}, u32[]{:S(2)}) collective-permute-start(f32[8,512]{1,0:T(8,128)S(1)} %stack.8), channel_id=1, source_target_pairs={{0,3},{1,0},{2,1},{3,2},{4,7},{5,4},{6,5},{7,6},{8,11},{9,8},{10,9... | collective-permute-start | bytes 49160 | tf_op jit(solution)/shard_map/ppermute | solution.py:315
  98.7 2.9 %collective-permute-done.23 = f32[8,512]{1,0:T(8,128)S(1)} collective-permute-done((f32[8,512]{1,0:T(8,128)S(1)}, f32[8,512]{1,0:T(8,128)S(1)}, u32[]{:S(2)}, u32[]{:S(2)}) %collective-permute-start.23) | collective-permute-done | bytes 16416 | tf_op jit(solution)/shard_map/ppermute | solution.py:315
  101.7 2.2 %collective-permute-start.25 = (f32[4,512]{1,0:T(4,128)S(1)}, f32[4,512]{1,0:T(4,128)S(1)}, u32[]{:S(2)}, u32[]{:S(2)}) collective-permute-start(f32[4,512]{1,0:T(4,128)S(1)} %pad_maximum_fusion.3), channel_id=1, source_target_pairs={{0,8},{8,0},{1,9},{9,1},{2,10},{10,2},{3,11},{11,3},{4,12},{12,4},... | collective-permute-start | bytes 24584 | tf_op jit(solution)/shard_map/ppermute | solution.py:315
  105.1 1.2 %collective-permute-start.26 = (f32[1,2048]{1,0:T(1,128)S(1)}, f32[1,2048]{1,0:T(1,128)S(1)}, u32[]{:S(2)}, u32[]{:S(2)}) collective-permute-start(f32[1,2048]{1,0:T(1,128)S(1)} %add_bitcast_fusion.knn_own_ref), channel_id=1, source_target_pairs={{0,8},{8,0},{1,9},{9,1},{2,10},{10,2},{3,11},{11,3},{4,12},{12,4},... | collective-permute-start | bytes 24584 | tf_op jit(solution)/shard_map/ppermute | solution.py:315
  108.4 5.5 %margin.1 = f32[512,4096]{1,0:T(8,128)} custom-call(bf16[512,1024]{1,0:T(8,128)(2,1)S(1)} %copy-done, bf16[512,1024]{1,0:T(8,128)(2,1)S(1)} %copy-done.1, bf16[512,1024]{1,0:T(8,128)(2,1)S(1)} %collective-permute-done.18.got0, bf16[512,1024]{1,0:T(8,128)(2,1)S(1)} %collective-permute-done.19.got1, f32[4,512]{1,0:T(4,128)S(1)} %pad_maximum_fusion.4.row_ref, ...), custom_call_target="tpu_custom_call" | custom-call | tf_op jit(solution)/shard_map/margin/pallas_call | solution.py:300
  (63 shorter events, 11.2 us)
Async XLA Ops:
  0.9 8.9 %collective-permute-start = (bf16[32,2048]{1,0:T(8,128)(2,1)S(1)}, bf16[32,2048]{1,0:T(8,128)(2,1)S(1)}, u32[]{:S(2)}, u32[]{:S(2)}) collective-permute-start(bf16[32,2048]{1,0:T(8,128)(2,1)S(1)} %dynamic-slice_bitcast_fusion), channel_id=1, source_target_pairs={{0,8},{8,0},{1,9},{9,1},{2,10},{10,2},{3,11},{11,3},{4,12},{12,4},... | collective-permute-start | bytes 393224 | tf_op jit(solution)/shard_map/ppermute | solution.py:315
  6.3 25.3 %all-to-all-start = ((bf16[8,512,128]{2,1,0:T(8,128)(2,1)}), bf16[8,512,128]{2,1,0:T(8,128)(2,1)S(1)}, u32[]{:S(2)}, u32[]{:S(2)}) async-start(bf16[8,512,128]{2,1,0:T(8,128)(2,1)} %broadcast_in_dim.8), calls=%async_computation | async-start | bytes 2097152 | tf_op jit(solution)/shard_map/all_to_all | solution.py:320
  10.8 11.8 %collective-permute-start.3 = (bf16[64,2048]{1,0:T(8,128)(2,1)S(1)}, bf16[64,2048]{1,0:T(8,128)(2,1)S(1)}, u32[]{:S(2)}, u32[]{:S(2)}) collective-permute-start(bf16[64,2048]{1,0:T(8,128)(2,1)S(1)} %pad_maximum_fusion.refs_0_), channel_id=1, source_target_pairs={{0,32},{32,64},{64,96},{96,128},{128,160},{160,192},{192,224},{224... | collective-permute-start | bytes 786440 | tf_op jit(solution)/shard_map/ppermute | solution.py:315
  12.3 10.4 %collective-permute-start.1 = (bf16[64,2048]{1,0:T(8,128)(2,1)S(1)}, bf16[64,2048]{1,0:T(8,128)(2,1)S(1)}, u32[]{:S(2)}, u32[]{:S(2)}) collective-permute-start(bf16[64,2048]{1,0:T(8,128)(2,1)S(1)} %pad_maximum_fusion.refs_0_), channel_id=1, source_target_pairs={{0,224},{32,0},{64,32},{96,64},{128,96},{160,128},{192,160},{224,1... | collective-permute-start | bytes 786440 | tf_op jit(solution)/shard_map/ppermute | solution.py:315
  16.3 15.3 %collective-permute-start.5 = (bf16[64,2048]{1,0:T(8,128)(2,1)S(1)}, bf16[64,2048]{1,0:T(8,128)(2,1)S(1)}, u32[]{:S(2)}, u32[]{:S(2)}) collective-permute-start(bf16[64,2048]{1,0:T(8,128)(2,1)S(1)} %pad_maximum_fusion.refs_0_), channel_id=1, source_target_pairs={{0,16},{16,0},{1,17},{17,1},{2,18},{18,2},{3,19},{19,3},{4,20},{20... | collective-permute-start | bytes 786440 | tf_op jit(solution)/shard_map/ppermute | solution.py:315
  22.7 8.9 %collective-permute-start.4 = (bf16[64,2048]{1,0:T(8,128)(2,1)S(1)}, bf16[64,2048]{1,0:T(8,128)(2,1)S(1)}, u32[]{:S(2)}, u32[]{:S(2)}) collective-permute-start(bf16[64,2048]{1,0:T(8,128)(2,1)S(1)} %collective-permute-done.3.refs_2_), channel_id=1, source_target_pairs={{0,32},{32,64},{64,96},{96,128},{128,160},{160,192},{192,224},{224... | collective-permute-start | bytes 786440 | tf_op jit(solution)/shard_map/ppermute | solution.py:315
  22.7 8.9 %collective-permute-start.2 = (bf16[64,2048]{1,0:T(8,128)(2,1)S(1)}, bf16[64,2048]{1,0:T(8,128)(2,1)S(1)}, u32[]{:S(2)}, u32[]{:S(2)}) collective-permute-start(bf16[64,2048]{1,0:T(8,128)(2,1)S(1)} %collective-permute-done.1.refs_4_), channel_id=1, source_target_pairs={{0,224},{32,0},{64,32},{96,64},{128,96},{160,128},{192,160},{224,1... | collective-permute-start | bytes 786440 | tf_op jit(solution)/shard_map/ppermute | solution.py:315
  31.6 8.0 %collective-permute-start.7 = (bf16[64,2048]{1,0:T(8,128)(2,1)S(1)}, bf16[64,2048]{1,0:T(8,128)(2,1)S(1)}, u32[]{:S(2)}, u32[]{:S(2)}) collective-permute-start(bf16[64,2048]{1,0:T(8,128)(2,1)S(1)} %collective-permute-done.5.refs_1_), channel_id=1, source_target_pairs={{0,224},{32,0},{64,32},{96,64},{128,96},{160,128},{192,160},{224,1... | collective-permute-start | bytes 786440 | tf_op jit(solution)/shard_map/ppermute | solution.py:315
  35.7 32.2 %collective-permute-start.16 = (bf16[512,1024]{1,0:T(8,128)(2,1)S(1)}, bf16[512,1024]{1,0:T(8,128)(2,1)S(1)}, u32[]{:S(2)}, u32[]{:S(2)}) collective-permute-start(bf16[512,1024]{1,0:T(8,128)(2,1)S(1)} %unit.1.refs_16_), channel_id=1, source_target_pairs={{0,8},{8,0},{1,9},{9,1},{2,10},{10,2},{3,11},{11,3},{4,12},{12,4},... | collective-permute-start | bytes 3145736 | tf_op jit(solution)/shard_map/ppermute | solution.py:315
  37.3 9.1 %collective-permute-start.6 = (bf16[64,2048]{1,0:T(8,128)(2,1)S(1)}, bf16[64,2048]{1,0:T(8,128)(2,1)S(1)}, u32[]{:S(2)}, u32[]{:S(2)}) collective-permute-start(bf16[64,2048]{1,0:T(8,128)(2,1)S(1)} %collective-permute-done.5.refs_1_), channel_id=1, source_target_pairs={{0,32},{32,64},{64,96},{96,128},{128,160},{160,192},{192,224},{224... | collective-permute-start | bytes 786440 | tf_op jit(solution)/shard_map/ppermute | solution.py:315
  39.6 6.8 %collective-permute-start.9 = (bf16[64,2048]{1,0:T(8,128)(2,1)S(1)}, bf16[64,2048]{1,0:T(8,128)(2,1)S(1)}, u32[]{:S(2)}, u32[]{:S(2)}) collective-permute-start(bf16[64,2048]{1,0:T(8,128)(2,1)S(1)} %collective-permute-done.7.refs_5_), channel_id=1, source_target_pairs={{0,224},{32,0},{64,32},{96,64},{128,96},{160,128},{192,160},{224,1... | collective-permute-start | bytes 786440 | tf_op jit(solution)/shard_map/ppermute | solution.py:315
  43.0 11.2 %collective-permute-start.10 = (bf16[64,2048]{1,0:T(8,128)(2,1)S(1)}, bf16[64,2048]{1,0:T(8,128)(2,1)S(1)}, u32[]{:S(2)}, u32[]{:S(2)}) collective-permute-start(bf16[64,2048]{1,0:T(8,128)(2,1)S(1)} %collective-permute-done.4.refs_6_), channel_id=1, source_target_pairs={{0,32},{32,64},{64,96},{96,128},{128,160},{160,192},{192,224},{224... | collective-permute-start | bytes 786440 | tf_op jit(solution)/shard_map/ppermute | solution.py:315
  46.4 9.5 %collective-permute-start.8 = (bf16[64,2048]{1,0:T(8,128)(2,1)S(1)}, bf16[64,2048]{1,0:T(8,128)(2,1)S(1)}, u32[]{:S(2)}, u32[]{:S(2)}) collective-permute-start(bf16[64,2048]{1,0:T(8,128)(2,1)S(1)} %collective-permute-done.6.refs_3_), channel_id=1, source_target_pairs={{0,32},{32,64},{64,96},{96,128},{128,160},{160,192},{192,224},{224... | collective-permute-start | bytes 786440 | tf_op jit(solution)/shard_map/ppermute | solution.py:315
  46.4 9.5 %collective-permute-start.13 = (bf16[64,2048]{1,0:T(8,128)(2,1)S(1)}, bf16[64,2048]{1,0:T(8,128)(2,1)S(1)}, u32[]{:S(2)}, u32[]{:S(2)}) collective-permute-start(bf16[64,2048]{1,0:T(8,128)(2,1)S(1)} %collective-permute-done.9.refs_9_), channel_id=1, source_target_pairs={{0,224},{32,0},{64,32},{96,64},{128,96},{160,128},{192,160},{224,1... | collective-permute-start | bytes 786440 | tf_op jit(solution)/shard_map/ppermute | solution.py:315
  49.9 4.4 %collective-permute-start.17 = (s32[512]{0:T(512)}, s32[512]{0:T(512)S(1)}, u32[]{:S(2)}, u32[]{:S(2)}) collective-permute-start(s32[512]{0:T(512)} %param.6), channel_id=1, source_target_pairs={{0,8},{8,0},{1,9},{9,1},{2,10},{10,2},{3,11},{11,3},{4,12},{12,4},... | collective-permute-start | bytes 6152 | tf_op jit(solution)/shard_map/ppermute | solution.py:315
  54.3 7.6 %collective-permute-start.12 = (bf16[64,2048]{1,0:T(8,128)(2,1)S(1)}, bf16[64,2048]{1,0:T(8,128)(2,1)S(1)}, u32[]{:S(2)}, u32[]{:S(2)}) collective-permute-start(bf16[64,2048]{1,0:T(8,128)(2,1)S(1)} %collective-permute-done.2.refs_8_), channel_id=1, source_target_pairs={{0,224},{32,0},{64,32},{96,64},{128,96},{160,128},{192,160},{224,1... | collective-permute-start | bytes 786440 | tf_op jit(solution)/shard_map/ppermute | solution.py:315
  54.3 8.0 %collective-permute-start.14 = (bf16[64,2048]{1,0:T(8,128)(2,1)S(1)}, bf16[64,2048]{1,0:T(8,128)(2,1)S(1)}, u32[]{:S(2)}, u32[]{:S(2)}) collective-permute-start(bf16[64,2048]{1,0:T(8,128)(2,1)S(1)} %collective-permute-done.10.refs_10_), channel_id=1, source_target_pairs={{0,32},{32,64},{64,96},{96,128},{128,160},{160,192},{192,224},{224... | collective-permute-start | bytes 786440 | tf_op jit(solution)/shard_map/ppermute | solution.py:315
  55.8 12.0 %collective-permute-start.11 = (bf16[64,2048]{1,0:T(8,128)(2,1)S(1)}, bf16[64,2048]{1,0:T(8,128)(2,1)S(1)}, u32[]{:S(2)}, u32[]{:S(2)}) collective-permute-start(bf16[64,2048]{1,0:T(8,128)(2,1)S(1)} %collective-permute-done.8.refs_7_), channel_id=1, source_target_pairs={{0,32},{32,64},{64,96},{96,128},{128,160},{160,192},{192,224},{224... | collective-permute-start | bytes 786440 | tf_op jit(solution)/shard_map/ppermute | solution.py:315
  55.8 12.0 %collective-permute-start.15 = (bf16[64,2048]{1,0:T(8,128)(2,1)S(1)}, bf16[64,2048]{1,0:T(8,128)(2,1)S(1)}, u32[]{:S(2)}, u32[]{:S(2)}) collective-permute-start(bf16[64,2048]{1,0:T(8,128)(2,1)S(1)} %collective-permute-done.13.refs_13_), channel_id=1, source_target_pairs={{0,224},{32,0},{64,32},{96,64},{128,96},{160,128},{192,160},{224,1... | collective-permute-start | bytes 786440 | tf_op jit(solution)/shard_map/ppermute | solution.py:315
  74.3 32.9 %copy-start = (bf16[512,1024]{1,0:T(8,128)(2,1)S(1)}, bf16[512,1024]{1,0:T(8,128)(2,1)}, u32[]{:S(2)}) copy-start(bf16[512,1024]{1,0:T(8,128)(2,1)} %get-tuple-element.24.kept0) | copy-start | bytes 3145732
  80.8 4.8 %collective-permute-start.21 = (bf16[4,2048]{1,0:T(4,128)(2,1)S(1)}, bf16[4,2048]{1,0:T(4,128)(2,1)S(1)}, u32[]{:S(2)}, u32[]{:S(2)}) collective-permute-start(bf16[4,2048]{1,0:T(4,128)(2,1)S(1)} %constant_dynamic-update-slice_fusion), channel_id=1, source_target_pairs={{0,16},{16,0},{1,17},{17,1},{2,18},{18,2},{3,19},{19,3},{4,20},{20... | collective-permute-start | bytes 49160 | tf_op jit(solution)/shard_map/ppermute | solution.py:315
  84.3 3.2 %collective-permute-start.20 = (f32[8,512]{1,0:T(8,128)S(1)}, f32[8,512]{1,0:T(8,128)S(1)}, u32[]{:S(2)}, u32[]{:S(2)}) collective-permute-start(f32[8,512]{1,0:T(8,128)S(1)} %pad_maximum_fusion.1), channel_id=1, source_target_pairs={{0,4},{4,0},{1,5},{5,1},{2,6},{6,2},{3,7},{7,3},{8,12},{12,8},{9,1... | collective-permute-start | bytes 49160 | tf_op jit(solution)/shard_map/ppermute | solution.py:315
  88.2 10.4 %collective-permute-start.22 = (f32[8,512]{1,0:T(8,128)S(1)}, f32[8,512]{1,0:T(8,128)S(1)}, u32[]{:S(2)}, u32[]{:S(2)}) collective-permute-start(f32[8,512]{1,0:T(8,128)S(1)} %stack.8), channel_id=1, source_target_pairs={{0,1},{1,2},{2,3},{3,0},{4,5},{5,6},{6,7},{7,4},{8,9},{9,10},{10,1... | collective-permute-start | bytes 49160 | tf_op jit(solution)/shard_map/ppermute | solution.py:315
  89.4 17.7 %collective-permute-start.19 = (bf16[512,1024]{1,0:T(8,128)(2,1)}, bf16[512,1024]{1,0:T(8,128)(2,1)S(1)}, u32[]{:S(2)}, u32[]{:S(2)}) collective-permute-start(bf16[512,1024]{1,0:T(8,128)(2,1)} %get-tuple-element.29), channel_id=1, source_target_pairs={{0,8},{8,0},{1,9},{9,1},{2,10},{10,2},{3,11},{11,3},{4,12},{12,4},... | collective-permute-start | bytes 3145736 | tf_op jit(solution)/shard_map/ppermute | solution.py:315
  92.6 14.6 %collective-permute-start.18 = (bf16[512,1024]{1,0:T(8,128)(2,1)}, bf16[512,1024]{1,0:T(8,128)(2,1)S(1)}, u32[]{:S(2)}, u32[]{:S(2)}) collective-permute-start(bf16[512,1024]{1,0:T(8,128)(2,1)} %get-tuple-element.28), channel_id=1, source_target_pairs={{0,8},{8,0},{1,9},{9,1},{2,10},{10,2},{3,11},{11,3},{4,12},{12,4},... | collective-permute-start | bytes 3145736 | tf_op jit(solution)/shard_map/ppermute | solution.py:315
  92.6 12.2 %all-to-all-start.1 = ((bf16[8,4,2048]{2,1,0:T(4,128)(2,1)}), bf16[8,4,2048]{2,1,0:T(4,128)(2,1)S(1)}, u32[]{:S(2)}, u32[]{:S(2)}) async-start(bf16[8,4,2048]{2,1,0:T(4,128)(2,1)} %broadcast_in_dim.22), calls=%async_computation.1 | async-start | bytes 262144 | tf_op jit(solution)/shard_map/all_to_all | solution.py:398
  95.9 2.7 %collective-permute-start.24 = (f32[8,512]{1,0:T(8,128)S(1)}, f32[8,512]{1,0:T(8,128)S(1)}, u32[]{:S(2)}, u32[]{:S(2)}) collective-permute-start(f32[8,512]{1,0:T(8,128)S(1)} %stack.8), channel_id=1, source_target_pairs={{0,3},{1,0},{2,1},{3,2},{4,7},{5,4},{6,5},{7,6},{8,11},{9,8},{10,9... | collective-permute-start | bytes 49160 | tf_op jit(solution)/shard_map/ppermute | solution.py:315
  97.5 4.1 %collective-permute-start.23 = (f32[8,512]{1,0:T(8,128)S(1)}, f32[8,512]{1,0:T(8,128)S(1)}, u32[]{:S(2)}, u32[]{:S(2)}) collective-permute-start(f32[8,512]{1,0:T(8,128)S(1)} %stack.8), channel_id=1, source_target_pairs={{0,2},{1,3},{2,0},{3,1},{4,6},{5,7},{6,4},{7,5},{8,10},{9,11},{10,... | collective-permute-start | bytes 49160 | tf_op jit(solution)/shard_map/ppermute | solution.py:315
  101.7 3.0 %collective-permute-start.25 = (f32[4,512]{1,0:T(4,128)S(1)}, f32[4,512]{1,0:T(4,128)S(1)}, u32[]{:S(2)}, u32[]{:S(2)}) collective-permute-start(f32[4,512]{1,0:T(4,128)S(1)} %pad_maximum_fusion.3), channel_id=1, source_target_pairs={{0,8},{8,0},{1,9},{9,1},{2,10},{10,2},{3,11},{11,3},{4,12},{12,4},... | collective-permute-start | bytes 24584 | tf_op jit(solution)/shard_map/ppermute | solution.py:315
  105.1 2.1 %collective-permute-start.26 = (f32[1,2048]{1,0:T(1,128)S(1)}, f32[1,2048]{1,0:T(1,128)S(1)}, u32[]{:S(2)}, u32[]{:S(2)}) collective-permute-start(f32[1,2048]{1,0:T(1,128)S(1)} %add_bitcast_fusion.knn_own_ref), channel_id=1, source_target_pairs={{0,8},{8,0},{1,9},{9,1},{2,10},{10,2},{3,11},{11,3},{4,12},{12,4},... | collective-permute-start | bytes 24584 | tf_op jit(solution)/shard_map/ppermute | solution.py:315
  107.2 1.2 %copy-start.1 = (bf16[512,1024]{1,0:T(8,128)(2,1)S(1)}, bf16[512,1024]{1,0:T(8,128)(2,1)}, u32[]{:S(2)}) copy-start(bf16[512,1024]{1,0:T(8,128)(2,1)} %get-tuple-element.27.kept1) | copy-start | bytes 3145732

commit v4 on v3

--- a/solution.py
+++ b/solution.py
@@ -55,13 +55,11 @@
     return lists
 
 
-def score_kernel(n_blocks, side, *refs):
+def score_kernel(n_blocks, *refs):
     blocks = refs[:n_blocks]
     unit_refs = refs[n_blocks : n_blocks + 2]
     sid_ref, tid_ref = refs[n_blocks + 2 : n_blocks + 4]
     refs = refs[n_blocks + 4 :]
-    if side:
-        row_before, refs = refs[:2], refs[2:]
     score_refs, row_refs, col_ref = refs[:2], refs[2:4], refs[4]
     tall, unit, even, odd, rows, sids, stage, tsem, usem, osem = refs[5:]
     feats, width = tall.shape
@@ -76,9 +74,8 @@
         dz, dy = PLACES[n]
         owner = lax.rem(z + (8 + dz), 8) * 2 + lax.rem(yh + dy, 2)
         where = pl.ds(pl.multiple_of(owner * 64, 64), 64)
-        offset = side * width if blocks[n].shape[1] > width else 0
         return pltpu.make_async_copy(
-            blocks[n].at[:, pl.ds(offset + t * tile, tile)],
+            blocks[n].at[:, pl.ds(t * tile, tile)],
             tall.at[where, pl.ds(t * tile, tile)],
             tsem.at[t, n],
         )
@@ -187,25 +184,22 @@
         ]
         final = tuple(p[0:1, :] for p in over_sublanes(merged_all(lists)))
         here = slice(r % half, r % half + 128)
-        if side:
-            before = row_before[r // half]
-            final = merged(final, tuple(before[i : i + 1, here] for i in range(4)))
         for i in range(4):
             row_refs[r // half][i : i + 1, here] = final[i]
     for k in range(len(sequence)):
         out_copy(k).wait()
 
 
-def scores_and_lists(side, blocks, units, sid, tid, row_before):
+def scores_and_lists(blocks, units, sid, tid):
     tile, chunk = 512, 256
     feats = 1024
     width = tid.shape[1]
     half = units[0].shape[0]
     vmem = pl.BlockSpec(memory_space=pltpu.VMEM)
     hbm = pl.BlockSpec(memory_space=pltpu.HBM)
-    rest = [sid, tid, *row_before]
+    rest = [sid, tid]
     return pl.pallas_call(
-        functools.partial(score_kernel, len(blocks), side),
+        functools.partial(score_kernel, len(blocks)),
         out_shape=(
             pltpu.HBM((half, width), jnp.bfloat16),
             pltpu.HBM((half, width), jnp.bfloat16),
@@ -227,24 +221,30 @@
             pltpu.SemaphoreType.DMA((2,)),
             pltpu.SemaphoreType.DMA((width // tile * (2 * half // chunk),)),
         ],
-        compiler_params=pltpu.CompilerParams(vmem_limit_bytes=20 << 20),
+        compiler_params=pltpu.CompilerParams(vmem_limit_bytes=24 << 20),
         cost_estimate=pl.CostEstimate(
-            flops=4 * half * width * feats, bytes_accessed=9 << 20, transcendentals=0
+            flops=4 * half * width * feats, bytes_accessed=12 << 20, transcendentals=0
         ),
-        name=f"scores{side}",
+        name="scores",
     )(*blocks, *units, *rest)
 
 
 def unit_kernel(src_ref, out_ref):
     rows_n = out_ref.shape[0]
+    yl = lax.axis_index("yl")
     for r in range(0, rows_n, 64):
-        pieces = [src_ref[j, r : r + 64, :].astype(jnp.float32) for j in range(8)]
-        total = sum(x * x for x in pieces)
+        here = slice(r, r + 64)
+        pieces = [
+            (x, k, src_ref[x, k, here, :].astype(jnp.float32))
+            for x in range(4)
+            for k in range(2)
+        ]
+        total = sum(p * p for _, _, p in pieces)
         scale = jnp.sqrt(jnp.sum(total, axis=1, keepdims=True) + EPS)
-        for j in range(8):
-            out_ref[r : r + 64, 128 * j : 128 * j + 128] = (pieces[j] / scale).astype(
-                jnp.bfloat16
-            )
+        for x, k, p in pieces:
+            owner = lax.rem(yl + k, 2) * 4 + x
+            cols = pl.ds(pl.multiple_of(owner * 128, 128), 128)
+            out_ref[here, cols] = (p / scale).astype(jnp.bfloat16)
 
 
 def after(array, others):
@@ -255,7 +255,7 @@
     vmem = pl.BlockSpec(memory_space=pltpu.VMEM)
     return pl.pallas_call(
         unit_kernel,
-        out_shape=jax.ShapeDtypeStruct((src_all.shape[1], 1024), jnp.bfloat16),
+        out_shape=jax.ShapeDtypeStruct((src_all.shape[2], 1024), jnp.bfloat16),
         in_specs=[vmem],
         out_specs=vmem,
         compiler_params=pltpu.CompilerParams(vmem_limit_bytes=8 << 20),
@@ -263,8 +263,8 @@
     )(src_all)
 
 
-def margin_kernel(kept0, kept1, got0, got1, row_ref, knn_own_ref, knn_got_ref, out_ref, ksrc):
-    width = kept0.shape[1]
+def margin_kernel(kept_ref, got_ref, row_ref, knn_own_ref, knn_got_ref, out_ref, ksrc):
+    width = kept_ref.shape[1]
     core = lax.axis_index("core")
 
     @pl.when(pl.program_id(0) == 0)
@@ -275,16 +275,12 @@
 
     rows_n = out_ref.shape[0]
     start = pl.multiple_of(pl.program_id(0) * rows_n, rows_n)
-    own_place = core * (2 * width)
-    got_place = (1 - core) * (2 * width)
     sides = (
-        (kept0, knn_own_ref, 0, own_place),
-        (kept1, knn_own_ref, width, own_place + width),
-        (got0, knn_got_ref, 0, got_place),
-        (got1, knn_got_ref, width, got_place + width),
+        (kept_ref, knn_own_ref, core * width),
+        (got_ref, knn_got_ref, (1 - core) * width),
     )
-    for scores_ref, knn_ref, offset, place in sides:
-        knn_tgt = 0.125 * knn_ref[:, offset : offset + width]
+    for scores_ref, knn_ref, place in sides:
+        knn_tgt = 0.125 * knn_ref[...]
         cols = pl.ds(pl.multiple_of(place, width), width)
         for r in range(0, rows_n, 16):
             here = pl.ds(pl.multiple_of(start + r, 16), 16)
@@ -293,22 +289,22 @@
             out_ref[r : r + 16, cols] = jnp.where(x < -1.5, jnp.float32(0.0), ratio)
 
 
-def margin(scores, row_list, knn_own, knn_got):
-    rows_n, width = scores[0].shape
+def margin(kept, got, row_list, knn_own, knn_got):
+    rows_n, width = kept.shape
     block = 64
     vmem = pl.BlockSpec(memory_space=pltpu.VMEM)
     return pl.pallas_call(
         margin_kernel,
         grid=(rows_n // block,),
-        out_shape=jax.ShapeDtypeStruct((rows_n, 4 * width), jnp.float32),
-        in_specs=[pl.BlockSpec((block, width), lambda i: (i, 0))] * 4 + [vmem] * 3,
-        out_specs=pl.BlockSpec((block, 4 * width), lambda i: (i, 0)),
+        out_shape=jax.ShapeDtypeStruct((rows_n, 2 * width), jnp.float32),
+        in_specs=[pl.BlockSpec((block, width), lambda i: (i, 0))] * 2 + [vmem] * 3,
+        out_specs=pl.BlockSpec((block, 2 * width), lambda i: (i, 0)),
         scratch_shapes=[pltpu.VMEM((rows_n, 128), jnp.float32)],
         compiler_params=pltpu.CompilerParams(
             dimension_semantics=("arbitrary",), vmem_limit_bytes=16 << 20
         ),
         name="margin",
-    )(*scores, row_list, knn_own, knn_got)
+    )(kept, got, row_list, knn_own, knn_got)
 
 
 def shifted(array, axis, size, by):
@@ -353,16 +349,18 @@
     a = {0: own, -1: up(own), 1: down(own)}
     a[2], a[-2] = down(a[1]), up(a[-1])
     b = {0: across(own)}
-    src_all = from_everyone(src_emb, TGT, 8)
-    a[2], a[-2], b[0], src_all = lax.optimization_barrier(
-        (a[2], a[-2], b[0], src_all)
+    beside = shifted(src_emb, "yl", 2, 1)
+    src_all = from_everyone(jnp.stack([src_emb, beside]), "x", 4)
+    a[3], a[-3] = down(a[2]), up(a[-2])
+    b[1], b[-1] = down(b[0]), up(b[0])
+    a[3], a[-3], b[1], b[-1], src_all = lax.optimization_barrier(
+        (a[3], a[-3], b[1], b[-1], src_all)
     )
     unit = unit_rows(src_all)
-    a[3], a[-3] = down(a[2]), up(a[-2])
     a[4] = up(a[-3])
-    for k in range(1, 4):
-        b[k], b[-k] = down(b[k - 1]), up(b[1 - k])
-    b[4] = down(b[3])
+    b[2], b[-2] = down(b[1]), up(b[-1])
+    b[3], b[-3] = down(b[2]), across(a[-3])
+    b[4] = across(a[4])
     return [(b if dy else a)[dz] for dz, dy in PLACES], unit
 
 
@@ -381,17 +379,9 @@
     sid = jnp.concatenate([src_ids, over(src_ids)])[None, :]
     tid = lax.dynamic_slice_in_dim(tgt_ids, core * half, half, 0)[None, :]
 
-    quarter = half // 2
-    kept0, sent0, row0, row0_pair, col0 = scores_and_lists(
-        0, blocks, units, sid, tid[:, :quarter], ()
-    )
-    got0 = over(sent0)
-    kept1, sent1, row1, row1_pair, col1 = scores_and_lists(
-        1, blocks, units, sid, tid[:, quarter:], (row0, row0_pair)
-    )
-    got1 = over(sent1)
-    cols = jnp.concatenate([col0, col1], axis=1)
-    rows = jnp.concatenate([row1, row1_pair])
+    kept, sent, rows, rows_pair, cols = scores_and_lists(blocks, units, sid, tid)
+    got = over(sent)
+    rows = jnp.concatenate([rows, rows_pair])
     rows = joined([rows, shifted(rows, "yl", 2, 1)])
     cols = joined([cols, across(cols)])
     spread = jnp.broadcast_to(cols[None], (8, *cols.shape))
@@ -402,7 +392,7 @@
     far = far.astype(jnp.float32)
     a, b, c, d = merged_all([tuple(far[k]) for k in range(8)])
     knn_own = ((a + b) + (c + d))[None, :]
-    return margin((kept0, kept1, got0, got1), row_list, knn_own, over(knn_own))
+    return margin(kept, got, row_list, knn_own, over(knn_own))
 
 
 def solution(mesh):

time: 114 us -> 108 us (0.947)
  starting transfers between devices: 55.9 us -> 51.9 us
  local copies, waits for them, and re-layouts: 5.59 us -> 4.34 us
  Pallas kernels: 18.8 us -> 17.6 us
    ppermute x27, starting transfers between devices: 49 us -> 42.5 us  [shifted(): lax.ppermute(array, axis, [(i, (i + by) % size) for i in range(size)])]
    all_to_all x1, starting transfers between devices: 3.37 us -> 5.29 us  [body(): far = lax.all_to_all(spread, 'z', 0, 0, tiled=True)]
    pallas_call x2 -> x1, Pallas kernels: 12.9 us -> 11.6 us  [scores_and_lists(): pl.pallas_call(functools.partial(score_kernel, len(blocks)), out_shape=(p...]
  transfers between devices with their start and end apart: 29 -> 29, of which waited for: 13 -> 16; matrix products, arithmetic and copies ran while one was open for 4% -> 3% of each run, Pallas kernels for 0% -> 0%
where the time goes in v4:
time: 108 us
  starting transfers between devices  51.9 us (48%)
  waiting for transfers between devices  31.4 us (29%)
  Pallas kernels  17.6 us (16%)
  local copies, waits for them, and re-layouts  4.34 us (4%)
  other arithmetic  2.59 us (2%)
    ppermute x27, starting transfers between devices, shifted(): lax.ppermute(array, axis, [(i, (i + by) % size) for i in range(size)])  42.5 us
    ppermute x27, waiting for transfers between devices, shifted(): lax.ppermute(array, axis, [(i, (i + by) % size) for i in range(size)])  31.2 us
    pallas_call x1, Pallas kernels, scores_and_lists(): pl.pallas_call(functools.partial(score_kernel, len(blocks)), out_shape=(p...  11.6 us
    pallas_call x1, Pallas kernels, margin(): pl.pallas_call(margin_kernel, grid=(rows_n // block,), out_shape=jax.Shap...  5.62 us
    all_to_all x1, starting transfers between devices, body(): far = lax.all_to_all(spread, 'z', 0, 0, tiled=True)  5.29 us
    all_to_all x1, starting transfers between devices, from_everyone(): return lax.all_to_all(spread, axes, 0, 0, tiled=True)  4.14 us
  transfers between devices with their start and end apart: 29, of which 16 were waited for; matrix products, arithmetic and copies ran while one was open for 3% of the time, Pallas kernels for 0%

profile of v4, /device:TPU:1, one launch (start us, length us, event | category | flops | bytes accessed | tf_op | source)
XLA Modules:
  0.0 108.0 jit_solution(9431452250838169180)
XLA Ops:
  0.9 3.3 %collective-permute-start = (bf16[32,2048]{1,0:T(8,128)(2,1)S(1)}, bf16[32,2048]{1,0:T(8,128)(2,1)S(1)}, u32[]{:S(2)}, u32[]{:S(2)}) collective-permute-start(bf16[32,2048]{1,0:T(8,128)(2,1)S(1)} %dynamic-slice_bitcast_fusion), channel_id=1, source_target_pairs={{0,8},{8,0},{1,9},{9,1},{2,10},{10,2},{3,11},{11,3},{4,12},{12,4},... | collective-permute-start | bytes 393224 | tf_op jit(solution)/shard_map/ppermute | solution.py:311
  6.2 4.2 %collective-permute-start.3 = (bf16[64,2048]{1,0:T(8,128)(2,1)S(1)}, bf16[64,2048]{1,0:T(8,128)(2,1)S(1)}, u32[]{:S(2)}, u32[]{:S(2)}) collective-permute-start(bf16[64,2048]{1,0:T(8,128)(2,1)S(1)} %pad_maximum_fusion.refs_0_), channel_id=1, source_target_pairs={{0,224},{32,0},{64,32},{96,64},{128,96},{160,128},{192,160},{224,1... | collective-permute-start | bytes 786440 | tf_op jit(solution)/shard_map/ppermute | solution.py:311
  11.4 1.1 %broadcast_in_dim.8 = bf16[4,2,512,128]{3,2,1,0:T(8,128)(2,1)} broadcast(bf16[2,512,128]{2,1,0:T(8,128)(2,1)S(1)} %pad_maximum_fusion.1), dimensions={1,2,3} | broadcast | bytes 1310720 | tf_op jit(solution)/shard_map/broadcast_in_dim | solution.py:315
  12.5 4.1 %all-to-all-start = ((bf16[4,2,512,128]{3,2,1,0:T(8,128)(2,1)}), bf16[4,2,512,128]{3,2,1,0:T(8,128)(2,1)S(1)}, u32[]{:S(2)}, u32[]{:S(2)}) async-start(bf16[4,2,512,128]{3,2,1,0:T(8,128)(2,1)} %broadcast_in_dim.8), calls=%async_computation | async-start | bytes 2097152 | tf_op jit(solution)/shard_map/all_to_all | solution.py:316
  16.7 2.6 %collective-permute-start.1 = (bf16[64,2048]{1,0:T(8,128)(2,1)S(1)}, bf16[64,2048]{1,0:T(8,128)(2,1)S(1)}, u32[]{:S(2)}, u32[]{:S(2)}) collective-permute-start(bf16[64,2048]{1,0:T(8,128)(2,1)S(1)} %pad_maximum_fusion.refs_0_), channel_id=1, source_target_pairs={{0,16},{16,0},{1,17},{17,1},{2,18},{18,2},{3,19},{19,3},{4,20},{20... | collective-permute-start | bytes 786440 | tf_op jit(solution)/shard_map/ppermute | solution.py:311
  19.3 3.2 %collective-permute-start.4 = (bf16[64,2048]{1,0:T(8,128)(2,1)S(1)}, bf16[64,2048]{1,0:T(8,128)(2,1)S(1)}, u32[]{:S(2)}, u32[]{:S(2)}) collective-permute-start(bf16[64,2048]{1,0:T(8,128)(2,1)S(1)} %collective-permute-done.3.refs_4_), channel_id=1, source_target_pairs={{0,224},{32,0},{64,32},{96,64},{128,96},{160,128},{192,160},{224,1... | collective-permute-start | bytes 786440 | tf_op jit(solution)/shard_map/ppermute | solution.py:311
  22.5 2.6 %collective-permute-done.1.refs_1_ = bf16[64,2048]{1,0:T(8,128)(2,1)S(1)} collective-permute-done((bf16[64,2048]{1,0:T(8,128)(2,1)S(1)}, bf16[64,2048]{1,0:T(8,128)(2,1)S(1)}, u32[]{:S(2)}, u32[]{:S(2)}) %collective-permute-start.1) | collective-permute-done | bytes 262176 | tf_op jit(solution)/shard_map/ppermute | solution.py:311
  25.1 2.7 %collective-permute-start.8 = (bf16[64,2048]{1,0:T(8,128)(2,1)S(1)}, bf16[64,2048]{1,0:T(8,128)(2,1)S(1)}, u32[]{:S(2)}, u32[]{:S(2)}) collective-permute-start(bf16[64,2048]{1,0:T(8,128)(2,1)S(1)} %collective-permute-done.1.refs_1_), channel_id=1, source_target_pairs={{0,224},{32,0},{64,32},{96,64},{128,96},{160,128},{192,160},{224,1... | collective-permute-start | bytes 786440 | tf_op jit(solution)/shard_map/ppermute | solution.py:311
  27.7 2.3 %collective-permute-start.5 = (bf16[64,2048]{1,0:T(8,128)(2,1)S(1)}, bf16[64,2048]{1,0:T(8,128)(2,1)S(1)}, u32[]{:S(2)}, u32[]{:S(2)}) collective-permute-start(bf16[64,2048]{1,0:T(8,128)(2,1)S(1)} %collective-permute-done.4.refs_8_), channel_id=1, source_target_pairs={{0,224},{32,0},{64,32},{96,64},{128,96},{160,128},{192,160},{224,1... | collective-permute-start | bytes 786440 | tf_op jit(solution)/shard_map/ppermute | solution.py:311
  30.0 5.3 %collective-permute-done.9.refs_3_ = bf16[64,2048]{1,0:T(8,128)(2,1)S(1)} collective-permute-done((bf16[64,2048]{1,0:T(8,128)(2,1)S(1)}, bf16[64,2048]{1,0:T(8,128)(2,1)S(1)}, u32[]{:S(2)}, u32[]{:S(2)}) %collective-permute-start.9) | collective-permute-done | bytes 262176 | tf_op jit(solution)/shard_map/ppermute | solution.py:311
  35.4 2.1 %collective-permute-done.5.refs_12_ = bf16[64,2048]{1,0:T(8,128)(2,1)S(1)} collective-permute-done((bf16[64,2048]{1,0:T(8,128)(2,1)S(1)}, bf16[64,2048]{1,0:T(8,128)(2,1)S(1)}, u32[]{:S(2)}, u32[]{:S(2)}) %collective-permute-start.5) | collective-permute-done | bytes 262176 | tf_op jit(solution)/shard_map/ppermute | solution.py:311
  37.5 3.6 %collective-permute-done.7.refs_10_ = bf16[64,2048]{1,0:T(8,128)(2,1)} collective-permute-done((bf16[64,2048]{1,0:T(8,128)(2,1)S(1)}, bf16[64,2048]{1,0:T(8,128)(2,1)}, u32[]{:S(2)}, u32[]{:S(2)}) %collective-permute-start.7) | collective-permute-done | bytes 262176 | tf_op jit(solution)/shard_map/ppermute | solution.py:311
  41.6 2.7 %collective-permute-start.17 = (bf16[512,1024]{1,0:T(8,128)(2,1)S(1)}, bf16[512,1024]{1,0:T(8,128)(2,1)S(1)}, u32[]{:S(2)}, u32[]{:S(2)}) collective-permute-start(bf16[512,1024]{1,0:T(8,128)(2,1)S(1)} %unit.1.refs_16_), channel_id=1, source_target_pairs={{0,8},{8,0},{1,9},{9,1},{2,10},{10,2},{3,11},{11,3},{4,12},{12,4},... | collective-permute-start | bytes 3145736 | tf_op jit(solution)/shard_map/ppermute | solution.py:311
  44.3 1.5 %collective-permute-start.15 = (bf16[64,2048]{1,0:T(8,128)(2,1)}, bf16[64,2048]{1,0:T(8,128)(2,1)S(1)}, u32[]{:S(2)}, u32[]{:S(2)}) collective-permute-start(bf16[64,2048]{1,0:T(8,128)(2,1)} %collective-permute-done.7.refs_10_), channel_id=1, source_target_pairs={{0,32},{32,64},{64,96},{96,128},{128,160},{160,192},{192,224},{224... | collective-permute-start | bytes 786440 | tf_op jit(solution)/shard_map/ppermute | solution.py:311
  47.2 4.9 %collective-permute-done.12.refs_9_ = bf16[64,2048]{1,0:T(8,128)(2,1)S(1)} collective-permute-done((bf16[64,2048]{1,0:T(8,128)(2,1)S(1)}, bf16[64,2048]{1,0:T(8,128)(2,1)S(1)}, u32[]{:S(2)}, u32[]{:S(2)}) %collective-permute-start.12) | collective-permute-done | bytes 262176 | tf_op jit(solution)/shard_map/ppermute | solution.py:311
  52.1 1.3 %collective-permute-start.14 = (bf16[64,2048]{1,0:T(8,128)(2,1)S(1)}, bf16[64,2048]{1,0:T(8,128)(2,1)S(1)}, u32[]{:S(2)}, u32[]{:S(2)}) collective-permute-start(bf16[64,2048]{1,0:T(8,128)(2,1)S(1)} %collective-permute-done.12.refs_9_), channel_id=1, source_target_pairs={{0,224},{32,0},{64,32},{96,64},{128,96},{160,128},{192,160},{224,1... | collective-permute-start | bytes 786440 | tf_op jit(solution)/shard_map/ppermute | solution.py:311
  53.5 2.3 %collective-permute-start.16 = (bf16[64,2048]{1,0:T(8,128)(2,1)S(1)}, bf16[64,2048]{1,0:T(8,128)(2,1)S(1)}, u32[]{:S(2)}, u32[]{:S(2)}) collective-permute-start(bf16[64,2048]{1,0:T(8,128)(2,1)S(1)} %collective-permute-done.15.refs_14_), channel_id=1, source_target_pairs={{0,16},{16,0},{1,17},{17,1},{2,18},{18,2},{3,19},{19,3},{4,20},{20... | collective-permute-start | bytes 786440 | tf_op jit(solution)/shard_map/ppermute | solution.py:311
  55.8 3.2 %collective-permute-done.11.refs_7_ = bf16[64,2048]{1,0:T(8,128)(2,1)S(1)} collective-permute-done((bf16[64,2048]{1,0:T(8,128)(2,1)S(1)}, bf16[64,2048]{1,0:T(8,128)(2,1)S(1)}, u32[]{:S(2)}, u32[]{:S(2)}) %collective-permute-start.11) | collective-permute-done | bytes 262176 | tf_op jit(solution)/shard_map/ppermute | solution.py:311
  59.1 2.0 %collective-permute-done.16.refs_15_ = bf16[64,2048]{1,0:T(8,128)(2,1)S(1)} collective-permute-done((bf16[64,2048]{1,0:T(8,128)(2,1)S(1)}, bf16[64,2048]{1,0:T(8,128)(2,1)S(1)}, u32[]{:S(2)}, u32[]{:S(2)}) %collective-permute-start.16) | collective-permute-done | bytes 262176 | tf_op jit(solution)/shard_map/ppermute | solution.py:311
  61.1 11.6 %scores.1 = (bf16[512,2048]{1,0:T(8,128)(2,1)}, bf16[512,2048]{1,0:T(8,128)(2,1)}, f32[4,512]{1,0:T(4,128)S(1)}, f32[4,512]{1,0:T(4,128)S(1)}, bf16[4,2048]{1,0:T(4,128)(2,1)S(1)}) custom-call(bf16[64,2048]{1,0:T(8,128)(2,1)S(1)} %pad_maximum_fusion.refs_0_, bf16[64,2048]{1,0:T(8,128)(2,1)S(1)} %collective-permute-done.1.refs_1_, ...), custom_call_target="tpu_custom_call" | custom-call | flops 4294967296 | bytes 12582912 | tf_op jit(solution)/shard_map/scores/pallas_call | solution.py:201
  72.7 2.2 %collective-permute-start.21 = (bf16[4,2048]{1,0:T(4,128)(2,1)S(1)}, bf16[4,2048]{1,0:T(4,128)(2,1)S(1)}, u32[]{:S(2)}, u32[]{:S(2)}) collective-permute-start(bf16[4,2048]{1,0:T(4,128)(2,1)S(1)} %get-tuple-element.25), channel_id=1, source_target_pairs={{0,16},{16,0},{1,17},{17,1},{2,18},{18,2},{3,19},{19,3},{4,20},{20... | collective-permute-start | bytes 49160 | tf_op jit(solution)/shard_map/ppermute | solution.py:311
  75.6 1.3 %collective-permute-done.21 = bf16[4,2048]{1,0:T(4,128)(2,1)S(1)} collective-permute-done((bf16[4,2048]{1,0:T(4,128)(2,1)S(1)}, bf16[4,2048]{1,0:T(4,128)(2,1)S(1)}, u32[]{:S(2)}, u32[]{:S(2)}) %collective-permute-start.21) | collective-permute-done | bytes 16416 | tf_op jit(solution)/shard_map/ppermute | solution.py:311
  78.6 1.2 %collective-permute-start.22 = (f32[8,512]{1,0:T(8,128)S(1)}, f32[8,512]{1,0:T(8,128)S(1)}, u32[]{:S(2)}, u32[]{:S(2)}) collective-permute-start(f32[8,512]{1,0:T(8,128)S(1)} %stack.17), channel_id=1, source_target_pairs={{0,1},{1,2},{2,3},{3,0},{4,5},{5,6},{6,7},{7,4},{8,9},{9,10},{10,1... | collective-permute-start | bytes 49160 | tf_op jit(solution)/shard_map/ppermute | solution.py:311
  79.8 4.5 %collective-permute-start.19 = (bf16[512,2048]{1,0:T(8,128)(2,1)}, bf16[512,2048]{1,0:T(8,128)(2,1)S(1)}, u32[]{:S(2)}, u32[]{:S(2)}) collective-permute-start(bf16[512,2048]{1,0:T(8,128)(2,1)} %get-tuple-element.22), channel_id=1, source_target_pairs={{0,8},{8,0},{1,9},{9,1},{2,10},{10,2},{3,11},{11,3},{4,12},{12,4},... | collective-permute-start | bytes 6291464 | tf_op jit(solution)/shard_map/ppermute | solution.py:311
  84.3 5.3 %all-to-all-start.1 = ((bf16[8,4,2048]{2,1,0:T(4,128)(2,1)}), bf16[8,4,2048]{2,1,0:T(4,128)(2,1)S(1)}, u32[]{:S(2)}, u32[]{:S(2)}) async-start(bf16[8,4,2048]{2,1,0:T(4,128)(2,1)} %broadcast_in_dim.22), calls=%async_computation.1 | async-start | bytes 262144 | tf_op jit(solution)/shard_map/all_to_all | solution.py:388
  89.6 1.5 %collective-permute-start.24 = (f32[8,512]{1,0:T(8,128)S(1)}, f32[8,512]{1,0:T(8,128)S(1)}, u32[]{:S(2)}, u32[]{:S(2)}) collective-permute-start(f32[8,512]{1,0:T(8,128)S(1)} %stack.17), channel_id=1, source_target_pairs={{0,3},{1,0},{2,1},{3,2},{4,7},{5,4},{6,5},{7,6},{8,11},{9,8},{10,9... | collective-permute-start | bytes 49160 | tf_op jit(solution)/shard_map/ppermute | solution.py:311
  91.0 1.5 %collective-permute-start.23 = (f32[8,512]{1,0:T(8,128)S(1)}, f32[8,512]{1,0:T(8,128)S(1)}, u32[]{:S(2)}, u32[]{:S(2)}) collective-permute-start(f32[8,512]{1,0:T(8,128)S(1)} %stack.17), channel_id=1, source_target_pairs={{0,2},{1,3},{2,0},{3,1},{4,6},{5,7},{6,4},{7,5},{8,10},{9,11},{10,... | collective-permute-start | bytes 49160 | tf_op jit(solution)/shard_map/ppermute | solution.py:311
  92.6 2.6 %collective-permute-done.23 = f32[8,512]{1,0:T(8,128)S(1)} collective-permute-done((f32[8,512]{1,0:T(8,128)S(1)}, f32[8,512]{1,0:T(8,128)S(1)}, u32[]{:S(2)}, u32[]{:S(2)}) %collective-permute-start.23) | collective-permute-done | bytes 16416 | tf_op jit(solution)/shard_map/ppermute | solution.py:311
  95.3 1.8 %collective-permute-start.25 = (f32[4,512]{1,0:T(4,128)S(1)}, f32[4,512]{1,0:T(4,128)S(1)}, u32[]{:S(2)}, u32[]{:S(2)}) collective-permute-start(f32[4,512]{1,0:T(4,128)S(1)} %pad_maximum_fusion.4), channel_id=1, source_target_pairs={{0,8},{8,0},{1,9},{9,1},{2,10},{10,2},{3,11},{11,3},{4,12},{12,4},... | collective-permute-start | bytes 24584 | tf_op jit(solution)/shard_map/ppermute | solution.py:311
  98.4 1.6 %collective-permute-start.26 = (f32[1,2048]{1,0:T(1,128)S(1)}, f32[1,2048]{1,0:T(1,128)S(1)}, u32[]{:S(2)}, u32[]{:S(2)}) collective-permute-start(f32[1,2048]{1,0:T(1,128)S(1)} %add_bitcast_fusion.knn_own_ref), channel_id=1, source_target_pairs={{0,8},{8,0},{1,9},{9,1},{2,10},{10,2},{3,11},{11,3},{4,12},{12,4},... | collective-permute-start | bytes 24584 | tf_op jit(solution)/shard_map/ppermute | solution.py:311
  100.8 1.6 %copy-done = bf16[512,2048]{1,0:T(8,128)(2,1)S(1)} copy-done((bf16[512,2048]{1,0:T(8,128)(2,1)S(1)}, bf16[512,2048]{1,0:T(8,128)(2,1)}, u32[]{:S(2)}) %copy-start) | copy-done | bytes 2097176
  102.4 5.6 %margin.1 = f32[512,4096]{1,0:T(8,128)} custom-call(bf16[512,2048]{1,0:T(8,128)(2,1)S(1)} %copy-done, bf16[512,2048]{1,0:T(8,128)(2,1)S(1)} %collective-permute-done.19.got_ref, f32[4,512]{1,0:T(4,128)S(1)} %pad_maximum_fusion.5.row_ref, f32[1,2048]{1,0:T(1,128)S(1)} %add_bitcast_fusion.knn_own_ref, f32[1,2048]{1,0:T(1,128)S(1)} %collective-permute-done.26.knn_got_ref), custom_call_target="tpu_custom_call" | custom-call | tf_op jit(solution)/shard_map/margin/pallas_call | solution.py:296
  (62 shorter events, 10.5 us)
Async XLA Ops:
  0.9 4.3 %collective-permute-start = (bf16[32,2048]{1,0:T(8,128)(2,1)S(1)}, bf16[32,2048]{1,0:T(8,128)(2,1)S(1)}, u32[]{:S(2)}, u32[]{:S(2)}) collective-permute-start(bf16[32,2048]{1,0:T(8,128)(2,1)S(1)} %dynamic-slice_bitcast_fusion), channel_id=1, source_target_pairs={{0,8},{8,0},{1,9},{9,1},{2,10},{10,2},{3,11},{11,3},{4,12},{12,4},... | collective-permute-start | bytes 393224 | tf_op jit(solution)/shard_map/ppermute | solution.py:311
  4.2 6.2 %collective-permute-start.10 = (bf16[512,128]{1,0:T(8,128)(2,1)}, bf16[512,128]{1,0:T(8,128)(2,1)S(1)}, u32[]{:S(2)}, u32[]{:S(2)}) collective-permute-start(bf16[512,128]{1,0:T(8,128)(2,1)} %param.4), channel_id=1, source_target_pairs={{0,4},{4,0},{1,5},{5,1},{2,6},{6,2},{3,7},{7,3},{8,12},{12,8},{9,1... | collective-permute-start | bytes 393224 | tf_op jit(solution)/shard_map/ppermute | solution.py:311
  6.2 13.1 %collective-permute-start.3 = (bf16[64,2048]{1,0:T(8,128)(2,1)S(1)}, bf16[64,2048]{1,0:T(8,128)(2,1)S(1)}, u32[]{:S(2)}, u32[]{:S(2)}) collective-permute-start(bf16[64,2048]{1,0:T(8,128)(2,1)S(1)} %pad_maximum_fusion.refs_0_), channel_id=1, source_target_pairs={{0,224},{32,0},{64,32},{96,64},{128,96},{160,128},{192,160},{224,1... | collective-permute-start | bytes 786440 | tf_op jit(solution)/shard_map/ppermute | solution.py:311
  10.5 12.0 %collective-permute-start.2 = (bf16[64,2048]{1,0:T(8,128)(2,1)S(1)}, bf16[64,2048]{1,0:T(8,128)(2,1)S(1)}, u32[]{:S(2)}, u32[]{:S(2)}) collective-permute-start(bf16[64,2048]{1,0:T(8,128)(2,1)S(1)} %pad_maximum_fusion.refs_0_), channel_id=1, source_target_pairs={{0,32},{32,64},{64,96},{96,128},{128,160},{160,192},{192,224},{224... | collective-permute-start | bytes 786440 | tf_op jit(solution)/shard_map/ppermute | solution.py:311
  12.5 33.3 %copy-start.2 = (s32[512]{0:T(512)S(1)}, s32[512]{0:T(512)}, u32[]{:S(2)}) copy-start(s32[512]{0:T(512)} %param.6) | copy-start | bytes 6148
  12.5 43.3 %copy-start.1 = (s32[4096]{0:T(1024)S(1)}, s32[4096]{0:T(1024)}, u32[]{:S(2)}) copy-start(s32[4096]{0:T(1024)} %param.7) | copy-start | bytes 49156
  12.5 28.6 %all-to-all-start = ((bf16[4,2,512,128]{3,2,1,0:T(8,128)(2,1)}), bf16[4,2,512,128]{3,2,1,0:T(8,128)(2,1)S(1)}, u32[]{:S(2)}, u32[]{:S(2)}) async-start(bf16[4,2,512,128]{3,2,1,0:T(8,128)(2,1)} %broadcast_in_dim.8), calls=%async_computation | async-start | bytes 2097152 | tf_op jit(solution)/shard_map/all_to_all | solution.py:316
  16.7 8.4 %collective-permute-start.1 = (bf16[64,2048]{1,0:T(8,128)(2,1)S(1)}, bf16[64,2048]{1,0:T(8,128)(2,1)S(1)}, u32[]{:S(2)}, u32[]{:S(2)}) collective-permute-start(bf16[64,2048]{1,0:T(8,128)(2,1)S(1)} %pad_maximum_fusion.refs_0_), channel_id=1, source_target_pairs={{0,16},{16,0},{1,17},{17,1},{2,18},{18,2},{3,19},{19,3},{4,20},{20... | collective-permute-start | bytes 786440 | tf_op jit(solution)/shard_map/ppermute | solution.py:311
  19.3 8.5 %collective-permute-start.4 = (bf16[64,2048]{1,0:T(8,128)(2,1)S(1)}, bf16[64,2048]{1,0:T(8,128)(2,1)S(1)}, u32[]{:S(2)}, u32[]{:S(2)}) collective-permute-start(bf16[64,2048]{1,0:T(8,128)(2,1)S(1)} %collective-permute-done.3.refs_4_), channel_id=1, source_target_pairs={{0,224},{32,0},{64,32},{96,64},{128,96},{160,128},{192,160},{224,1... | collective-permute-start | bytes 786440 | tf_op jit(solution)/shard_map/ppermute | solution.py:311
  22.5 7.6 %collective-permute-start.6 = (bf16[64,2048]{1,0:T(8,128)(2,1)S(1)}, bf16[64,2048]{1,0:T(8,128)(2,1)S(1)}, u32[]{:S(2)}, u32[]{:S(2)}) collective-permute-start(bf16[64,2048]{1,0:T(8,128)(2,1)S(1)} %collective-permute-done.2.refs_2_), channel_id=1, source_target_pairs={{0,32},{32,64},{64,96},{96,128},{128,160},{160,192},{192,224},{224... | collective-permute-start | bytes 786440 | tf_op jit(solution)/shard_map/ppermute | solution.py:311
  25.1 10.3 %collective-permute-start.9 = (bf16[64,2048]{1,0:T(8,128)(2,1)S(1)}, bf16[64,2048]{1,0:T(8,128)(2,1)S(1)}, u32[]{:S(2)}, u32[]{:S(2)}) collective-permute-start(bf16[64,2048]{1,0:T(8,128)(2,1)S(1)} %collective-permute-done.1.refs_1_), channel_id=1, source_target_pairs={{0,32},{32,64},{64,96},{96,128},{128,160},{160,192},{192,224},{224... | collective-permute-start | bytes 786440 | tf_op jit(solution)/shard_map/ppermute | solution.py:311
  25.1 10.3 %collective-permute-start.8 = (bf16[64,2048]{1,0:T(8,128)(2,1)S(1)}, bf16[64,2048]{1,0:T(8,128)(2,1)S(1)}, u32[]{:S(2)}, u32[]{:S(2)}) collective-permute-start(bf16[64,2048]{1,0:T(8,128)(2,1)S(1)} %collective-permute-done.1.refs_1_), channel_id=1, source_target_pairs={{0,224},{32,0},{64,32},{96,64},{128,96},{160,128},{192,160},{224,1... | collective-permute-start | bytes 786440 | tf_op jit(solution)/shard_map/ppermute | solution.py:311
  27.7 9.8 %collective-permute-start.5 = (bf16[64,2048]{1,0:T(8,128)(2,1)S(1)}, bf16[64,2048]{1,0:T(8,128)(2,1)S(1)}, u32[]{:S(2)}, u32[]{:S(2)}) collective-permute-start(bf16[64,2048]{1,0:T(8,128)(2,1)S(1)} %collective-permute-done.4.refs_8_), channel_id=1, source_target_pairs={{0,224},{32,0},{64,32},{96,64},{128,96},{160,128},{192,160},{224,1... | collective-permute-start | bytes 786440 | tf_op jit(solution)/shard_map/ppermute | solution.py:311
  30.0 11.1 %collective-permute-start.7 = (bf16[64,2048]{1,0:T(8,128)(2,1)S(1)}, bf16[64,2048]{1,0:T(8,128)(2,1)}, u32[]{:S(2)}, u32[]{:S(2)}) collective-permute-start(bf16[64,2048]{1,0:T(8,128)(2,1)S(1)} %collective-permute-done.6.refs_6_), channel_id=1, source_target_pairs={{0,32},{32,64},{64,96},{96,128},{128,160},{160,192},{192,224},{224... | collective-permute-start | bytes 786440 | tf_op jit(solution)/shard_map/ppermute | solution.py:311
  41.6 19.6 %collective-permute-start.17 = (bf16[512,1024]{1,0:T(8,128)(2,1)S(1)}, bf16[512,1024]{1,0:T(8,128)(2,1)S(1)}, u32[]{:S(2)}, u32[]{:S(2)}) collective-permute-start(bf16[512,1024]{1,0:T(8,128)(2,1)S(1)} %unit.1.refs_16_), channel_id=1, source_target_pairs={{0,8},{8,0},{1,9},{9,1},{2,10},{10,2},{3,11},{11,3},{4,12},{12,4},... | collective-permute-start | bytes 3145736 | tf_op jit(solution)/shard_map/ppermute | solution.py:311
  44.3 7.9 %collective-permute-start.12 = (bf16[64,2048]{1,0:T(8,128)(2,1)S(1)}, bf16[64,2048]{1,0:T(8,128)(2,1)S(1)}, u32[]{:S(2)}, u32[]{:S(2)}) collective-permute-start(bf16[64,2048]{1,0:T(8,128)(2,1)S(1)} %collective-permute-done.8.refs_5_), channel_id=1, source_target_pairs={{0,224},{32,0},{64,32},{96,64},{128,96},{160,128},{192,160},{224,1... | collective-permute-start | bytes 786440 | tf_op jit(solution)/shard_map/ppermute | solution.py:311
  44.3 9.2 %collective-permute-start.15 = (bf16[64,2048]{1,0:T(8,128)(2,1)}, bf16[64,2048]{1,0:T(8,128)(2,1)S(1)}, u32[]{:S(2)}, u32[]{:S(2)}) collective-permute-start(bf16[64,2048]{1,0:T(8,128)(2,1)} %collective-permute-done.7.refs_10_), channel_id=1, source_target_pairs={{0,32},{32,64},{64,96},{96,128},{128,160},{160,192},{192,224},{224... | collective-permute-start | bytes 786440 | tf_op jit(solution)/shard_map/ppermute | solution.py:311
  45.8 1.5 %collective-permute-start.18 = (s32[512]{0:T(512)S(1)}, s32[512]{0:T(512)S(1)}, u32[]{:S(2)}, u32[]{:S(2)}) collective-permute-start(s32[512]{0:T(512)S(1)} %copy-done.2), channel_id=1, source_target_pairs={{0,8},{8,0},{1,9},{9,1},{2,10},{10,2},{3,11},{11,3},{4,12},{12,4},... | collective-permute-start | bytes 6152 | tf_op jit(solution)/shard_map/ppermute | solution.py:311
  46.4 12.6 %collective-permute-start.13 = (bf16[64,2048]{1,0:T(8,128)(2,1)}, bf16[64,2048]{1,0:T(8,128)(2,1)S(1)}, u32[]{:S(2)}, u32[]{:S(2)}) collective-permute-start(bf16[64,2048]{1,0:T(8,128)(2,1)} %collective-permute-done.7.refs_10_), channel_id=1, source_target_pairs={{0,16},{16,0},{1,17},{17,1},{2,18},{18,2},{3,19},{19,3},{4,20},{20... | collective-permute-start | bytes 786440 | tf_op jit(solution)/shard_map/ppermute | solution.py:311
  47.2 11.7 %collective-permute-start.11 = (bf16[64,2048]{1,0:T(8,128)(2,1)S(1)}, bf16[64,2048]{1,0:T(8,128)(2,1)S(1)}, u32[]{:S(2)}, u32[]{:S(2)}) collective-permute-start(bf16[64,2048]{1,0:T(8,128)(2,1)S(1)} %collective-permute-done.9.refs_3_), channel_id=1, source_target_pairs={{0,32},{32,64},{64,96},{96,128},{128,160},{160,192},{192,224},{224... | collective-permute-start | bytes 786440 | tf_op jit(solution)/shard_map/ppermute | solution.py:311
  52.1 7.0 %collective-permute-start.14 = (bf16[64,2048]{1,0:T(8,128)(2,1)S(1)}, bf16[64,2048]{1,0:T(8,128)(2,1)S(1)}, u32[]{:S(2)}, u32[]{:S(2)}) collective-permute-start(bf16[64,2048]{1,0:T(8,128)(2,1)S(1)} %collective-permute-done.12.refs_9_), channel_id=1, source_target_pairs={{0,224},{32,0},{64,32},{96,64},{128,96},{160,128},{192,160},{224,1... | collective-permute-start | bytes 786440 | tf_op jit(solution)/shard_map/ppermute | solution.py:311
  53.5 7.7 %collective-permute-start.16 = (bf16[64,2048]{1,0:T(8,128)(2,1)S(1)}, bf16[64,2048]{1,0:T(8,128)(2,1)S(1)}, u32[]{:S(2)}, u32[]{:S(2)}) collective-permute-start(bf16[64,2048]{1,0:T(8,128)(2,1)S(1)} %collective-permute-done.15.refs_14_), channel_id=1, source_target_pairs={{0,16},{16,0},{1,17},{17,1},{2,18},{18,2},{3,19},{19,3},{4,20},{20... | collective-permute-start | bytes 786440 | tf_op jit(solution)/shard_map/ppermute | solution.py:311
  72.7 4.2 %collective-permute-start.21 = (bf16[4,2048]{1,0:T(4,128)(2,1)S(1)}, bf16[4,2048]{1,0:T(4,128)(2,1)S(1)}, u32[]{:S(2)}, u32[]{:S(2)}) collective-permute-start(bf16[4,2048]{1,0:T(4,128)(2,1)S(1)} %get-tuple-element.25), channel_id=1, source_target_pairs={{0,16},{16,0},{1,17},{17,1},{2,18},{18,2},{3,19},{19,3},{4,20},{20... | collective-permute-start | bytes 49160 | tf_op jit(solution)/shard_map/ppermute | solution.py:311
  74.9 2.9 %collective-permute-start.20 = (f32[8,512]{1,0:T(8,128)S(1)}, f32[8,512]{1,0:T(8,128)S(1)}, u32[]{:S(2)}, u32[]{:S(2)}) collective-permute-start(f32[8,512]{1,0:T(8,128)S(1)} %pad_maximum_fusion.2), channel_id=1, source_target_pairs={{0,4},{4,0},{1,5},{5,1},{2,6},{6,2},{3,7},{7,3},{8,12},{12,8},{9,1... | collective-permute-start | bytes 49160 | tf_op jit(solution)/shard_map/ppermute | solution.py:311
  78.6 13.9 %collective-permute-start.22 = (f32[8,512]{1,0:T(8,128)S(1)}, f32[8,512]{1,0:T(8,128)S(1)}, u32[]{:S(2)}, u32[]{:S(2)}) collective-permute-start(f32[8,512]{1,0:T(8,128)S(1)} %stack.17), channel_id=1, source_target_pairs={{0,1},{1,2},{2,3},{3,0},{4,5},{5,6},{6,7},{7,4},{8,9},{9,10},{10,1... | collective-permute-start | bytes 49160 | tf_op jit(solution)/shard_map/ppermute | solution.py:311
  79.8 21.0 %collective-permute-start.19 = (bf16[512,2048]{1,0:T(8,128)(2,1)}, bf16[512,2048]{1,0:T(8,128)(2,1)S(1)}, u32[]{:S(2)}, u32[]{:S(2)}) collective-permute-start(bf16[512,2048]{1,0:T(8,128)(2,1)} %get-tuple-element.22), channel_id=1, source_target_pairs={{0,8},{8,0},{1,9},{9,1},{2,10},{10,2},{3,11},{11,3},{4,12},{12,4},... | collective-permute-start | bytes 6291464 | tf_op jit(solution)/shard_map/ppermute | solution.py:311
  84.3 13.8 %all-to-all-start.1 = ((bf16[8,4,2048]{2,1,0:T(4,128)(2,1)}), bf16[8,4,2048]{2,1,0:T(4,128)(2,1)S(1)}, u32[]{:S(2)}, u32[]{:S(2)}) async-start(bf16[8,4,2048]{2,1,0:T(4,128)(2,1)} %broadcast_in_dim.22), calls=%async_computation.1 | async-start | bytes 262144 | tf_op jit(solution)/shard_map/all_to_all | solution.py:388
  89.6 3.0 %collective-permute-start.24 = (f32[8,512]{1,0:T(8,128)S(1)}, f32[8,512]{1,0:T(8,128)S(1)}, u32[]{:S(2)}, u32[]{:S(2)}) collective-permute-start(f32[8,512]{1,0:T(8,128)S(1)} %stack.17), channel_id=1, source_target_pairs={{0,3},{1,0},{2,1},{3,2},{4,7},{5,4},{6,5},{7,6},{8,11},{9,8},{10,9... | collective-permute-start | bytes 49160 | tf_op jit(solution)/shard_map/ppermute | solution.py:311
  91.0 4.1 %collective-permute-start.23 = (f32[8,512]{1,0:T(8,128)S(1)}, f32[8,512]{1,0:T(8,128)S(1)}, u32[]{:S(2)}, u32[]{:S(2)}) collective-permute-start(f32[8,512]{1,0:T(8,128)S(1)} %stack.17), channel_id=1, source_target_pairs={{0,2},{1,3},{2,0},{3,1},{4,6},{5,7},{6,4},{7,5},{8,10},{9,11},{10,... | collective-permute-start | bytes 49160 | tf_op jit(solution)/shard_map/ppermute | solution.py:311
  95.3 2.6 %collective-permute-start.25 = (f32[4,512]{1,0:T(4,128)S(1)}, f32[4,512]{1,0:T(4,128)S(1)}, u32[]{:S(2)}, u32[]{:S(2)}) collective-permute-start(f32[4,512]{1,0:T(4,128)S(1)} %pad_maximum_fusion.4), channel_id=1, source_target_pairs={{0,8},{8,0},{1,9},{9,1},{2,10},{10,2},{3,11},{11,3},{4,12},{12,4},... | collective-permute-start | bytes 24584 | tf_op jit(solution)/shard_map/ppermute | solution.py:311
  98.4 2.4 %collective-permute-start.26 = (f32[1,2048]{1,0:T(1,128)S(1)}, f32[1,2048]{1,0:T(1,128)S(1)}, u32[]{:S(2)}, u32[]{:S(2)}) collective-permute-start(f32[1,2048]{1,0:T(1,128)S(1)} %add_bitcast_fusion.knn_own_ref), channel_id=1, source_target_pairs={{0,8},{8,0},{1,9},{9,1},{2,10},{10,2},{3,11},{11,3},{4,12},{12,4},... | collective-permute-start | bytes 24584 | tf_op jit(solution)/shard_map/ppermute | solution.py:311
  100.8 1.6 %copy-start = (bf16[512,2048]{1,0:T(8,128)(2,1)S(1)}, bf16[512,2048]{1,0:T(8,128)(2,1)}, u32[]{:S(2)}) copy-start(bf16[512,2048]{1,0:T(8,128)(2,1)} %get-tuple-element.21.kept_ref) | copy-start | bytes 6291460
